TPU v7x, 256 devices: a whole 4x4x8 slice. The times are simulated.
256 devices in a mesh: dp: 8 (over z_hi, core), seq: 32 (over z_lo, x, y).
Axes of the slice: x: 4, y: 4, z: 8 (z_hi: 4, z_lo: 2; z = z_hi * 2 + z_lo), core: 2. Of those that a mesh axis runs over, the one named last changes fastest.
Arguments:
- query: bfloat16 [8, 16384, 1536], P('dp', 'seq'), may hold values from -6 to 6
- key: bfloat16 [8, 16384, 1536], P('dp', 'seq'), may hold values from -6 to 6
- value: bfloat16 [8, 16384, 1536], P('dp', 'seq'), may hold values from -6 to 6
- block_weights: bfloat16 [128, 128, 128], P('seq', 'dp'), may hold values from -0.5 to 0.5
- mix_weights: bfloat16 [128, 128, 128], P('seq', 'dp'), may hold values from -1.5 to 1.5
- block_index: int32 [128, 16], replicated, may hold values from 0 to 127, all different within a row
- cotangent: bfloat16 [8, 16384, 1536], P('dp', 'seq'), may hold values from -6 to 6
Outputs:
- output: bfloat16 [8, 16384, 1536], P('dp', 'seq')
- grad_query: bfloat16 [8, 16384, 1536], P('dp', 'seq')
- grad_key: bfloat16 [8, 16384, 1536], P('dp', 'seq')
- grad_value: bfloat16 [8, 16384, 1536], P('dp', 'seq')
- grad_blocks: float32 [128, 128, 128], P('seq', 'dp')
- grad_mix: float32 [128, 128, 128], P('seq', 'dp')
Inputs may be any that keep to these rules, and one draw needn't show every extreme that they name: `block_index`: each row names 16 different blocks, and every block is named by some row.
All inputs are finite; a program needn't handle non-finite values.
Results may differ from a plain program's by a relative error of at most 0.0064.
Values may be sent and summed in bfloat16 or wider, within the bound.
No kernel may reach another device: no remote copies, remote signals or barrier semaphores. Data moves between devices by JAX's collectives and lax.ppermute only.
A program may use at most 64 MiB of HBM per device.

v0:
```python
import jax
import jax.numpy as jnp
from jax import lax
from jax.sharding import PartitionSpec as P


def on_device(query, key, value, block_weights, mix_weights, block_index, cotangent):
    block_count = block_index.shape[0]
    block_size = block_weights.shape[2]
    samples, positions, channels = query.shape
    local_blocks = positions // block_size
    full_blocks = lax.all_gather(block_weights, "dp", axis=1, tiled=True)
    full_mix = lax.all_gather(mix_weights, "dp", axis=1, tiled=True)
    columns_all = jnp.arange(block_count, dtype=jnp.int32)
    pattern = jnp.max(
        (block_index[:, :, None] == columns_all[None, None, :]).astype(jnp.float32), axis=1
    )
    masked = (full_mix.astype(jnp.float32) * pattern[None]).astype(jnp.bfloat16)
    query_f = query.astype(jnp.float32)
    cot_f = cotangent.astype(jnp.float32)
    product = (key.astype(jnp.float32) * value.astype(jnp.float32)).astype(jnp.bfloat16)
    split_parts = product.reshape(samples, local_blocks, block_size, channels)
    first_factor = jnp.einsum(
        "iac,nicd->niad", full_blocks, split_parts, preferred_element_type=jnp.float32
    ).astype(jnp.bfloat16)
    grad_mixed = (
        (cot_f * query_f).astype(jnp.bfloat16).reshape(samples, local_blocks, block_size, channels)
    )

    def second(columns):
        return jnp.einsum(
            "jik,nkjd->nijd", masked, columns, preferred_element_type=jnp.float32
        ).astype(jnp.bfloat16)

    across, mixed_cols = (lambda columns: (columns, second(columns)))(
        lax.all_to_all(first_factor, "seq", split_axis=2, concat_axis=1, tiled=True)
    )
    returned = lax.all_to_all(mixed_cols, "seq", split_axis=1, concat_axis=2, tiled=True)
    grad_cols = lax.all_to_all(grad_mixed, "seq", split_axis=2, concat_axis=1, tiled=True)
    grad_first_cols = jnp.einsum(
        "jik,nijd->nkjd", masked, grad_cols, preferred_element_type=jnp.float32
    ).astype(jnp.bfloat16)
    first_factor_gradient = lax.all_to_all(
        grad_first_cols, "seq", split_axis=1, concat_axis=2, tiled=True
    )
    mix_terms = (
        jnp.einsum("nijd,nkjd->jik", grad_cols, across, preferred_element_type=jnp.float32)
        * pattern[None]
    )
    mixed_f = returned.reshape(samples, positions, channels).astype(jnp.float32)
    output = (query_f * mixed_f).astype(jnp.bfloat16)
    grad_query = (cot_f * mixed_f).astype(jnp.bfloat16)
    product_gradient = jnp.einsum(
        "iac,niad->nicd", full_blocks, first_factor_gradient, preferred_element_type=jnp.float32
    ).reshape(samples, positions, channels)
    grad_key = (product_gradient * value.astype(jnp.float32)).astype(jnp.bfloat16)
    grad_value = (product_gradient * key.astype(jnp.float32)).astype(jnp.bfloat16)
    block_terms = jnp.einsum(
        "niad,nicd->iac", first_factor_gradient, split_parts, preferred_element_type=jnp.float32
    )
    grad_mix = lax.psum_scatter(mix_terms, "dp", scatter_dimension=1, tiled=True)
    grad_blocks = lax.psum_scatter(block_terms, "dp", scatter_dimension=1, tiled=True)
    return (output, grad_query, grad_key, grad_value, grad_blocks, grad_mix)


def solution(mesh):
    placed = (
        P("dp", "seq", None),
        P("dp", "seq", None),
        P("dp", "seq", None),
        P("seq", "dp", None),
        P("seq", "dp", None),
        P(),
        P("dp", "seq", None),
    )
    return jax.shard_map(
        on_device,
        mesh=mesh,
        in_specs=placed,
        out_specs=(
            P("dp", "seq", None),
            P("dp", "seq", None),
            P("dp", "seq", None),
            P("dp", "seq", None),
            P("seq", "dp", None),
            P("seq", "dp", None),
        ),
        check_vma=False,
    )
```

profile of v0, /device:TPU:8, one launch (start us, length us, event | category | flops | bytes accessed | tf_op | source)
XLA Modules:
  0.0 236.4 jit_solution(17266383945671638147)
XLA Ops:
  7.2 5.4 %multiply_convert_fusion = bf16[1,512,1536]{2,0,1:T(2,128)(2,1)S(1)} fusion(bf16[1,512,1536]{2,1,0:T(8,128)(2,1)} %param.7, bf16[1,512,1536]{2,1,0:T(8,128)(2,1)} %param.13), kind=kLoop, calls=%fused_computation.13 | loop fusion | flops 3145728 | bytes 4718592 | tf_op jit(solution)/shard_map/convert_element_type | solution.py:27
  12.9 2.4 copy.96
  15.3 9.0 %all-to-all-start.2 = ((bf16[1,4,128,1536]{3,1,0,2:T(4,128)(2,1)}), bf16[1,4,128,1536]{3,1,0,2:T(4,128)(2,1)S(1)}, u32[]{:S(2)}, u32[]{:S(2)}) async-start(bf16[1,4,128,1536]{3,1,0,2:T(4,128)(2,1)} %copy.96), calls=%async_computation.2 | async-start | bytes 3145728 | tf_op jit(solution)/shard_map/all_to_all | solution.py:39
  24.4 30.9 %all_gather.7 = bf16[4,128,128]{2,1,0:T(8,128)(2,1)S(1)} all-gather(bf16[4,16,128]{2,1,0:T(8,128)(2,1)S(1)} %copy-done.6), channel_id=1, replica_groups=mesh['dp'=8,'seq'=32] {'dp'}, dimensions={1}, use_global_device_ids=true | all-gather | bytes 147456 | tf_op jit(solution)/shard_map/all_gather | solution.py:13
  55.7 0.8 copy.97
  56.5 1.1 copy-done.2
  57.7 0.7 fusion.7
  58.4 2.5 %copy.99 = bf16[1,128,4,1536]{3,2,0,1:T(4,128)(2,1)} copy(bf16[1,128,4,1536]{1,3,2,0:T(8,128)(2,1)S(1)} %fusion.7) | data formatting | bytes 3145728 | tf_op jit(solution)/shard_map/convert_element_type | solution.py:42
  60.9 7.5 %all-to-all-start.3 = ((bf16[1,128,4,1536]{3,2,0,1:T(4,128)(2,1)}), bf16[1,128,4,1536]{3,2,0,1:T(4,128)(2,1)S(1)}, u32[]{:S(2)}, u32[]{:S(2)}) async-start(bf16[1,128,4,1536]{3,2,0,1:T(4,128)(2,1)} %copy.99), calls=%async_computation.3 | async-start | bytes 3145728 | tf_op jit(solution)/shard_map/all_to_all | solution.py:43
  68.4 28.5 %all_gather.6 = bf16[4,128,128]{2,1,0:T(8,128)(2,1)S(1)} all-gather(bf16[4,16,128]{2,1,0:T(8,128)(2,1)S(1)} %copy-done.7), channel_id=1, replica_groups=mesh['dp'=8,'seq'=32] {'dp'}, dimensions={1}, use_global_device_ids=true | all-gather | bytes 147456 | tf_op jit(solution)/shard_map/all_gather | solution.py:12
  96.9 0.5 copy.100
  97.8 0.6 fusion.18
  98.4 0.8 copy-done.4
  99.2 0.5 copy-done.5
  99.7 2.6 %fusion = (bf16[1,512,1536]{2,1,0:T(8,128)(2,1)}, bf16[1,512,1536]{2,1,0:T(8,128)(2,1)}, bf16[1,512,1536]{2,1,0:T(8,128)(2,1)S(1)}) fusion(bf16[1,512,1536]{2,1,0:T(8,128)(2,1)S(1)} %copy-done.4, f32[4,1536,128]{1,2,0:T(8,128)S(1)} %fusion.18, bf16[1,512,1536]{2,1,0:T(8,128)(2,1)S(1)} %copy-done.5), kind=kLoop, calls=%fused_computation.3 | loop fusion | flops 6291456 | bytes 11010048 | tf_op jit(solution)/shard_map/convert_element_type | solution.py:57
  102.3 1.9 fusion.5
  104.2 3.9 %copy.89 = bf16[1,4,128,1536]{3,1,0,2:T(4,128)(2,1)} copy(bf16[1,4,128,1536]{2,3,1,0:T(8,128)(2,1)} %fusion.5) | data formatting | bytes 3145728 | tf_op jit(solution)/shard_map/convert_element_type | solution.py:25
  108.0 30.3 %all_to_all.54 = bf16[1,4,128,1536]{3,1,0,2:T(4,128)(2,1)S(1)} all-to-all(bf16[1,4,128,1536]{3,1,0,2:T(4,128)(2,1)} %copy.89), channel_id=1, replica_groups=mesh['dp'=8,'seq'=32] {'seq'}, dimensions={2} | all-to-all | bytes 3145728 | tf_op jit(solution)/shard_map/all_to_all | solution.py:36
  138.4 0.8 copy.90
  139.2 1.1 copy-done.3
  140.3 1.9 fusion.6
  142.1 3.9 %copy.93 = bf16[1,128,4,1536]{3,2,0,1:T(4,128)(2,1)} copy(bf16[1,128,4,1536]{1,3,2,0:T(8,128)(2,1)} %fusion.6) | data formatting | bytes 3145728 | tf_op jit(solution)/shard_map/convert_element_type | solution.py:33
  146.0 5.7 %all-to-all-start.1 = ((bf16[1,128,4,1536]{3,2,0,1:T(4,128)(2,1)}), bf16[1,128,4,1536]{3,2,0,1:T(4,128)(2,1)}, u32[]{:S(2)}, u32[]{:S(2)}) async-start(bf16[1,128,4,1536]{3,2,0,1:T(4,128)(2,1)} %copy.93), calls=%async_computation.1 | async-start | bytes 3145728 | tf_op jit(solution)/shard_map/all_to_all | solution.py:38
  151.8 1.3 fusion.19
  153.2 3.2 %fusion.13 = f32[4,128,128]{2,1,0:T(8,128)} fusion(bf16[128,4,1536]{2,1,0:T(4,128)(2,1)} %bitcast.54, bf16[128,4,1536]{2,1,0:T(4,128)(2,1)} %bitcast.52, f32[128,128]{1,0:T(8,128)S(1)} %convert_reduce_fusion), kind=kOutput, calls=%fused_computation.25 | convolution fusion | flops 201392128 | bytes 3473408 | tf_op jit(solution)/shard_map/nijd,nkjd->jik/dot_general | solution.py:47
  156.4 16.4 %all-to-all-done.1 = bf16[1,128,4,1536]{3,2,0,1:T(4,128)(2,1)} async-done(((bf16[1,128,4,1536]{3,2,0,1:T(4,128)(2,1)}), bf16[1,128,4,1536]{3,2,0,1:T(4,128)(2,1)}, u32[]{:S(2)}, u32[]{:S(2)}) %all-to-all-start.1) | async-done | bytes 1572896 | tf_op jit(solution)/shard_map/all_to_all | solution.py:38
  172.8 1.9 convert_bitcast_fusion
  174.7 3.2 %copy.94 = f32[1,4,32,4,1536]{4,0,3,2,1:T(1,128)S(1)} copy(f32[1,4,32,4,1536]{4,3,1,2,0:T(4,128)S(1)} %convert_bitcast_fusion) | data formatting | bytes 6291456 | tf_op jit(solution)/shard_map/convert_element_type | solution.py:50
  178.0 26.3 %fusion.4 = (bf16[1,512,1536]{2,0,1:T(2,128)(2,1)S(1)}, bf16[1,512,1536]{2,0,1:T(2,128)(2,1)S(1)}) fusion(f32[1,4,32,4,1536]{4,0,3,2,1:T(1,128)S(1)} %copy.94, bf16[1,512,1536]{2,1,0:T(8,128)(2,1)S(1)} %copy-done.1, bf16[1,512,1536]{2,1,0:T(8,128)(2,1)S(1)} %copy-done), kind=kLoop, calls=%fused_computation.10 | loop fusion | flops 4718592 | bytes 9437184 | tf_op jit(solution)/shard_map/convert_element_type | solution.py:52
  204.2 1.5 copy.104
  205.7 1.5 copy.103
  207.2 22.4 %reduce-scatter.5.cloned.1.call-done = f32[4,16,128]{2,1,0:T(8,128)} async-done(((f32[4,128,128]{2,1,0:T(8,128)}), f32[4,16,128]{2,1,0:T(8,128)}) %reduce-scatter.5.cloned.1.call-update) | async-done | bytes 32784 | tf_op jit(solution)/shard_map/reduce_scatter | solution.py:61
  (25 shorter events, 1.4 us)
Async XLA Ops:
  15.3 9.0 %copy-start.8 = (s32[128,16]{0,1:T(8,128)S(1)}, s32[128,16]{0,1:T(8,128)}, u32[]{:S(2)}) copy-start(s32[128,16]{0,1:T(8,128)} %param.12) | copy-start | bytes 24580
  15.3 9.1 %copy-start.6 = (bf16[4,16,128]{2,1,0:T(8,128)(2,1)S(1)}, bf16[4,16,128]{2,1,0:T(8,128)(2,1)}, u32[]{:S(2)}) copy-start(bf16[4,16,128]{2,1,0:T(8,128)(2,1)} %param.11) | copy-start | bytes 49156
  15.3 40.5 %all-to-all-start.2 = ((bf16[1,4,128,1536]{3,1,0,2:T(4,128)(2,1)}), bf16[1,4,128,1536]{3,1,0,2:T(4,128)(2,1)S(1)}, u32[]{:S(2)}, u32[]{:S(2)}) async-start(bf16[1,4,128,1536]{3,1,0,2:T(4,128)(2,1)} %copy.96), calls=%async_computation.2 | async-start | bytes 3145728 | tf_op jit(solution)/shard_map/all_to_all | solution.py:39
  56.5 1.2 copy-start.2
  60.9 7.5 %copy-start.7 = (bf16[4,16,128]{2,1,0:T(8,128)(2,1)S(1)}, bf16[4,16,128]{2,1,0:T(8,128)(2,1)}, u32[]{:S(2)}) copy-start(bf16[4,16,128]{2,1,0:T(8,128)(2,1)} %param.10) | copy-start | bytes 49156
  60.9 36.0 %all-to-all-start.3 = ((bf16[1,128,4,1536]{3,2,0,1:T(4,128)(2,1)}), bf16[1,128,4,1536]{3,2,0,1:T(4,128)(2,1)S(1)}, u32[]{:S(2)}, u32[]{:S(2)}) async-start(bf16[1,128,4,1536]{3,2,0,1:T(4,128)(2,1)} %copy.99), calls=%async_computation.3 | async-start | bytes 3145728 | tf_op jit(solution)/shard_map/all_to_all | solution.py:43
  97.8 1.4 copy-start.4
  97.8 1.9 copy-start.5
  139.1 1.1 copy-start.3
  146.0 26.8 %all-to-all-start.1 = ((bf16[1,128,4,1536]{3,2,0,1:T(4,128)(2,1)}), bf16[1,128,4,1536]{3,2,0,1:T(4,128)(2,1)}, u32[]{:S(2)}, u32[]{:S(2)}) async-start(bf16[1,128,4,1536]{3,2,0,1:T(4,128)(2,1)} %copy.93), calls=%async_computation.1 | async-start | bytes 3145728 | tf_op jit(solution)/shard_map/all_to_all | solution.py:38
  151.7 55.5 %reduce-scatter.3.cloned.1.call-start = ((), (), s32[]{:S(2)}) async-start(), calls=%async_computation.6 | async-start | bytes 294912 | tf_op jit(solution)/shard_map/reduce_scatter | solution.py:62
  153.1 76.5 %reduce-scatter.5.cloned.1.call-start = ((), (), s32[]{:S(2)}) async-start(), calls=%async_computation.7 | async-start | bytes 294912 | tf_op jit(solution)/shard_map/reduce_scatter | solution.py:61
  174.7 3.3 %copy-start = (bf16[1,512,1536]{2,1,0:T(8,128)(2,1)S(1)}, bf16[1,512,1536]{2,1,0:T(8,128)(2,1)}, u32[]{:S(2)}) copy-start(bf16[1,512,1536]{2,1,0:T(8,128)(2,1)} %param.7) | copy-start | bytes 4718596
  174.7 3.3 %copy-start.1 = (bf16[1,512,1536]{2,1,0:T(8,128)(2,1)S(1)}, bf16[1,512,1536]{2,1,0:T(8,128)(2,1)}, u32[]{:S(2)}) copy-start(bf16[1,512,1536]{2,1,0:T(8,128)(2,1)} %param.13) | copy-start | bytes 4718596
Sparse Core Ops, SparseCore 0:
  155.7 35.7 reduce-scatter.2
  194.7 34.8 reduce-scatter.4
where the time goes:
time: 237 us; the launch traced here: 236 us
  blocking collectives  89.7 us (38%)
  waiting for transfers between devices  38.8 us (16%)
  other arithmetic  36.5 us (15%)
  local copies, waits for them, and re-layouts  25.2 us (11%)
  starting transfers between devices  22.3 us (9%)
  between operations  14.2 us (6%)
  matrix products  9.53 us (4%)
    all_gather x1, blocking collectives, on_device(): full_mix = lax.all_gather(mix_weights, 'dp', axis=1, tiled=True)  30.9 us
    all_to_all x1, blocking collectives, on_device(): lax.all_to_all(first_factor, 'seq', split_axis=2, concat_axis=1, tiled=True)  30.3 us
    all_gather x1, blocking collectives, on_device(): full_blocks = lax.all_gather(block_weights, 'dp', axis=1, tiled=True)  28.5 us
    convert_element_type x1, other arithmetic, on_device(): grad_query = (cot_f * mixed_f).astype(jnp.bfloat16)  26.3 us
    reduce_scatter x1, waiting for transfers between devices, on_device(): lax.psum_scatter(mix_terms, 'dp', scatter_dimension=1, tiled=True)  22.4 us
    all_to_all x1, waiting for transfers between devices, on_device(): lax.all_to_all(mixed_cols, 'seq', split_axis=1, concat_axis=2, tiled=True)  16.4 us
    all_to_all x1, starting transfers between devices, on_device(): lax.all_to_all(grad_mixed, 'seq', split_axis=2, concat_axis=1, tiled=True)  9.02 us
    all_to_all x1, starting transfers between devices, on_device(): lax.all_to_all(grad_first_cols, 'seq', split_axis=1, concat_axis=2, tiled...  7.5 us
  transfers between devices with their start and end apart: 5, of which 2 were waited for; matrix products, arithmetic and copies ran while one was open for 17% of the time, Pallas kernels for 0%

commit v1 on v0

v1 whole, which is shorter than its diff:
```python
import jax
import jax.numpy as jnp
from jax import lax
from jax.experimental import pallas as pl
from jax.experimental.pallas import tpu as pltpu
from jax.sharding import PartitionSpec as P

BF16 = jnp.bfloat16
F32 = jnp.float32
VMEM_LIMIT = 48 * 1024 * 1024


def dot(a, b, ca=1, cb=0):
    return lax.dot_general(a, b, (((ca,), (cb,)), ((), ())), preferred_element_type=F32)


def one_hot(size, column_of):
    rows = lax.broadcasted_iota(jnp.int32, (size, size), 0)
    columns = lax.broadcasted_iota(jnp.int32, (size, size), 1)
    return (columns == column_of(rows)).astype(F32).astype(BF16)


def slab_order(r):
    return ((r >> 2) & 3) * 64 + (r >> 4) * 4 + (r & 3)


def offset_order(r):
    return (r & 63) * 4 + (r >> 6)


def to_slabs(perm, x):
    halves = []
    for g in range(2):
        part = jnp.concatenate([x[k * 128 + g * 64 : k * 128 + g * 64 + 64] for k in range(4)], axis=0)
        halves.append(dot(perm, part).astype(BF16))
    return jnp.concatenate(halves, axis=0)


def from_slabs(perm, x):
    halves = [dot(perm, x[g * 256 : g * 256 + 256], ca=0).astype(BF16) for g in range(2)]
    return [jnp.concatenate([h[k * 64 : k * 64 + 64] for h in halves], axis=0) for k in range(4)]


def by_offset(perm, x):
    halves = [dot(perm, x[g * 256 : g * 256 + 256]).astype(BF16) for g in range(2)]
    return [jnp.concatenate([h[j * 64 : j * 64 + 64] for h in halves], axis=0) for j in range(4)]


def times(a, b):
    return (a.astype(F32) * b.astype(F32)).astype(BF16)


def call(kernel, name, grid, in_specs, out_specs, out_shape, scratch=(), flops=0, nbytes=0, aliases=None):
    return pl.pallas_call(
        kernel,
        name=name,
        grid=grid,
        in_specs=in_specs,
        out_specs=out_specs,
        out_shape=out_shape,
        scratch_shapes=list(scratch),
        input_output_aliases=aliases or {},
        cost_estimate=pl.CostEstimate(flops=flops, transcendentals=0, bytes_accessed=nbytes),
        compiler_params=pltpu.CompilerParams(
            vmem_limit_bytes=VMEM_LIMIT, dimension_semantics=("arbitrary",) * len(grid)
        ),
    )


def rows_spec(width):
    return pl.BlockSpec((512, width), lambda d: (0, d))


def slab_spec(width, half=0):
    return pl.BlockSpec((32, 16, width), lambda d: (0, half, d))


def whole(*shape):
    return pl.BlockSpec(shape, lambda *g: (0,) * len(shape))


def gate_kernel(q_ref, c_ref, o_ref, perm):
    @pl.when(pl.program_id(0) == 0)
    def _():
        perm[...] = one_hot(256, slab_order)

    o_ref[...] = to_slabs(perm[...], times(q_ref[...], c_ref[...])).reshape(o_ref.shape)


def first_kernel(w_ref, k_ref, v_ref, o_ref, perm, blocks):
    @pl.when(pl.program_id(0) == 0)
    def _():
        perm[...] = one_hot(256, slab_order)
        for s in range(8):
            blocks[:, s * 16 : s * 16 + 16, :] = w_ref[s, 0:4]

    product = times(k_ref[...], v_ref[...])
    first = jnp.concatenate(
        [dot(blocks[k], product[k * 128 : k * 128 + 128]).astype(BF16) for k in range(4)], axis=0
    )
    o_ref[...] = to_slabs(perm[...], first).reshape(o_ref.shape)


def factor_kernel(w_ref, idx_ref, m_ref, mt_ref, p_ref, diag):
    columns = lax.broadcasted_iota(jnp.int32, (128, 128), 1)
    hits = jnp.zeros((128, 128), F32)
    for n in range(idx_ref.shape[1]):
        hits = jnp.maximum(hits, (idx_ref[:, n : n + 1] == columns).astype(F32))
    p_ref[...] = hits
    diag[...] = jnp.zeros_like(diag)
    for j in range(4):
        mix = jnp.concatenate([w_ref[s, 4 + j] for s in range(8)], axis=0).astype(F32)
        diag[j * 128 : j * 128 + 128, j * 128 : j * 128 + 128] = (mix * hits).astype(BF16)
    spread = one_hot(512, lambda r: (r & 3) * 128 + (r >> 2))
    rows = dot(spread, diag[...]).astype(BF16)
    m_ref[...] = dot(rows, spread, cb=1).astype(BF16)
    rows_t = dot(spread, diag[...], cb=1).astype(BF16)
    mt_ref[...] = dot(rows_t, spread, cb=1).astype(BF16)


def back_kernel(m_ref, x_ref, _, o_ref):
    x = x_ref[...].reshape(512, x_ref.shape[2])
    o_ref[...] = dot(m_ref[...], x).astype(BF16).reshape(o_ref.shape)


def mix_kernel(m_ref, x_ref, o_ref):
    x = x_ref[...].reshape(512, x_ref.shape[2])
    o_ref[...] = dot(m_ref[...], x).astype(BF16).reshape(o_ref.shape)


def grads_kernel(core_ref, w_ref, pat_ref, gm_ref, f_ref, gf_ref, k_ref, v_ref, gk_ref, gv_ref, send_ref, keep_ref,
                 perm, sort, blocks, acc):
    @pl.when(pl.program_id(0) == 0)
    def _():
        perm[...] = one_hot(256, slab_order)
        sort[...] = one_hot(256, offset_order)
        for s in range(8):
            blocks[:, s * 16 : s * 16 + 16, :] = w_ref[s, 0:4]
        acc[...] = jnp.zeros_like(acc)

    width = k_ref.shape[1]
    grad_first = from_slabs(perm[...], gf_ref[...].reshape(512, width))
    for k in range(4):
        rows = slice(k * 128, k * 128 + 128)
        key, value = k_ref[rows, :].astype(F32), v_ref[rows, :].astype(F32)
        acc[k] += dot(grad_first[k], (key * value).astype(BF16), cb=1)
        grad = dot(blocks[k], grad_first[k], ca=0)
        gk_ref[rows, :] = (grad * value).astype(BF16)
        gv_ref[rows, :] = (grad * key).astype(BF16)
    left = by_offset(sort[...], gm_ref[...].reshape(512, width))
    right = by_offset(sort[...], f_ref[...].reshape(512, width))
    for j in range(4):
        acc[4 + j] += dot(left[j], right[j], cb=1)

    @pl.when(pl.program_id(0) == pl.num_programs(0) - 1)
    def _():
        for j in range(4):
            acc[4 + j] = acc[4 + j] * pat_ref[...]
        core = core_ref[0]
        for z in range(4):
            keep_ref[z] = acc[:, pl.ds(pl.multiple_of(z * 32 + core * 16, 16), 16), :]
            send_ref[z] = acc[:, pl.ds(pl.multiple_of(z * 32 + 16 - core * 16, 16), 16), :]


def pair_kernel(z_ref, keep_ref, got_ref, own_ref, *out_refs):
    z = z_ref[0]
    own_ref[...] = keep_ref[z] + got_ref[z]
    for r, out in enumerate(out_refs, start=1):
        t = lax.rem(z + r, 4)
        out[...] = (keep_ref[t] + got_ref[t]).astype(BF16)


def tail_kernel(x_ref, q_ref, c_ref, o_ref, gq_ref, perm):
    @pl.when(pl.program_id(0) == 0)
    def _():
        perm[...] = one_hot(256, slab_order)

    mixed = from_slabs(perm[...], x_ref[...].reshape(512, x_ref.shape[2]))
    for k in range(4):
        rows = slice(k * 128, k * 128 + 128)
        m = mixed[k].astype(F32)
        o_ref[rows, :] = (q_ref[rows, :].astype(F32) * m).astype(BF16)
        gq_ref[rows, :] = (c_ref[rows, :].astype(F32) * m).astype(BF16)


def on_device(query, key, value, block_weights, mix_weights, block_index, cotangent):
    channels = query.shape[2]
    q, k, v, cot = (a.reshape(512, channels) for a in (query, key, value, cotangent))
    width = 256
    grid = (channels // width,)
    rows, slab = rows_spec(width), slab_spec(width)
    smem = pl.BlockSpec(memory_space=pltpu.SMEM)
    row_shape = jax.ShapeDtypeStruct((512, channels), BF16)
    slab_shape = jax.ShapeDtypeStruct((32, 16, channels), BF16)
    pair_shape = jax.ShapeDtypeStruct((32, 32, channels), BF16)
    perm = pltpu.VMEM((256, 256), BF16)
    size = 512 * channels * 2
    work = 2 * 512 * 512 * channels

    def exchange(x):
        return lax.all_to_all(x, "seq", split_axis=0, concat_axis=0, tiled=True)

    place = lax.axis_index("dp")
    core = (place % 2).reshape(1)
    z = (place // 2).reshape(1)

    gated = call(gate_kernel, "gate", grid, [rows, rows], slab, slab_shape, [perm], work // 2, 3 * size)(q, cot)
    grad_cols = exchange(gated)

    weights = lax.all_gather(jnp.concatenate([block_weights, mix_weights], axis=0), "dp", axis=0)
    weights_spec = whole(8, 8, 16, 128)
    out = call(
        first_kernel, "first", grid, [weights_spec, rows, rows], slab, pair_shape,
        [perm, pltpu.VMEM((4, 128, 128), BF16)], work, 3 * size,
    )(weights, k, v)
    factor, factor_t, pattern = call(
        factor_kernel, "factor", (), [weights_spec, whole(128, 16)],
        [whole(512, 512), whole(512, 512), whole(128, 128)],
        [jax.ShapeDtypeStruct((512, 512), BF16), jax.ShapeDtypeStruct((512, 512), BF16), jax.ShapeDtypeStruct((128, 128), F32)],
        [pltpu.VMEM((512, 512), BF16)], work, size,
    )(weights, block_index)
    square = whole(512, 512)
    out = call(
        back_kernel, "back", grid, [square, slab, pl.BlockSpec(memory_space=pl.ANY)],
        slab_spec(width, 1), pair_shape, (), work, 2 * size, {2: 0},
    )(factor_t, grad_cols, out)
    got = exchange(out)
    mixed_cols = call(mix_kernel, "mix", grid, [square, slab], slab, slab_shape, (), work, 2 * size)(factor, got)
    returned = exchange(mixed_cols)

    part = jax.ShapeDtypeStruct((4, 8, 16, 128), F32)
    grad_key, grad_value, send, keep = call(
        grads_kernel, "grads", grid,
        [smem, weights_spec, whole(128, 128), slab, slab, slab_spec(width, 1), rows, rows],
        [rows, rows, whole(4, 8, 16, 128), whole(4, 8, 16, 128)], [row_shape, row_shape, part, part],
        [perm, perm, pltpu.VMEM((4, 128, 128), BF16), pltpu.VMEM((8, 128, 128), F32)], 4 * work, 7 * size,
    )(core, weights, pattern, grad_cols, got, got, k, v)
    swapped = lax.ppermute(send, "dp", [(i, i ^ 1) for i in range(8)])
    shard = jax.ShapeDtypeStruct((8, 16, 128), BF16)
    own, *others = call(
        pair_kernel, "pair", (), [smem, whole(4, 8, 16, 128), whole(4, 8, 16, 128)], [whole(8, 16, 128)] * 4,
        [jax.ShapeDtypeStruct((8, 16, 128), F32), shard, shard, shard],
    )(z, keep, swapped)
    total = own
    for r, other in enumerate(others, start=1):
        hop = [(i, ((i // 2 + r) % 4) * 2 + i % 2) for i in range(8)]
        total = total + lax.ppermute(other, "dp", hop).astype(F32)

    output, grad_query = call(
        tail_kernel, "tail", grid, [slab, rows, rows], [rows, rows], [row_shape, row_shape], [perm], work // 2, 5 * size
    )(returned, q, cot)
    wide = query.shape
    return (
        output.reshape(wide), grad_query.reshape(wide), grad_key.reshape(wide), grad_value.reshape(wide),
        total[0:4], total[4:8],
    )


def solution(mesh):
    placed = (
        P("dp", "seq", None),
        P("dp", "seq", None),
        P("dp", "seq", None),
        P("seq", "dp", None),
        P("seq", "dp", None),
        P(),
        P("dp", "seq", None),
    )
    return jax.shard_map(
        on_device,
        mesh=mesh,
        in_specs=placed,
        out_specs=(
            P("dp", "seq", None),
            P("dp", "seq", None),
            P("dp", "seq", None),
            P("dp", "seq", None),
            P("seq", "dp", None),
            P("seq", "dp", None),
        ),
        check_vma=False,
    )
```

time: 237 us -> 147 us (0.62)
  other arithmetic: 36.5 us -> 0.02 us
  waiting for transfers between devices: 38.8 us -> 4.57 us
  Pallas kernels: 0 us -> 25.3 us
  between operations: 14.2 us -> 0.81 us
  blocking collectives: 89.7 us -> 77.5 us
  matrix products: 9.53 us -> 0 us
  local copies, waits for them, and re-layouts: 25.2 us -> 15.8 us
    convert_element_type x4 -> x0, other arithmetic: 36.1 us -> none  [the longest x1 26.3 us: on_device(): grad_query = (cot_f * mixed_f).astype(jnp.bfloat16)]
    all_gather x2 -> x1, blocking collectives: 59.4 us -> 31.2 us  [on_device(): lax.all_gather(jnp.concatenate([block_weights, mix_weights], axis=0), 'dp...]
    pallas_call x0 -> x8, Pallas kernels: none -> 25.3 us  [the longest x1 8.02 us: on_device(): call(grads_kernel, 'grads', grid, [smem, weights_spec, whole(128, 128), s...]
    reduce_scatter x2 -> x0, waiting for transfers between devices: 22.4 us -> none  [the longest x1 22.4 us: on_device(): lax.psum_scatter(mix_terms, 'dp', scatter_dimension=1, tiled=True)]
    all_to_all x3 -> x2, waiting for transfers between devices: 16.4 us -> 0.01 us  [exchange(): return lax.all_to_all(x, 'seq', split_axis=0, concat_axis=0, tiled=True)]
    all_to_all x1, blocking collectives: 30.3 us -> 46.3 us  [exchange(): return lax.all_to_all(x, 'seq', split_axis=0, concat_axis=0, tiled=True)]
    convert_element_type x4 -> x0, local copies, waits for them, and re-layouts: 13.4 us -> none  [the longest x1 3.86 us: on_device(): first_factor = jnp.einsum('iac,nicd->niad', full_blocks, split_parts, pre...]
    dot_general x6 -> x0, matrix products: 9.53 us -> none  [the longest x1 3.19 us: on_device(): jnp.einsum('nijd,nkjd->jik', grad_cols, across, preferred_element_type=jn...]
  transfers between devices with their start and end apart: 5 -> 6, of which waited for: 2 -> 2; matrix products, arithmetic and copies ran while one was open for 17% -> 1% of each run, Pallas kernels for 0% -> 10%
where the time goes in v1:
time: 147 us; the launch traced here: 146 us
  blocking collectives  77.5 us (53%)
  Pallas kernels  25.3 us (17%)
  starting transfers between devices  22.1 us (15%)
  local copies, waits for them, and re-layouts  15.8 us (11%)
  waiting for transfers between devices  4.57 us (3%)
    all_to_all x1, blocking collectives, exchange(): return lax.all_to_all(x, 'seq', split_axis=0, concat_axis=0, tiled=True)  46.3 us
    all_gather x1, blocking collectives, on_device(): lax.all_gather(jnp.concatenate([block_weights, mix_weights], axis=0), 'dp...  31.2 us
    unnamed x41, local copies, waits for them, and re-layouts  15.2 us
    all_to_all x2, starting transfers between devices, exchange(): return lax.all_to_all(x, 'seq', split_axis=0, concat_axis=0, tiled=True)  14.4 us
    pallas_call x1, Pallas kernels, on_device(): call(grads_kernel, 'grads', grid, [smem, weights_spec, whole(128, 128), s...  8.02 us
    ppermute x3, starting transfers between devices, on_device(): total = total + lax.ppermute(other, 'dp', hop).astype(F32)  7.77 us
    pallas_call x1, Pallas kernels, on_device(): call(first_kernel, 'first', grid, [weights_spec, rows, rows], slab, pair_...  4.2 us
    pallas_call x1, Pallas kernels, on_device(): call(tail_kernel, 'tail', grid, [slab, rows, rows], [rows, rows], [row_sh...  3.86 us
  transfers between devices with their start and end apart: 6, of which 2 were waited for; matrix products, arithmetic and copies ran while one was open for 1% of the time, Pallas kernels for 10%

profile of v1, /device:TPU:8, one launch (start us, length us, event | category | flops | bytes accessed | tf_op | source)
XLA Modules:
  0.0 146.1 jit_solution(4086581407966548064)
XLA Ops:
  0.6 0.0 copy-start.5
  0.6 1.4 copy-done.5
  2.0 1.4 copy-done.7
  3.5 3.4 %gate.1 = bf16[32,16,1536]{2,1,0:T(8,128)(2,1)} custom-call(bf16[512,1536]{1,0:T(8,128)(2,1)S(1)} %bitcast.11, bf16[512,1536]{1,0:T(8,128)(2,1)S(1)} %bitcast.13), custom_call_target="tpu_custom_call" | custom-call | flops 402653184 | bytes 4718592 | tf_op jit(solution)/shard_map/gate/pallas_call | solution.py:207
  6.9 9.0 %all-to-all-start = ((bf16[32,16,1536]{2,1,0:T(8,128)(2,1)}), bf16[32,16,1536]{2,1,0:T(8,128)(2,1)S(1)}, u32[]{:S(2)}, u32[]{:S(2)}) async-start(bf16[32,16,1536]{2,1,0:T(8,128)(2,1)} %gate.1), calls=%async_computation | async-start | bytes 3145728 | tf_op jit(solution)/shard_map/all_to_all | solution.py:201
  15.9 0.1 copy.15.idx_ref
  16.0 31.2 %all-gather = bf16[64,16,128]{2,1,0:T(8,128)(2,1)S(1)} all-gather(bf16[8,16,128]{2,1,0:T(8,128)(2,1)S(1)} %pad_maximum_fusion), channel_id=2, replica_groups=mesh['dp'=8,'seq'=32] {'dp'}, dimensions={0}, use_global_device_ids=true | all-gather | bytes 294912 | tf_op jit(solution)/shard_map/all_gather | solution.py:210
  47.3 1.8 %factor.1 = (bf16[512,512]{1,0:T(8,128)(2,1)S(1)}, bf16[512,512]{1,0:T(8,128)(2,1)S(1)}, f32[128,128]{1,0:T(8,128)S(1)}) custom-call(bf16[8,8,16,128]{3,2,1,0:T(8,128)(2,1)S(1)} %bitcast.19, s32[128,16]{1,0:T(8,128)S(1)} %copy.15.idx_ref), custom_call_target="tpu_custom_call" | custom-call | flops 805306368 | bytes 1572864 | tf_op jit(solution)/shard_map/factor/pallas_call | solution.py:216
  49.0 0.0 copy-start.13
  49.0 0.8 copy-done.13
  49.8 4.2 %first.1._ = bf16[32,32,1536]{2,1,0:T(8,128)(2,1)} custom-call(bf16[8,8,16,128]{3,2,1,0:T(8,128)(2,1)S(1)} %bitcast.20, bf16[512,1536]{1,0:T(8,128)(2,1)S(1)} %bitcast.15, bf16[512,1536]{1,0:T(8,128)(2,1)S(1)} %bitcast.17), custom_call_target="tpu_custom_call" | custom-call | flops 805306368 | bytes 4718592 | tf_op jit(solution)/shard_map/first/pallas_call | solution.py:212
  54.0 1.9 %copy-done = bf16[32,32,1536]{2,1,0:T(8,128)(2,1)S(1)} copy-done((bf16[32,32,1536]{2,1,0:T(8,128)(2,1)S(1)}, bf16[32,32,1536]{2,1,0:T(8,128)(2,1)}, u32[]{:S(2)}) %copy-start) | copy-done | bytes 3145752
  55.9 2.0 %back.1 = bf16[32,32,1536]{2,1,0:T(8,128)(2,1)S(1)} custom-call(bf16[512,512]{1,0:T(8,128)(2,1)S(1)} %get-tuple-element.20.m_ref, bf16[32,16,1536]{2,1,0:T(8,128)(2,1)S(1)} %all-to-all-done.x_ref.gm_ref, bf16[32,32,1536]{2,1,0:T(8,128)(2,1)S(1)} %copy-done), custom_call_target="tpu_custom_call", output_to_operand_aliasing={{}: (2, {})} | custom-call | flops 805306368 | bytes 3145728 | tf_op jit(solution)/shard_map/back/pallas_call | solution.py:223
  57.9 1.1 copy-done.2
  59.1 46.3 %all_to_all.15.x_ref.f_ref.gf_ref = bf16[32,32,1536]{2,1,0:T(8,128)(2,1)S(1)} all-to-all(bf16[32,32,1536]{2,1,0:T(8,128)(2,1)S(1)} %back.1), channel_id=1, replica_groups=mesh['dp'=8,'seq'=32] {'seq'}, dimensions={0} | all-to-all | bytes 6291456 | tf_op jit(solution)/shard_map/all_to_all | solution.py:201
  105.3 2.0 %mix.1 = bf16[32,16,1536]{2,1,0:T(8,128)(2,1)S(1)} custom-call(bf16[512,512]{1,0:T(8,128)(2,1)S(1)} %copy-done.14, bf16[32,32,1536]{2,1,0:T(8,128)(2,1)S(1)} %all_to_all.15.x_ref.f_ref.gf_ref), custom_call_target="tpu_custom_call" | custom-call | flops 805306368 | bytes 3145728 | tf_op jit(solution)/shard_map/mix/pallas_call | solution.py:228
  107.4 1.1 copy-done.4
  108.5 5.4 %all-to-all-start.2 = ((bf16[32,16,1536]{2,1,0:T(8,128)(2,1)}), bf16[32,16,1536]{2,1,0:T(8,128)(2,1)S(1)}, u32[]{:S(2)}, u32[]{:S(2)}) async-start(bf16[32,16,1536]{2,1,0:T(8,128)(2,1)} %copy-done.4), calls=%async_computation.2 | async-start | bytes 3145728 | tf_op jit(solution)/shard_map/all_to_all | solution.py:201
  113.9 1.4 copy-done.3
  115.3 1.4 copy-done.10
  116.7 1.4 copy-done.12
  118.1 8.0 %grads.1 = (bf16[512,1536]{1,0:T(8,128)(2,1)}, bf16[512,1536]{1,0:T(8,128)(2,1)}, f32[4,8,16,128]{3,2,1,0:T(8,128)}, f32[4,8,16,128]{3,2,1,0:T(8,128)S(1)}) custom-call(s32[1]{0:T(128)} %bitcast.7.core_ref, bf16[8,8,16,128]{3,2,1,0:T(8,128)(2,1)S(1)} %bitcast.21, f32[128,128]{1,0:T(8,128)S(1)} %get-tuple-element.23.pat_ref, ...), custom_call_target="tpu_custom_call" | custom-call | flops 3221225472 | bytes 11010048 | tf_op jit(solution)/shard_map/grads/pallas_call | solution.py:232
  126.1 0.7 copy-done.15
  126.8 1.7 %collective-permute-done.got_ref = f32[4,8,16,128]{3,2,1,0:T(8,128)S(1)} collective-permute-done((f32[4,8,16,128]{3,2,1,0:T(8,128)}, f32[4,8,16,128]{3,2,1,0:T(8,128)S(1)}, u32[]{:S(2)}, u32[]{:S(2)}) %collective-permute-start) | collective-permute-done | bytes 262176 | tf_op jit(solution)/shard_map/ppermute | solution.py:238
  128.6 0.9 copy-done.16
  129.5 2.4 %collective-permute-start.1 = (bf16[8,16,128]{2,1,0:T(8,128)(2,1)S(1)}, bf16[8,16,128]{2,1,0:T(8,128)(2,1)S(1)}, u32[]{:S(2)}, u32[]{:S(2)}) collective-permute-start(bf16[8,16,128]{2,1,0:T(8,128)(2,1)S(1)} %get-tuple-element.29), channel_id=1, source_target_pairs={{0,64},{32,96},{64,128},{96,160},{128,192},{160,224},{192,0},{224,... | collective-permute-start | bytes 98312 | tf_op jit(solution)/shard_map/ppermute | solution.py:247
  132.0 2.5 %collective-permute-start.2 = (bf16[8,16,128]{2,1,0:T(8,128)(2,1)S(1)}, bf16[8,16,128]{2,1,0:T(8,128)(2,1)S(1)}, u32[]{:S(2)}, u32[]{:S(2)}) collective-permute-start(bf16[8,16,128]{2,1,0:T(8,128)(2,1)S(1)} %get-tuple-element.30), channel_id=1, source_target_pairs={{0,128},{32,160},{64,192},{96,224},{128,0},{160,32},{192,64},{224,... | collective-permute-start | bytes 98312 | tf_op jit(solution)/shard_map/ppermute | solution.py:247
  134.5 2.8 %collective-permute-start.3 = (bf16[8,16,128]{2,1,0:T(8,128)(2,1)S(1)}, bf16[8,16,128]{2,1,0:T(8,128)(2,1)S(1)}, u32[]{:S(2)}, u32[]{:S(2)}) collective-permute-start(bf16[8,16,128]{2,1,0:T(8,128)(2,1)S(1)} %get-tuple-element.31), channel_id=1, source_target_pairs={{0,192},{32,224},{64,0},{96,32},{128,64},{160,96},{192,128},{224,1... | collective-permute-start | bytes 98312 | tf_op jit(solution)/shard_map/ppermute | solution.py:247
  137.3 2.8 %collective-permute-done.2 = bf16[8,16,128]{2,1,0:T(8,128)(2,1)S(1)} collective-permute-done((bf16[8,16,128]{2,1,0:T(8,128)(2,1)S(1)}, bf16[8,16,128]{2,1,0:T(8,128)(2,1)S(1)}, u32[]{:S(2)}, u32[]{:S(2)}) %collective-permute-start.2) | collective-permute-done | bytes 32800 | tf_op jit(solution)/shard_map/ppermute | solution.py:247
  140.2 0.6 fusion
  140.8 1.4 copy-done.8
  142.2 3.9 %tail.1 = (bf16[512,1536]{1,0:T(8,128)(2,1)}, bf16[512,1536]{1,0:T(8,128)(2,1)}) custom-call(bf16[32,16,1536]{2,1,0:T(8,128)(2,1)S(1)} %all-to-all-done.2.x_ref, bf16[512,1536]{1,0:T(8,128)(2,1)S(1)} %bitcast.12, bf16[512,1536]{1,0:T(8,128)(2,1)S(1)} %bitcast.14), custom_call_target="tpu_custom_call" | custom-call | flops 402653184 | bytes 7864320 | tf_op jit(solution)/shard_map/tail/pallas_call | solution.py:249
  (34 shorter events, 0.1 us)
Async XLA Ops:
  0.6 1.4 copy-start.5
  2.0 1.4 copy-start.7
  6.9 9.0 %copy-start.19 = (s32[128,16]{0,1:T(8,128)S(1)}, s32[128,16]{0,1:T(8,128)}, u32[]{:S(2)}) copy-start(s32[128,16]{0,1:T(8,128)} %param.12) | copy-start | bytes 24580
  6.9 9.1 %copy-start.17 = (bf16[4,16,128]{2,1,0:T(8,128)(2,1)S(1)}, bf16[4,16,128]{2,1,0:T(8,128)(2,1)}, u32[]{:S(2)}) copy-start(bf16[4,16,128]{2,1,0:T(8,128)(2,1)} %param.11) | copy-start | bytes 49156
  6.9 9.1 %copy-start.18 = (bf16[4,16,128]{2,1,0:T(8,128)(2,1)S(1)}, bf16[4,16,128]{2,1,0:T(8,128)(2,1)}, u32[]{:S(2)}) copy-start(bf16[4,16,128]{2,1,0:T(8,128)(2,1)} %param.10) | copy-start | bytes 49156
  6.9 47.2 %all-to-all-start = ((bf16[32,16,1536]{2,1,0:T(8,128)(2,1)}), bf16[32,16,1536]{2,1,0:T(8,128)(2,1)S(1)}, u32[]{:S(2)}, u32[]{:S(2)}) async-start(bf16[32,16,1536]{2,1,0:T(8,128)(2,1)} %gate.1), calls=%async_computation | async-start | bytes 3145728 | tf_op jit(solution)/shard_map/all_to_all | solution.py:201
  16.0 33.8 %copy-start.9 = (bf16[1,512,1536]{2,1,0:T(8,128)(2,1)S(1)}, bf16[1,512,1536]{2,1,0:T(8,128)(2,1)}, u32[]{:S(2)}) copy-start(bf16[1,512,1536]{2,1,0:T(8,128)(2,1)} %param.8) | copy-start | bytes 4718596
  16.0 33.8 %copy-start.11 = (bf16[1,512,1536]{2,1,0:T(8,128)(2,1)S(1)}, bf16[1,512,1536]{2,1,0:T(8,128)(2,1)}, u32[]{:S(2)}) copy-start(bf16[1,512,1536]{2,1,0:T(8,128)(2,1)} %param.9) | copy-start | bytes 4718596
  49.0 0.8 copy-start.13
  54.0 1.9 %copy-start = (bf16[32,32,1536]{2,1,0:T(8,128)(2,1)S(1)}, bf16[32,32,1536]{2,1,0:T(8,128)(2,1)}, u32[]{:S(2)}) copy-start(bf16[32,32,1536]{2,1,0:T(8,128)(2,1)} %first.1._) | copy-start | bytes 9437188
  57.9 1.1 copy-start.2
  59.1 46.3 %copy-start.14 = (bf16[512,512]{1,0:T(8,128)(2,1)S(1)}, bf16[512,512]{1,0:T(8,128)(2,1)}, u32[]{:S(2)}) copy-start(bf16[512,512]{1,0:T(8,128)(2,1)} %copy-done.13) | copy-start | bytes 1572868
  105.3 2.0 %copy-start.1 = (bf16[32,32,1536]{2,1,0:T(8,128)(2,1)}, bf16[32,32,1536]{2,1,0:T(8,128)(2,1)S(1)}, u32[]{:S(2)}) copy-start(bf16[32,32,1536]{2,1,0:T(8,128)(2,1)S(1)} %all_to_all.15.x_ref.f_ref.gf_ref) | copy-start | bytes 9437188
  107.3 1.1 copy-start.4
  108.5 32.3 %all-to-all-start.2 = ((bf16[32,16,1536]{2,1,0:T(8,128)(2,1)}), bf16[32,16,1536]{2,1,0:T(8,128)(2,1)S(1)}, u32[]{:S(2)}, u32[]{:S(2)}) async-start(bf16[32,16,1536]{2,1,0:T(8,128)(2,1)} %copy-done.4), calls=%async_computation.2 | async-start | bytes 3145728 | tf_op jit(solution)/shard_map/all_to_all | solution.py:201
  113.9 1.4 copy-start.3
  115.3 1.4 copy-start.10
  116.7 1.4 copy-start.12
  118.1 22.7 %copy-start.6 = (bf16[1,512,1536]{2,1,0:T(8,128)(2,1)S(1)}, bf16[1,512,1536]{2,1,0:T(8,128)(2,1)}, u32[]{:S(2)}) copy-start(bf16[1,512,1536]{2,1,0:T(8,128)(2,1)} %param.7) | copy-start | bytes 4718596
  126.1 0.7 copy-start.15
  126.8 1.7 %collective-permute-start = (f32[4,8,16,128]{3,2,1,0:T(8,128)}, f32[4,8,16,128]{3,2,1,0:T(8,128)S(1)}, u32[]{:S(2)}, u32[]{:S(2)}) collective-permute-start(f32[4,8,16,128]{3,2,1,0:T(8,128)} %get-tuple-element.27), channel_id=1, source_target_pairs={{0,32},{32,0},{64,96},{96,64},{128,160},{160,128},{192,224},{224,1... | collective-permute-start | bytes 786440 | tf_op jit(solution)/shard_map/ppermute | solution.py:238
  128.6 1.0 copy-start.16
  129.5 7.8 %collective-permute-start.1 = (bf16[8,16,128]{2,1,0:T(8,128)(2,1)S(1)}, bf16[8,16,128]{2,1,0:T(8,128)(2,1)S(1)}, u32[]{:S(2)}, u32[]{:S(2)}) collective-permute-start(bf16[8,16,128]{2,1,0:T(8,128)(2,1)S(1)} %get-tuple-element.29), channel_id=1, source_target_pairs={{0,64},{32,96},{64,128},{96,160},{128,192},{160,224},{192,0},{224,... | collective-permute-start | bytes 98312 | tf_op jit(solution)/shard_map/ppermute | solution.py:247
  132.0 8.2 %collective-permute-start.2 = (bf16[8,16,128]{2,1,0:T(8,128)(2,1)S(1)}, bf16[8,16,128]{2,1,0:T(8,128)(2,1)S(1)}, u32[]{:S(2)}, u32[]{:S(2)}) collective-permute-start(bf16[8,16,128]{2,1,0:T(8,128)(2,1)S(1)} %get-tuple-element.30), channel_id=1, source_target_pairs={{0,128},{32,160},{64,192},{96,224},{128,0},{160,32},{192,64},{224,... | collective-permute-start | bytes 98312 | tf_op jit(solution)/shard_map/ppermute | solution.py:247
  134.5 5.6 %collective-permute-start.3 = (bf16[8,16,128]{2,1,0:T(8,128)(2,1)S(1)}, bf16[8,16,128]{2,1,0:T(8,128)(2,1)S(1)}, u32[]{:S(2)}, u32[]{:S(2)}) collective-permute-start(bf16[8,16,128]{2,1,0:T(8,128)(2,1)S(1)} %get-tuple-element.31), channel_id=1, source_target_pairs={{0,192},{32,224},{64,0},{96,32},{128,64},{160,96},{192,128},{224,1... | collective-permute-start | bytes 98312 | tf_op jit(solution)/shard_map/ppermute | solution.py:247
  140.8 1.4 copy-start.8

commit v2 on v1

--- a/solution.py
+++ b/solution.py
@@ -7,7 +7,7 @@
 
 BF16 = jnp.bfloat16
 F32 = jnp.float32
-VMEM_LIMIT = 48 * 1024 * 1024
+MIB = 1024 * 1024
 
 
 def dot(a, b, ca=1, cb=0):
@@ -50,7 +50,7 @@
     return (a.astype(F32) * b.astype(F32)).astype(BF16)
 
 
-def call(kernel, name, grid, in_specs, out_specs, out_shape, scratch=(), flops=0, nbytes=0, aliases=None):
+def call(kernel, name, grid, in_specs, out_specs, out_shape, scratch=(), flops=0, nbytes=0, aliases=None, vmem=8):
     return pl.pallas_call(
         kernel,
         name=name,
@@ -62,7 +62,7 @@
         input_output_aliases=aliases or {},
         cost_estimate=pl.CostEstimate(flops=flops, transcendentals=0, bytes_accessed=nbytes),
         compiler_params=pltpu.CompilerParams(
-            vmem_limit_bytes=VMEM_LIMIT, dimension_semantics=("arbitrary",) * len(grid)
+            vmem_limit_bytes=vmem * MIB, dimension_semantics=("arbitrary",) * len(grid)
         ),
     )
 
@@ -79,6 +79,9 @@
     return pl.BlockSpec(shape, lambda *g: (0,) * len(shape))
 
 
+VMEM_SPEC = pl.BlockSpec(memory_space=pltpu.VMEM)
+
+
 def gate_kernel(q_ref, c_ref, o_ref, perm):
     @pl.when(pl.program_id(0) == 0)
     def _():
@@ -87,12 +90,10 @@
     o_ref[...] = to_slabs(perm[...], times(q_ref[...], c_ref[...])).reshape(o_ref.shape)
 
 
-def first_kernel(w_ref, k_ref, v_ref, o_ref, perm, blocks):
-    @pl.when(pl.program_id(0) == 0)
-    def _():
-        perm[...] = one_hot(256, slab_order)
-        for s in range(8):
-            blocks[:, s * 16 : s * 16 + 16, :] = w_ref[s, 0:4]
+def first_kernel(blocks, k_ref, v_ref, o_ref, perm):
+    @pl.when(pl.program_id(0) == 0)
+    def _():
+        perm[...] = one_hot(256, slab_order)
 
     product = times(k_ref[...], v_ref[...])
     first = jnp.concatenate(
@@ -101,7 +102,17 @@
     o_ref[...] = to_slabs(perm[...], first).reshape(o_ref.shape)
 
 
-def factor_kernel(w_ref, idx_ref, m_ref, mt_ref, p_ref, diag):
+def factor_kernel(place_ref, w0_ref, w1_ref, w2_ref, w3_ref, mate_ref, idx_ref, b_ref, m_ref, mt_ref, p_ref, diag, mixes):
+    place = place_ref[0]
+    core = lax.rem(place, 2)
+    for r, w_ref in enumerate((w0_ref, w1_ref, w2_ref, w3_ref)):
+        z = lax.rem(lax.div(place, 2) + 4 - r, 4)
+        own = pl.ds(pl.multiple_of(z * 32 + core * 16, 16), 16)
+        mate = pl.ds(pl.multiple_of(z * 32 + 16 - core * 16, 16), 16)
+        b_ref[:, own, :] = w_ref[0:4]
+        b_ref[:, mate, :] = mate_ref[r, 0:4]
+        mixes[:, own, :] = w_ref[4:8]
+        mixes[:, mate, :] = mate_ref[r, 4:8]
     columns = lax.broadcasted_iota(jnp.int32, (128, 128), 1)
     hits = jnp.zeros((128, 128), F32)
     for n in range(idx_ref.shape[1]):
@@ -109,8 +120,7 @@
     p_ref[...] = hits
     diag[...] = jnp.zeros_like(diag)
     for j in range(4):
-        mix = jnp.concatenate([w_ref[s, 4 + j] for s in range(8)], axis=0).astype(F32)
-        diag[j * 128 : j * 128 + 128, j * 128 : j * 128 + 128] = (mix * hits).astype(BF16)
+        diag[j * 128 : j * 128 + 128, j * 128 : j * 128 + 128] = (mixes[j].astype(F32) * hits).astype(BF16)
     spread = one_hot(512, lambda r: (r & 3) * 128 + (r >> 2))
     rows = dot(spread, diag[...]).astype(BF16)
     m_ref[...] = dot(rows, spread, cb=1).astype(BF16)
@@ -128,25 +138,18 @@
     o_ref[...] = dot(m_ref[...], x).astype(BF16).reshape(o_ref.shape)
 
 
-def grads_kernel(core_ref, w_ref, pat_ref, gm_ref, f_ref, gf_ref, k_ref, v_ref, gk_ref, gv_ref, send_ref, keep_ref,
-                 perm, sort, blocks, acc):
+def sums_kernel(core_ref, pat_ref, gm_ref, f_ref, gf_ref, k_ref, v_ref, send_ref, keep_ref, perm, sort, acc):
     @pl.when(pl.program_id(0) == 0)
     def _():
         perm[...] = one_hot(256, slab_order)
         sort[...] = one_hot(256, offset_order)
-        for s in range(8):
-            blocks[:, s * 16 : s * 16 + 16, :] = w_ref[s, 0:4]
         acc[...] = jnp.zeros_like(acc)
 
     width = k_ref.shape[1]
     grad_first = from_slabs(perm[...], gf_ref[...].reshape(512, width))
+    product = times(k_ref[...], v_ref[...])
     for k in range(4):
-        rows = slice(k * 128, k * 128 + 128)
-        key, value = k_ref[rows, :].astype(F32), v_ref[rows, :].astype(F32)
-        acc[k] += dot(grad_first[k], (key * value).astype(BF16), cb=1)
-        grad = dot(blocks[k], grad_first[k], ca=0)
-        gk_ref[rows, :] = (grad * value).astype(BF16)
-        gv_ref[rows, :] = (grad * key).astype(BF16)
+        acc[k] += dot(grad_first[k], product[k * 128 : k * 128 + 128], cb=1)
     left = by_offset(sort[...], gm_ref[...].reshape(512, width))
     right = by_offset(sort[...], f_ref[...].reshape(512, width))
     for j in range(4):
@@ -160,6 +163,19 @@
         for z in range(4):
             keep_ref[z] = acc[:, pl.ds(pl.multiple_of(z * 32 + core * 16, 16), 16), :]
             send_ref[z] = acc[:, pl.ds(pl.multiple_of(z * 32 + 16 - core * 16, 16), 16), :]
+
+
+def grads_kernel(blocks, gf_ref, k_ref, v_ref, gk_ref, gv_ref, perm):
+    @pl.when(pl.program_id(0) == 0)
+    def _():
+        perm[...] = one_hot(256, slab_order)
+
+    grad_first = from_slabs(perm[...], gf_ref[...].reshape(512, k_ref.shape[1]))
+    for k in range(4):
+        rows = slice(k * 128, k * 128 + 128)
+        grad = dot(blocks[k], grad_first[k], ca=0)
+        gk_ref[rows, :] = (grad * v_ref[rows, :].astype(F32)).astype(BF16)
+        gv_ref[rows, :] = (grad * k_ref[rows, :].astype(F32)).astype(BF16)
 
 
 def pair_kernel(z_ref, keep_ref, got_ref, own_ref, *out_refs):
@@ -191,8 +207,8 @@
     rows, slab = rows_spec(width), slab_spec(width)
     smem = pl.BlockSpec(memory_space=pltpu.SMEM)
     row_shape = jax.ShapeDtypeStruct((512, channels), BF16)
-    slab_shape = jax.ShapeDtypeStruct((32, 16, channels), BF16)
-    pair_shape = jax.ShapeDtypeStruct((32, 32, channels), BF16)
+    slab_shape = pltpu.HBM((32, 16, channels), BF16)
+    pair_shape = pltpu.HBM((32, 32, channels), BF16)
     perm = pltpu.VMEM((256, 256), BF16)
     size = 512 * channels * 2
     work = 2 * 512 * 512 * channels
@@ -200,42 +216,59 @@
     def exchange(x):
         return lax.all_to_all(x, "seq", split_axis=0, concat_axis=0, tiled=True)
 
-    place = lax.axis_index("dp")
-    core = (place % 2).reshape(1)
-    z = (place // 2).reshape(1)
-
-    gated = call(gate_kernel, "gate", grid, [rows, rows], slab, slab_shape, [perm], work // 2, 3 * size)(q, cot)
-    grad_cols = exchange(gated)
-
-    weights = lax.all_gather(jnp.concatenate([block_weights, mix_weights], axis=0), "dp", axis=0)
-    weights_spec = whole(8, 8, 16, 128)
+    place = lax.axis_index("dp").astype(jnp.int32).reshape(1)
+    core, z = place & 1, place >> 1
+
+    def pinned(x):
+        return pltpu.with_memory_space_constraint(x, pltpu.HBM)
+
+    def held(x):
+        return pltpu.with_memory_space_constraint(x, pltpu.VMEM)
+
+    def hop(r):
+        return [(i, ((i // 2 + r) % 4) * 2 + i % 2) for i in range(8)]
+
+    mate = [(i, i ^ 1) for i in range(8)]
+    gated = call(gate_kernel, "gate", grid, [rows, rows], slab, slab_shape, [perm], work // 2, 3 * size)(
+        pinned(q), pinned(cot)
+    )
+    own_rows = jnp.concatenate([block_weights, mix_weights], axis=0)
+    gated, own_rows = lax.optimization_barrier((gated, own_rows))
+    grad_cols = pinned(exchange(gated))
+
+    column = [own_rows] + [lax.ppermute(own_rows, "dp", hop(r)) for r in (1, 2, 3)]
+    other = lax.ppermute(jnp.stack(column), "dp", mate)
+    shard_spec = whole(8, 16, 128)
+    blocks, factor, factor_t, pattern = call(
+        factor_kernel, "factor", (), [smem] + [shard_spec] * 4 + [whole(4, 8, 16, 128), whole(128, 16)],
+        [VMEM_SPEC] * 4,
+        [pltpu.VMEM((4, 128, 128), BF16), pltpu.VMEM((512, 512), BF16), pltpu.VMEM((512, 512), BF16),
+         pltpu.VMEM((128, 128), F32)],
+        [pltpu.VMEM((512, 512), BF16), pltpu.VMEM((4, 128, 128), BF16)], work, size,
+    )(place, *column, other, block_index)
+    out = call(first_kernel, "first", grid, [VMEM_SPEC, rows, rows], slab, pair_shape, [perm], work, 3 * size)(
+        held(blocks), pinned(k), pinned(v)
+    )
     out = call(
-        first_kernel, "first", grid, [weights_spec, rows, rows], slab, pair_shape,
-        [perm, pltpu.VMEM((4, 128, 128), BF16)], work, 3 * size,
-    )(weights, k, v)
-    factor, factor_t, pattern = call(
-        factor_kernel, "factor", (), [weights_spec, whole(128, 16)],
-        [whole(512, 512), whole(512, 512), whole(128, 128)],
-        [jax.ShapeDtypeStruct((512, 512), BF16), jax.ShapeDtypeStruct((512, 512), BF16), jax.ShapeDtypeStruct((128, 128), F32)],
-        [pltpu.VMEM((512, 512), BF16)], work, size,
-    )(weights, block_index)
-    square = whole(512, 512)
-    out = call(
-        back_kernel, "back", grid, [square, slab, pl.BlockSpec(memory_space=pl.ANY)],
+        back_kernel, "back", grid, [VMEM_SPEC, slab, pl.BlockSpec(memory_space=pl.ANY)],
         slab_spec(width, 1), pair_shape, (), work, 2 * size, {2: 0},
-    )(factor_t, grad_cols, out)
+    )(held(factor_t), grad_cols, out)
     got = exchange(out)
-    mixed_cols = call(mix_kernel, "mix", grid, [square, slab], slab, slab_shape, (), work, 2 * size)(factor, got)
+    mixed_cols = call(mix_kernel, "mix", grid, [VMEM_SPEC, slab], slab, slab_shape, (), work, 2 * size)(held(factor), got)
     returned = exchange(mixed_cols)
 
     part = jax.ShapeDtypeStruct((4, 8, 16, 128), F32)
-    grad_key, grad_value, send, keep = call(
-        grads_kernel, "grads", grid,
-        [smem, weights_spec, whole(128, 128), slab, slab, slab_spec(width, 1), rows, rows],
-        [rows, rows, whole(4, 8, 16, 128), whole(4, 8, 16, 128)], [row_shape, row_shape, part, part],
-        [perm, perm, pltpu.VMEM((4, 128, 128), BF16), pltpu.VMEM((8, 128, 128), F32)], 4 * work, 7 * size,
-    )(core, weights, pattern, grad_cols, got, got, k, v)
-    swapped = lax.ppermute(send, "dp", [(i, i ^ 1) for i in range(8)])
+    send, keep = call(
+        sums_kernel, "sums", grid,
+        [smem, VMEM_SPEC, slab, slab, slab_spec(width, 1), rows, rows],
+        [whole(4, 8, 16, 128), whole(4, 8, 16, 128)], [part, part],
+        [perm, perm, pltpu.VMEM((8, 128, 128), F32)], 3 * work, 5 * size,
+    )(core, held(pattern), grad_cols, got, got, pinned(k), pinned(v))
+    grad_key, grad_value = call(
+        grads_kernel, "grads", grid, [VMEM_SPEC, slab_spec(width, 1), rows, rows], [rows, rows],
+        [row_shape, row_shape], [perm], work, 5 * size,
+    )(held(blocks), got, pinned(k), pinned(v))
+    swapped = lax.ppermute(send, "dp", mate)
     shard = jax.ShapeDtypeStruct((8, 16, 128), BF16)
     own, *others = call(
         pair_kernel, "pair", (), [smem, whole(4, 8, 16, 128), whole(4, 8, 16, 128)], [whole(8, 16, 128)] * 4,
@@ -243,12 +276,11 @@
     )(z, keep, swapped)
     total = own
     for r, other in enumerate(others, start=1):
-        hop = [(i, ((i // 2 + r) % 4) * 2 + i % 2) for i in range(8)]
-        total = total + lax.ppermute(other, "dp", hop).astype(F32)
+        total = total + lax.ppermute(other, "dp", hop(r)).astype(F32)
 
     output, grad_query = call(
         tail_kernel, "tail", grid, [slab, rows, rows], [rows, rows], [row_shape, row_shape], [perm], work // 2, 5 * size
-    )(returned, q, cot)
+    )(returned, pinned(q), pinned(cot))
     wide = query.shape
     return (
         output.reshape(wide), grad_query.reshape(wide), grad_key.reshape(wide), grad_value.reshape(wide),

time: 147 us -> 143 us (0.973)
  blocking collectives: 77.5 us -> 46.8 us
  Pallas kernels: 25.3 us -> 41.4 us
  waiting for transfers between devices: 4.57 us -> 19 us
  local copies, waits for them, and re-layouts: 15.8 us -> 2.68 us
  starting transfers between devices: 22.1 us -> 31.4 us
    all_gather x1 -> x0, blocking collectives: 31.2 us -> none  [on_device(): lax.all_gather(jnp.concatenate([block_weights, mix_weights], axis=0), 'dp...]
    ppermute x4 -> x8, waiting for transfers between devices: 4.56 us -> 18.1 us  [the longest x3 15.4 us: on_device(): lax.ppermute(own_rows, 'dp', hop(r))]
    unnamed x41 -> x13, local copies, waits for them, and re-layouts: 15.2 us -> 2.05 us
    pallas_call x5 -> x6, Pallas kernels: 18 us -> 29.5 us  [the longest x1 6.56 us: on_device(): call(sums_kernel, 'sums', grid, [smem, VMEM_SPEC, slab, slab, slab_spec(w...]
    ppermute x4 -> x8, starting transfers between devices: 7.77 us -> 17.1 us  [the longest x3 10.5 us: on_device(): lax.ppermute(own_rows, 'dp', hop(r))]
    pallas_call x1, Pallas kernels: 3.86 us -> 6.31 us  [on_device(): call(tail_kernel, 'tail', grid, [slab, rows, rows], [rows, rows], [row_sh...]
    pallas_call x1, Pallas kernels: 3.4 us -> 5.54 us  [on_device(): call(gate_kernel, 'gate', grid, [rows, rows], slab, slab_shape, [perm], w...]
  transfers between devices with their start and end apart: 6 -> 10, of which waited for: 2 -> 5; matrix products, arithmetic and copies ran while one was open for 1% -> 1% of each run, Pallas kernels for 10% -> 15%
where the time goes in v2:
time: 143 us; the launch traced here: 142 us
  blocking collectives  46.8 us (33%)
  Pallas kernels  41.4 us (29%)
  starting transfers between devices  31.4 us (22%)
  waiting for transfers between devices  19 us (13%)
  local copies, waits for them, and re-layouts  2.68 us (2%)
    all_to_all x1, blocking collectives, exchange(): return lax.all_to_all(x, 'seq', split_axis=0, concat_axis=0, tiled=True)  46.8 us
    ppermute x3, waiting for transfers between devices, on_device(): lax.ppermute(own_rows, 'dp', hop(r))  15.4 us
    all_to_all x2, starting transfers between devices, exchange(): return lax.all_to_all(x, 'seq', split_axis=0, concat_axis=0, tiled=True)  14.3 us
    ppermute x3, starting transfers between devices, on_device(): lax.ppermute(own_rows, 'dp', hop(r))  10.5 us
    pallas_call x1, Pallas kernels, on_device(): call(sums_kernel, 'sums', grid, [smem, VMEM_SPEC, slab, slab, slab_spec(w...  6.56 us
    ppermute x3, starting transfers between devices, on_device(): total = total + lax.ppermute(other, 'dp', hop(r)).astype(F32)  6.38 us
    pallas_call x1, Pallas kernels, on_device(): call(tail_kernel, 'tail', grid, [slab, rows, rows], [rows, rows], [row_sh...  6.31 us
    pallas_call x1, Pallas kernels, on_device(): call(grads_kernel, 'grads', grid, [VMEM_SPEC, slab_spec(width, 1), rows,...  6.31 us
  transfers between devices with their start and end apart: 10, of which 5 were waited for; matrix products, arithmetic and copies ran while one was open for 1% of the time, Pallas kernels for 15%

profile of v2, /device:TPU:8, one launch (start us, length us, event | category | flops | bytes accessed | tf_op | source)
XLA Modules:
  0.0 142.1 jit_solution(14915400195145723917)
XLA Ops:
  0.7 5.5 %gate.1 = bf16[32,16,1536]{2,1,0:T(8,128)(2,1)} custom-call(bf16[512,1536]{1,0:T(8,128)(2,1)} %bitcast.23, bf16[512,1536]{1,0:T(8,128)(2,1)} %bitcast.25), custom_call_target="tpu_custom_call" | custom-call | flops 402653184 | bytes 4718592 | tf_op jit(solution)/shard_map/gate/pallas_call | solution.py:232
  6.2 0.0 copy-start.5
  6.2 8.9 %all-to-all-start = ((bf16[32,16,1536]{2,1,0:T(8,128)(2,1)}), bf16[32,16,1536]{2,1,0:T(8,128)(2,1)S(1)}, u32[]{:S(2)}, u32[]{:S(2)}) async-start(bf16[32,16,1536]{2,1,0:T(8,128)(2,1)} %gate.1), calls=%async_computation | async-start | bytes 3145728 | tf_op jit(solution)/shard_map/all_to_all | solution.py:217
  15.1 3.4 %collective-permute-start = (bf16[8,16,128]{2,1,0:T(8,128)(2,1)S(1)}, bf16[8,16,128]{2,1,0:T(8,128)(2,1)S(1)}, u32[]{:S(2)}, u32[]{:S(2)}) collective-permute-start(bf16[8,16,128]{2,1,0:T(8,128)(2,1)S(1)} %pad_maximum_fusion.1.w0_ref), channel_id=1, source_target_pairs={{0,64},{32,96},{64,128},{96,160},{128,192},{160,224},{192,0},{224,... | collective-permute-start | bytes 98312 | tf_op jit(solution)/shard_map/ppermute | solution.py:239
  18.5 4.5 %collective-permute-start.1 = (bf16[8,16,128]{2,1,0:T(8,128)(2,1)S(1)}, bf16[8,16,128]{2,1,0:T(8,128)(2,1)S(1)}, u32[]{:S(2)}, u32[]{:S(2)}) collective-permute-start(bf16[8,16,128]{2,1,0:T(8,128)(2,1)S(1)} %pad_maximum_fusion.1.w0_ref), channel_id=1, source_target_pairs={{0,128},{32,160},{64,192},{96,224},{128,0},{160,32},{192,64},{224,... | collective-permute-start | bytes 98312 | tf_op jit(solution)/shard_map/ppermute | solution.py:239
  23.0 2.7 %collective-permute-start.2 = (bf16[8,16,128]{2,1,0:T(8,128)(2,1)S(1)}, bf16[8,16,128]{2,1,0:T(8,128)(2,1)S(1)}, u32[]{:S(2)}, u32[]{:S(2)}) collective-permute-start(bf16[8,16,128]{2,1,0:T(8,128)(2,1)S(1)} %pad_maximum_fusion.1.w0_ref), channel_id=1, source_target_pairs={{0,192},{32,224},{64,0},{96,32},{128,64},{160,96},{192,128},{224,1... | collective-permute-start | bytes 98312 | tf_op jit(solution)/shard_map/ppermute | solution.py:239
  25.6 14.1 %collective-permute-done.w1_ref = bf16[8,16,128]{2,1,0:T(8,128)(2,1)S(1)} collective-permute-done((bf16[8,16,128]{2,1,0:T(8,128)(2,1)S(1)}, bf16[8,16,128]{2,1,0:T(8,128)(2,1)S(1)}, u32[]{:S(2)}, u32[]{:S(2)}) %collective-permute-start) | collective-permute-done | bytes 32800 | tf_op jit(solution)/shard_map/ppermute | solution.py:239
  39.8 1.3 collective-permute-done.1.w2_ref
  41.0 0.0 collective-permute-done.2.w3_ref
  41.1 0.1 collective-permute-start.3
  41.2 0.1 copy.14.idx_ref
  41.3 1.2 collective-permute-done.3.mate_ref
  42.5 1.8 %factor.1 = (bf16[4,128,128]{2,1,0:T(8,128)(2,1)S(1)}, bf16[512,512]{1,0:T(8,128)(2,1)S(1)}, bf16[512,512]{1,0:T(8,128)(2,1)S(1)}, f32[128,128]{1,0:T(8,128)S(1)}) custom-call(s32[1]{0:T(128)} %bitcast.place_ref, bf16[8,16,128]{2,1,0:T(8,128)(2,1)S(1)} %pad_maximum_fusion.1.w0_ref, bf16[8,16,128]{2,1,0:T(8,128)(2,1)S(1)} %collective-permute-done.w1_ref, ...), custom_call_target="tpu_custom_call" | custom-call | flops 805306368 | bytes 1572864 | tf_op jit(solution)/shard_map/factor/pallas_call | solution.py:242
  44.3 0.0 copy-start
  44.3 0.8 copy-done
  45.1 6.0 %first.1._ = bf16[32,32,1536]{2,1,0:T(8,128)(2,1)} custom-call(bf16[4,128,128]{2,1,0:T(8,128)(2,1)S(1)} %get-tuple-element.26.blocks, bf16[512,1536]{1,0:T(8,128)(2,1)} %bitcast.17, bf16[512,1536]{1,0:T(8,128)(2,1)} %bitcast.20), custom_call_target="tpu_custom_call" | custom-call | flops 805306368 | bytes 4718592 | tf_op jit(solution)/shard_map/first/pallas_call | solution.py:249
  51.1 1.1 copy-done.2
  52.2 5.4 %back.1 = bf16[32,32,1536]{2,1,0:T(8,128)(2,1)} custom-call(bf16[512,512]{1,0:T(8,128)(2,1)S(1)} %get-tuple-element.24.m_ref, bf16[32,16,1536]{2,1,0:T(8,128)(2,1)} %copy-done.2, bf16[32,32,1536]{2,1,0:T(8,128)(2,1)} %first.1._), custom_call_target="tpu_custom_call", output_to_operand_aliasing={{}: (2, {})} | custom-call | flops 805306368 | bytes 3145728 | tf_op jit(solution)/shard_map/back/pallas_call | solution.py:252
  57.7 46.8 %all_to_all.15.x_ref.gf_ref.f_ref = bf16[32,32,1536]{2,1,0:T(8,128)(2,1)S(1)} all-to-all(bf16[32,32,1536]{2,1,0:T(8,128)(2,1)} %back.1), channel_id=1, replica_groups=mesh['dp'=8,'seq'=32] {'seq'}, dimensions={0} | all-to-all | bytes 6291456 | tf_op jit(solution)/shard_map/all_to_all | solution.py:217
  104.5 3.4 %mix.1 = bf16[32,16,1536]{2,1,0:T(8,128)(2,1)} custom-call(bf16[512,512]{1,0:T(8,128)(2,1)S(1)} %copy-done.1, bf16[32,32,1536]{2,1,0:T(8,128)(2,1)S(1)} %all_to_all.15.x_ref.gf_ref.f_ref), custom_call_target="tpu_custom_call" | custom-call | flops 805306368 | bytes 3145728 | tf_op jit(solution)/shard_map/mix/pallas_call | solution.py:257
  107.9 5.4 %all-to-all-start.2 = ((bf16[32,16,1536]{2,1,0:T(8,128)(2,1)}), bf16[32,16,1536]{2,1,0:T(8,128)(2,1)}, u32[]{:S(2)}, u32[]{:S(2)}) async-start(bf16[32,16,1536]{2,1,0:T(8,128)(2,1)} %mix.1), calls=%async_computation.2 | async-start | bytes 3145728 | tf_op jit(solution)/shard_map/all_to_all | solution.py:217
  113.3 6.6 %sums.1 = (f32[4,8,16,128]{3,2,1,0:T(8,128)S(1)}, f32[4,8,16,128]{3,2,1,0:T(8,128)S(1)}) custom-call(s32[1]{0:T(128)S(6)} %and.4.core_ref, f32[128,128]{1,0:T(8,128)S(1)} %get-tuple-element.31.pat_ref, bf16[32,16,1536]{2,1,0:T(8,128)(2,1)} %copy-done.2, bf16[32,32,1536]{2,1,0:T(8,128)(2,1)S(1)} %all_to_all.15.x_ref.gf_ref.f_ref, ...), custom_call_target="tpu_custom_call" | custom-call | flops 2415919104 | bytes 7864320 | tf_op jit(solution)/shard_map/sums/pallas_call | solution.py:261
  119.9 0.1 collective-permute-start.4
  120.0 1.5 %collective-permute-done.4.got_ref = f32[4,8,16,128]{3,2,1,0:T(8,128)S(1)} collective-permute-done((f32[4,8,16,128]{3,2,1,0:T(8,128)S(1)}, f32[4,8,16,128]{3,2,1,0:T(8,128)S(1)}, u32[]{:S(2)}, u32[]{:S(2)}) %collective-permute-start.4) | collective-permute-done | bytes 262176 | tf_op jit(solution)/shard_map/ppermute | solution.py:271
  121.5 1.9 %collective-permute-start.5 = (bf16[8,16,128]{2,1,0:T(8,128)(2,1)S(1)}, bf16[8,16,128]{2,1,0:T(8,128)(2,1)S(1)}, u32[]{:S(2)}, u32[]{:S(2)}) collective-permute-start(bf16[8,16,128]{2,1,0:T(8,128)(2,1)S(1)} %get-tuple-element.35), channel_id=1, source_target_pairs={{0,64},{32,96},{64,128},{96,160},{128,192},{160,224},{192,0},{224,... | collective-permute-start | bytes 98312 | tf_op jit(solution)/shard_map/ppermute | solution.py:279
  123.4 0.9 collective-permute-start.6
  124.3 3.6 %collective-permute-start.7 = (bf16[8,16,128]{2,1,0:T(8,128)(2,1)S(1)}, bf16[8,16,128]{2,1,0:T(8,128)(2,1)S(1)}, u32[]{:S(2)}, u32[]{:S(2)}) collective-permute-start(bf16[8,16,128]{2,1,0:T(8,128)(2,1)S(1)} %get-tuple-element.37), channel_id=1, source_target_pairs={{0,192},{32,224},{64,0},{96,32},{128,64},{160,96},{192,128},{224,1... | collective-permute-start | bytes 98312 | tf_op jit(solution)/shard_map/ppermute | solution.py:279
  127.9 6.3 %grads.1 = (bf16[512,1536]{1,0:T(8,128)(2,1)}, bf16[512,1536]{1,0:T(8,128)(2,1)}) custom-call(bf16[4,128,128]{2,1,0:T(8,128)(2,1)S(1)} %get-tuple-element.26.blocks, bf16[32,32,1536]{2,1,0:T(8,128)(2,1)S(1)} %all_to_all.15.x_ref.gf_ref.f_ref, bf16[512,1536]{1,0:T(8,128)(2,1)} %bitcast.19, bf16[512,1536]{1,0:T(8,128)(2,1)} %bitcast.22), custom_call_target="tpu_custom_call" | custom-call | flops 805306368 | bytes 7864320 | tf_op jit(solution)/shard_map/grads/pallas_call | solution.py:267
  134.2 0.0 collective-permute-done.6
  134.3 0.6 fusion
  134.9 0.9 all-to-all-done.2.x_ref
  135.8 6.3 %tail.1 = (bf16[512,1536]{1,0:T(8,128)(2,1)}, bf16[512,1536]{1,0:T(8,128)(2,1)}) custom-call(bf16[32,16,1536]{2,1,0:T(8,128)(2,1)} %all-to-all-done.2.x_ref, bf16[512,1536]{1,0:T(8,128)(2,1)} %bitcast.24, bf16[512,1536]{1,0:T(8,128)(2,1)} %bitcast.26), custom_call_target="tpu_custom_call" | custom-call | flops 402653184 | bytes 7864320 | tf_op jit(solution)/shard_map/tail/pallas_call | solution.py:281
  (15 shorter events, 0.1 us)
Async XLA Ops:
  0.6 5.6 %copy-start.3 = (bf16[4,16,128]{2,1,0:T(8,128)(2,1)S(1)}, bf16[4,16,128]{2,1,0:T(8,128)(2,1)}, u32[]{:S(2)}) copy-start(bf16[4,16,128]{2,1,0:T(8,128)(2,1)} %param.11) | copy-start | bytes 49156
  0.6 5.6 %copy-start.4 = (bf16[4,16,128]{2,1,0:T(8,128)(2,1)S(1)}, bf16[4,16,128]{2,1,0:T(8,128)(2,1)}, u32[]{:S(2)}) copy-start(bf16[4,16,128]{2,1,0:T(8,128)(2,1)} %param.10) | copy-start | bytes 49156
  6.2 35.0 %copy-start.5 = (s32[128,16]{0,1:T(8,128)S(1)}, s32[128,16]{0,1:T(8,128)}, u32[]{:S(2)}) copy-start(s32[128,16]{0,1:T(8,128)} %param.12) | copy-start | bytes 24580
  6.2 44.9 %all-to-all-start = ((bf16[32,16,1536]{2,1,0:T(8,128)(2,1)}), bf16[32,16,1536]{2,1,0:T(8,128)(2,1)S(1)}, u32[]{:S(2)}, u32[]{:S(2)}) async-start(bf16[32,16,1536]{2,1,0:T(8,128)(2,1)} %gate.1), calls=%async_computation | async-start | bytes 3145728 | tf_op jit(solution)/shard_map/all_to_all | solution.py:217
  15.1 24.6 %collective-permute-start = (bf16[8,16,128]{2,1,0:T(8,128)(2,1)S(1)}, bf16[8,16,128]{2,1,0:T(8,128)(2,1)S(1)}, u32[]{:S(2)}, u32[]{:S(2)}) collective-permute-start(bf16[8,16,128]{2,1,0:T(8,128)(2,1)S(1)} %pad_maximum_fusion.1.w0_ref), channel_id=1, source_target_pairs={{0,64},{32,96},{64,128},{96,160},{128,192},{160,224},{192,0},{224,... | collective-permute-start | bytes 98312 | tf_op jit(solution)/shard_map/ppermute | solution.py:239
  18.5 22.6 %collective-permute-start.1 = (bf16[8,16,128]{2,1,0:T(8,128)(2,1)S(1)}, bf16[8,16,128]{2,1,0:T(8,128)(2,1)S(1)}, u32[]{:S(2)}, u32[]{:S(2)}) collective-permute-start(bf16[8,16,128]{2,1,0:T(8,128)(2,1)S(1)} %pad_maximum_fusion.1.w0_ref), channel_id=1, source_target_pairs={{0,128},{32,160},{64,192},{96,224},{128,0},{160,32},{192,64},{224,... | collective-permute-start | bytes 98312 | tf_op jit(solution)/shard_map/ppermute | solution.py:239
  23.0 18.1 %collective-permute-start.2 = (bf16[8,16,128]{2,1,0:T(8,128)(2,1)S(1)}, bf16[8,16,128]{2,1,0:T(8,128)(2,1)S(1)}, u32[]{:S(2)}, u32[]{:S(2)}) collective-permute-start(bf16[8,16,128]{2,1,0:T(8,128)(2,1)S(1)} %pad_maximum_fusion.1.w0_ref), channel_id=1, source_target_pairs={{0,192},{32,224},{64,0},{96,32},{128,64},{160,96},{192,128},{224,1... | collective-permute-start | bytes 98312 | tf_op jit(solution)/shard_map/ppermute | solution.py:239
  41.1 1.4 %collective-permute-start.3 = (bf16[4,8,16,128]{3,2,1,0:T(8,128)(2,1)S(1)}, bf16[4,8,16,128]{3,2,1,0:T(8,128)(2,1)S(1)}, u32[]{:S(2)}, u32[]{:S(2)}) collective-permute-start(bf16[4,8,16,128]{3,2,1,0:T(8,128)(2,1)S(1)} %pad_maximum_fusion), channel_id=1, source_target_pairs={{0,32},{32,0},{64,96},{96,64},{128,160},{160,128},{192,224},{224,1... | collective-permute-start | bytes 393224 | tf_op jit(solution)/shard_map/ppermute | solution.py:240
  44.3 0.8 copy-start
  51.1 1.1 copy-start.2
  57.7 46.8 %copy-start.1 = (bf16[512,512]{1,0:T(8,128)(2,1)S(1)}, bf16[512,512]{1,0:T(8,128)(2,1)}, u32[]{:S(2)}) copy-start(bf16[512,512]{1,0:T(8,128)(2,1)} %copy-done) | copy-start | bytes 1572868
  107.9 27.9 %all-to-all-start.2 = ((bf16[32,16,1536]{2,1,0:T(8,128)(2,1)}), bf16[32,16,1536]{2,1,0:T(8,128)(2,1)}, u32[]{:S(2)}, u32[]{:S(2)}) async-start(bf16[32,16,1536]{2,1,0:T(8,128)(2,1)} %mix.1), calls=%async_computation.2 | async-start | bytes 3145728 | tf_op jit(solution)/shard_map/all_to_all | solution.py:217
  119.9 1.6 %collective-permute-start.4 = (f32[4,8,16,128]{3,2,1,0:T(8,128)S(1)}, f32[4,8,16,128]{3,2,1,0:T(8,128)S(1)}, u32[]{:S(2)}, u32[]{:S(2)}) collective-permute-start(f32[4,8,16,128]{3,2,1,0:T(8,128)S(1)} %get-tuple-element.33), channel_id=1, source_target_pairs={{0,32},{32,0},{64,96},{96,64},{128,160},{160,128},{192,224},{224,1... | collective-permute-start | bytes 786440 | tf_op jit(solution)/shard_map/ppermute | solution.py:271
  121.5 12.7 %collective-permute-start.5 = (bf16[8,16,128]{2,1,0:T(8,128)(2,1)S(1)}, bf16[8,16,128]{2,1,0:T(8,128)(2,1)S(1)}, u32[]{:S(2)}, u32[]{:S(2)}) collective-permute-start(bf16[8,16,128]{2,1,0:T(8,128)(2,1)S(1)} %get-tuple-element.35), channel_id=1, source_target_pairs={{0,64},{32,96},{64,128},{96,160},{128,192},{160,224},{192,0},{224,... | collective-permute-start | bytes 98312 | tf_op jit(solution)/shard_map/ppermute | solution.py:279
  123.4 10.8 %collective-permute-start.6 = (bf16[8,16,128]{2,1,0:T(8,128)(2,1)S(1)}, bf16[8,16,128]{2,1,0:T(8,128)(2,1)S(1)}, u32[]{:S(2)}, u32[]{:S(2)}) collective-permute-start(bf16[8,16,128]{2,1,0:T(8,128)(2,1)S(1)} %get-tuple-element.36), channel_id=1, source_target_pairs={{0,128},{32,160},{64,192},{96,224},{128,0},{160,32},{192,64},{224,... | collective-permute-start | bytes 98312 | tf_op jit(solution)/shard_map/ppermute | solution.py:279
  124.3 9.9 %collective-permute-start.7 = (bf16[8,16,128]{2,1,0:T(8,128)(2,1)S(1)}, bf16[8,16,128]{2,1,0:T(8,128)(2,1)S(1)}, u32[]{:S(2)}, u32[]{:S(2)}) collective-permute-start(bf16[8,16,128]{2,1,0:T(8,128)(2,1)S(1)} %get-tuple-element.37), channel_id=1, source_target_pairs={{0,192},{32,224},{64,0},{96,32},{128,64},{160,96},{192,128},{224,1... | collective-permute-start | bytes 98312 | tf_op jit(solution)/shard_map/ppermute | solution.py:279

commit v3 on v2

--- a/solution.py
+++ b/solution.py
@@ -8,6 +8,7 @@
 BF16 = jnp.bfloat16
 F32 = jnp.float32
 MIB = 1024 * 1024
+STEP = 512
 
 
 def dot(a, b, ca=1, cb=0):
@@ -67,6 +68,75 @@
     )
 
 
+def chunk_of(ref, index, width, rows=0):
+    columns = pl.ds(index * width, width)
+    if len(ref.shape) == 2:
+        return ref.at[:, columns]
+    return ref.at[:, pl.ds(rows, 16), columns] if ref.shape[0] == 32 else ref.at[:, :, columns]
+
+
+def streamed(body, name, ins, out_shapes, width, consts=(), out_rows=0, extra=(), aliases=None, scratch=(), prepare=None,
+             flops=0, nbytes=0, vmem=16):
+    channels = ins[0].shape[-1]
+    count = channels // width
+    n_const, n_in, n_extra, n_out = len(consts), len(ins), len(extra), len(out_shapes)
+
+    def buffer(array):
+        shape = array.shape
+        return pltpu.VMEM((count, *((32, 16) if len(shape) == 3 and shape[0] == 32 else shape[:-1]), width), BF16)
+
+    def kernel(*refs):
+        const_refs, refs = refs[:n_const], refs[n_const:]
+        in_refs, refs = refs[:n_in], refs[n_in + n_extra :]
+        out_refs, refs = refs[:n_out], refs[n_out:]
+        bufs, refs = refs[:n_in], refs[n_in:]
+        outs, refs = refs[:n_out], refs[n_out:]
+        in_sem, out_sem, scratch_refs = refs[0], refs[1], refs[2:]
+        arriving, leaving = [], []
+        for c in range(count):
+            arriving.append([
+                pltpu.make_async_copy(chunk_of(in_refs[i], c, width), bufs[i].at[c], in_sem.at[i, c]) for i in range(n_in)
+            ])
+            for copy in arriving[c]:
+                copy.start()
+        if prepare is not None:
+            prepare(*scratch_refs)
+        for c in range(count):
+            for copy in arriving[c]:
+                copy.wait()
+            values = [buf[c].reshape(512, width) for buf in bufs]
+            for o, make in enumerate(body(const_refs, scratch_refs, *values)):
+                outs[o][c] = make().reshape(outs[o].shape[1:])
+                copy = pltpu.make_async_copy(outs[o].at[c], chunk_of(out_refs[o], c, width, out_rows), out_sem.at[o, c])
+                copy.start()
+                leaving.append(copy)
+        for copy in leaving:
+            copy.wait()
+
+    return pl.pallas_call(
+        kernel,
+        name=name,
+        in_specs=[VMEM_SPEC] * n_const + [pl.BlockSpec(memory_space=pl.ANY)] * (n_in + n_extra),
+        out_specs=[pl.BlockSpec(memory_space=pltpu.HBM)] * n_out,
+        out_shape=list(out_shapes),
+        scratch_shapes=[buffer(x) for x in ins]
+        + [buffer(x) for x in out_shapes]
+        + [pltpu.SemaphoreType.DMA((n_in, count)), pltpu.SemaphoreType.DMA((n_out, count))]
+        + list(scratch),
+        input_output_aliases=aliases or {},
+        cost_estimate=pl.CostEstimate(flops=flops, transcendentals=0, bytes_accessed=nbytes),
+        compiler_params=pltpu.CompilerParams(vmem_limit_bytes=vmem * MIB),
+    )(*[held(x) for x in consts], *ins, *extra)
+
+
+def pinned(x):
+    return pltpu.with_memory_space_constraint(x, pltpu.HBM)
+
+
+def held(x):
+    return pltpu.with_memory_space_constraint(x, pltpu.VMEM)
+
+
 def rows_spec(width):
     return pl.BlockSpec((512, width), lambda d: (0, d))
 
@@ -82,12 +152,32 @@
 VMEM_SPEC = pl.BlockSpec(memory_space=pltpu.VMEM)
 
 
-def gate_kernel(q_ref, c_ref, o_ref, perm):
-    @pl.when(pl.program_id(0) == 0)
-    def _():
-        perm[...] = one_hot(256, slab_order)
-
-    o_ref[...] = to_slabs(perm[...], times(q_ref[...], c_ref[...])).reshape(o_ref.shape)
+def make_slab_order(perm):
+    perm[...] = one_hot(256, slab_order)
+
+
+def make_offset_order(perm):
+    perm[...] = one_hot(256, offset_order)
+
+
+def gate_body(consts, scratch, q, cot):
+    return [lambda: to_slabs(scratch[0][...], times(q, cot))]
+
+
+def factor_body(consts, scratch, x):
+    return [lambda: dot(consts[0][...], x).astype(BF16)]
+
+
+def back_body(consts, scratch, x):
+    return [
+        lambda: dot(consts[0][...], x).astype(BF16),
+        lambda: jnp.concatenate(by_offset(scratch[0][...], x), axis=0),
+    ]
+
+
+def tail_body(consts, scratch, x, q, cot):
+    mixed = jnp.concatenate(from_slabs(scratch[0][...], x), axis=0)
+    return [lambda: times(q, mixed), lambda: times(cot, mixed)]
 
 
 def first_kernel(blocks, k_ref, v_ref, o_ref, perm):
@@ -128,16 +218,6 @@
     mt_ref[...] = dot(rows_t, spread, cb=1).astype(BF16)
 
 
-def back_kernel(m_ref, x_ref, _, o_ref):
-    x = x_ref[...].reshape(512, x_ref.shape[2])
-    o_ref[...] = dot(m_ref[...], x).astype(BF16).reshape(o_ref.shape)
-
-
-def mix_kernel(m_ref, x_ref, o_ref):
-    x = x_ref[...].reshape(512, x_ref.shape[2])
-    o_ref[...] = dot(m_ref[...], x).astype(BF16).reshape(o_ref.shape)
-
-
 def sums_kernel(core_ref, pat_ref, gm_ref, f_ref, gf_ref, k_ref, v_ref, send_ref, keep_ref, perm, sort, acc):
     @pl.when(pl.program_id(0) == 0)
     def _():
@@ -150,10 +230,9 @@
     product = times(k_ref[...], v_ref[...])
     for k in range(4):
         acc[k] += dot(grad_first[k], product[k * 128 : k * 128 + 128], cb=1)
-    left = by_offset(sort[...], gm_ref[...].reshape(512, width))
     right = by_offset(sort[...], f_ref[...].reshape(512, width))
     for j in range(4):
-        acc[4 + j] += dot(left[j], right[j], cb=1)
+        acc[4 + j] += dot(gm_ref[j], right[j], cb=1)
 
     @pl.when(pl.program_id(0) == pl.num_programs(0) - 1)
     def _():
@@ -186,19 +265,6 @@
         out[...] = (keep_ref[t] + got_ref[t]).astype(BF16)
 
 
-def tail_kernel(x_ref, q_ref, c_ref, o_ref, gq_ref, perm):
-    @pl.when(pl.program_id(0) == 0)
-    def _():
-        perm[...] = one_hot(256, slab_order)
-
-    mixed = from_slabs(perm[...], x_ref[...].reshape(512, x_ref.shape[2]))
-    for k in range(4):
-        rows = slice(k * 128, k * 128 + 128)
-        m = mixed[k].astype(F32)
-        o_ref[rows, :] = (q_ref[rows, :].astype(F32) * m).astype(BF16)
-        gq_ref[rows, :] = (c_ref[rows, :].astype(F32) * m).astype(BF16)
-
-
 def on_device(query, key, value, block_weights, mix_weights, block_index, cotangent):
     channels = query.shape[2]
     q, k, v, cot = (a.reshape(512, channels) for a in (query, key, value, cotangent))
@@ -207,6 +273,7 @@
     rows, slab = rows_spec(width), slab_spec(width)
     smem = pl.BlockSpec(memory_space=pltpu.SMEM)
     row_shape = jax.ShapeDtypeStruct((512, channels), BF16)
+    pinned_rows = pltpu.HBM((512, channels), BF16)
     slab_shape = pltpu.HBM((32, 16, channels), BF16)
     pair_shape = pltpu.HBM((32, 32, channels), BF16)
     perm = pltpu.VMEM((256, 256), BF16)
@@ -219,24 +286,18 @@
     place = lax.axis_index("dp").astype(jnp.int32).reshape(1)
     core, z = place & 1, place >> 1
 
-    def pinned(x):
-        return pltpu.with_memory_space_constraint(x, pltpu.HBM)
-
-    def held(x):
-        return pltpu.with_memory_space_constraint(x, pltpu.VMEM)
-
     def hop(r):
         return [(i, ((i // 2 + r) % 4) * 2 + i % 2) for i in range(8)]
 
     mate = [(i, i ^ 1) for i in range(8)]
-    gated = call(gate_kernel, "gate", grid, [rows, rows], slab, slab_shape, [perm], work // 2, 3 * size)(
-        pinned(q), pinned(cot)
-    )
     own_rows = jnp.concatenate([block_weights, mix_weights], axis=0)
-    gated, own_rows = lax.optimization_barrier((gated, own_rows))
-    grad_cols = pinned(exchange(gated))
-
     column = [own_rows] + [lax.ppermute(own_rows, "dp", hop(r)) for r in (1, 2, 3)]
+    (gated,) = streamed(
+        gate_body, "gate", [pinned(q), pinned(cot)], [slab_shape], STEP, scratch=[perm], prepare=make_slab_order,
+        flops=work // 2, nbytes=3 * size,
+    )
+    gated, *column = lax.optimization_barrier((gated, *column))
+    grad_cols = exchange(gated)
     other = lax.ppermute(jnp.stack(column), "dp", mate)
     shard_spec = whole(8, 16, 128)
     blocks, factor, factor_t, pattern = call(
@@ -249,21 +310,22 @@
     out = call(first_kernel, "first", grid, [VMEM_SPEC, rows, rows], slab, pair_shape, [perm], work, 3 * size)(
         held(blocks), pinned(k), pinned(v)
     )
-    out = call(
-        back_kernel, "back", grid, [VMEM_SPEC, slab, pl.BlockSpec(memory_space=pl.ANY)],
-        slab_spec(width, 1), pair_shape, (), work, 2 * size, {2: 0},
-    )(held(factor_t), grad_cols, out)
+    out, left = streamed(
+        back_body, "back", [grad_cols], [pair_shape, pltpu.HBM((4, 128, channels), BF16)], STEP, consts=[factor_t],
+        out_rows=16, extra=[out], aliases={2: 0}, scratch=[perm], prepare=make_offset_order,
+        flops=2 * work, nbytes=3 * size,
+    )
     got = exchange(out)
-    mixed_cols = call(mix_kernel, "mix", grid, [VMEM_SPEC, slab], slab, slab_shape, (), work, 2 * size)(held(factor), got)
+    (mixed_cols,) = streamed(factor_body, "mix", [got], [slab_shape], STEP, consts=[factor], flops=work, nbytes=2 * size)
     returned = exchange(mixed_cols)
 
     part = jax.ShapeDtypeStruct((4, 8, 16, 128), F32)
     send, keep = call(
         sums_kernel, "sums", grid,
-        [smem, VMEM_SPEC, slab, slab, slab_spec(width, 1), rows, rows],
+        [smem, VMEM_SPEC, pl.BlockSpec((4, 128, width), lambda d: (0, 0, d)), slab, slab_spec(width, 1), rows, rows],
         [whole(4, 8, 16, 128), whole(4, 8, 16, 128)], [part, part],
         [perm, perm, pltpu.VMEM((8, 128, 128), F32)], 3 * work, 5 * size,
-    )(core, held(pattern), grad_cols, got, got, pinned(k), pinned(v))
+    )(core, held(pattern), left, got, got, pinned(k), pinned(v))
     grad_key, grad_value = call(
         grads_kernel, "grads", grid, [VMEM_SPEC, slab_spec(width, 1), rows, rows], [rows, rows],
         [row_shape, row_shape], [perm], work, 5 * size,
@@ -278,9 +340,10 @@
     for r, other in enumerate(others, start=1):
         total = total + lax.ppermute(other, "dp", hop(r)).astype(F32)
 
-    output, grad_query = call(
-        tail_kernel, "tail", grid, [slab, rows, rows], [rows, rows], [row_shape, row_shape], [perm], work // 2, 5 * size
-    )(returned, pinned(q), pinned(cot))
+    output, grad_query = streamed(
+        tail_body, "tail", [returned, pinned(q), pinned(cot)], [pinned_rows, pinned_rows], STEP,
+        scratch=[perm], prepare=make_slab_order, flops=work // 2, nbytes=5 * size,
+    )
     wide = query.shape
     return (
         output.reshape(wide), grad_query.reshape(wide), grad_key.reshape(wide), grad_value.reshape(wide),

time: 143 us -> 125 us (0.87)
  Pallas kernels: 41.4 us -> 32.4 us
  waiting for transfers between devices: 19 us -> 13.3 us
  blocking collectives: 46.8 us -> 43.2 us
  starting transfers between devices: 31.4 us -> 29.6 us
  local copies, waits for them, and re-layouts: 2.68 us -> 4.38 us
    ppermute x3, waiting for transfers between devices: 15.4 us -> 0.01 us  [on_device(): lax.ppermute(own_rows, 'dp', hop(r))]
    all_to_all x2, waiting for transfers between devices: 0.87 us -> 10.5 us  [exchange(): return lax.all_to_all(x, 'seq', split_axis=0, concat_axis=0, tiled=True)]
    pallas_call x5, Pallas kernels: 27.2 us -> 18.2 us  [the longest x4 12 us: streamed(): pl.pallas_call(kernel, name=name, in_specs=[VMEM_SPEC] * n_const + [pl.Bl...]
    all_to_all x1, blocking collectives: 46.8 us -> 43.2 us  [exchange(): return lax.all_to_all(x, 'seq', split_axis=0, concat_axis=0, tiled=True)]
    ppermute x3, starting transfers between devices: 6.38 us -> 4.46 us  [on_device(): total = total + lax.ppermute(other, 'dp', hop(r)).astype(F32)]
    unnamed x13 -> x10, local copies, waits for them, and re-layouts: 2.05 us -> 3.02 us
  transfers between devices with their start and end apart: 10 -> 10, of which waited for: 5 -> 3; matrix products, arithmetic and copies ran while one was open for 1% -> 1% of each run, Pallas kernels for 15% -> 19%
where the time goes in v3:
time: 125 us; the launch traced here: 124 us
  blocking collectives  43.2 us (35%)
  Pallas kernels  32.4 us (26%)
  starting transfers between devices  29.6 us (24%)
  waiting for transfers between devices  13.3 us (11%)
  local copies, waits for them, and re-layouts  4.38 us (4%)
    all_to_all x1, blocking collectives, exchange(): return lax.all_to_all(x, 'seq', split_axis=0, concat_axis=0, tiled=True)  43.2 us
    all_to_all x2, starting transfers between devices, exchange(): return lax.all_to_all(x, 'seq', split_axis=0, concat_axis=0, tiled=True)  13.6 us
    pallas_call x4, Pallas kernels, streamed(): pl.pallas_call(kernel, name=name, in_specs=[VMEM_SPEC] * n_const + [pl.Bl...  12 us
    ppermute x3, starting transfers between devices, on_device(): lax.ppermute(own_rows, 'dp', hop(r))  11.3 us
    all_to_all x2, waiting for transfers between devices, exchange(): return lax.all_to_all(x, 'seq', split_axis=0, concat_axis=0, tiled=True)  10.5 us
    pallas_call x1, Pallas kernels, on_device(): call(grads_kernel, 'grads', grid, [VMEM_SPEC, slab_spec(width, 1), rows,...  6.33 us
    pallas_call x1, Pallas kernels, on_device(): call(sums_kernel, 'sums', grid, [smem, VMEM_SPEC, pl.BlockSpec((4, 128, w...  6.18 us
    pallas_call x1, Pallas kernels, on_device(): call(first_kernel, 'first', grid, [VMEM_SPEC, rows, rows], slab, pair_sha...  6.08 us
  transfers between devices with their start and end apart: 10, of which 3 were waited for; matrix products, arithmetic and copies ran while one was open for 1% of the time, Pallas kernels for 19%

profile of v3, /device:TPU:8, one launch (start us, length us, event | category | flops | bytes accessed | tf_op | source)
XLA Modules:
  0.0 123.7 jit_solution(368539534515606202)
XLA Ops:
  0.6 0.7 constant_dynamic-update-slice_fusion.1
  1.4 0.7 constant_dynamic-update-slice_fusion.w0_ref
  2.1 3.3 %collective-permute-start = (bf16[8,16,128]{2,1,0:T(8,128)(2,1)S(1)}, bf16[8,16,128]{2,1,0:T(8,128)(2,1)S(1)}, u32[]{:S(2)}, u32[]{:S(2)}) collective-permute-start(bf16[8,16,128]{2,1,0:T(8,128)(2,1)S(1)} %constant_dynamic-update-slice_fusion.w0_ref), channel_id=1, source_target_pairs={{0,64},{32,96},{64,128},{96,160},{128,192},{160,224},{192,0},{224,... | collective-permute-start | bytes 98312 | tf_op jit(solution)/shard_map/ppermute | solution.py:294
  5.3 5.4 %collective-permute-start.1 = (bf16[8,16,128]{2,1,0:T(8,128)(2,1)S(1)}, bf16[8,16,128]{2,1,0:T(8,128)(2,1)S(1)}, u32[]{:S(2)}, u32[]{:S(2)}) collective-permute-start(bf16[8,16,128]{2,1,0:T(8,128)(2,1)S(1)} %constant_dynamic-update-slice_fusion.w0_ref), channel_id=1, source_target_pairs={{0,128},{32,160},{64,192},{96,224},{128,0},{160,32},{192,64},{224,... | collective-permute-start | bytes 98312 | tf_op jit(solution)/shard_map/ppermute | solution.py:294
  10.7 2.7 %collective-permute-start.2 = (bf16[8,16,128]{2,1,0:T(8,128)(2,1)S(1)}, bf16[8,16,128]{2,1,0:T(8,128)(2,1)S(1)}, u32[]{:S(2)}, u32[]{:S(2)}) collective-permute-start(bf16[8,16,128]{2,1,0:T(8,128)(2,1)S(1)} %constant_dynamic-update-slice_fusion.w0_ref), channel_id=1, source_target_pairs={{0,192},{32,224},{64,0},{96,32},{128,64},{160,96},{192,128},{224,1... | collective-permute-start | bytes 98312 | tf_op jit(solution)/shard_map/ppermute | solution.py:294
  13.4 3.1 %gate.1 = bf16[32,16,1536]{2,1,0:T(8,128)(2,1)} custom-call(bf16[512,1536]{1,0:T(8,128)(2,1)} %bitcast.23, bf16[512,1536]{1,0:T(8,128)(2,1)} %bitcast.25), custom_call_target="tpu_custom_call" | custom-call | flops 402653184 | bytes 4718592 | tf_op jit(solution)/shard_map/gate/pallas_call | solution.py:116
  16.5 0.0 copy-start.3
  16.6 8.0 %all-to-all-start = ((bf16[32,16,1536]{2,1,0:T(8,128)(2,1)}), bf16[32,16,1536]{2,1,0:T(8,128)(2,1)S(1)}, u32[]{:S(2)}, u32[]{:S(2)}) async-start(bf16[32,16,1536]{2,1,0:T(8,128)(2,1)} %gate.1), calls=%async_computation | async-start | bytes 3145728 | tf_op jit(solution)/shard_map/all_to_all | solution.py:284
  24.6 0.1 collective-permute-start.3
  24.7 0.1 copy.14.idx_ref
  24.8 1.2 collective-permute-done.3.mate_ref
  26.0 1.8 %factor.1 = (bf16[4,128,128]{2,1,0:T(8,128)(2,1)S(1)}, bf16[512,512]{1,0:T(8,128)(2,1)S(1)}, bf16[512,512]{1,0:T(8,128)(2,1)S(1)}, f32[128,128]{1,0:T(8,128)S(1)}) custom-call(s32[1]{0:T(128)} %bitcast.place_ref, bf16[8,16,128]{2,1,0:T(8,128)(2,1)S(1)} %constant_dynamic-update-slice_fusion.w0_ref, bf16[8,16,128]{2,1,0:T(8,128)(2,1)S(1)} %collective-permute-done.w1_ref, ...), custom_call_target="tpu_custom_call" | custom-call | flops 805306368 | bytes 1572864 | tf_op jit(solution)/shard_map/factor/pallas_call | solution.py:303
  27.8 0.0 copy-start.1
  27.8 0.8 copy-done.1
  28.6 6.1 %first.1.refs_2_ = bf16[32,32,1536]{2,1,0:T(8,128)(2,1)} custom-call(bf16[4,128,128]{2,1,0:T(8,128)(2,1)S(1)} %get-tuple-element.34.blocks, bf16[512,1536]{1,0:T(8,128)(2,1)} %bitcast.17, bf16[512,1536]{1,0:T(8,128)(2,1)} %bitcast.20), custom_call_target="tpu_custom_call" | custom-call | flops 805306368 | bytes 4718592 | tf_op jit(solution)/shard_map/first/pallas_call | solution.py:310
  34.7 10.5 %all-to-all-done.refs_1_ = bf16[32,16,1536]{2,1,0:T(8,128)(2,1)S(1)} async-done(((bf16[32,16,1536]{2,1,0:T(8,128)(2,1)}), bf16[32,16,1536]{2,1,0:T(8,128)(2,1)S(1)}, u32[]{:S(2)}, u32[]{:S(2)}) %all-to-all-start) | async-done | bytes 1572896 | tf_op jit(solution)/shard_map/all_to_all | solution.py:284
  45.2 2.8 %back.1 = (bf16[32,32,1536]{2,1,0:T(8,128)(2,1)}, bf16[4,128,1536]{2,1,0:T(8,128)(2,1)}) custom-call(bf16[512,512]{1,0:T(8,128)(2,1)S(1)} %get-tuple-element.32.refs_0_, bf16[32,16,1536]{2,1,0:T(8,128)(2,1)S(1)} %all-to-all-done.refs_1_, bf16[32,32,1536]{2,1,0:T(8,128)(2,1)} %first.1.refs_2_), custom_call_target="tpu_custom_call", output_to_operand_aliasing={{0}: (2, {})} | custom-call | flops 1610612736 | bytes 4718592 | tf_op jit(solution)/shard_map/back/pallas_call | solution.py:116
  48.0 0.0 copy-start.2
  48.0 43.2 %all_to_all.15.refs_1_.gf_ref.f_ref = bf16[32,32,1536]{2,1,0:T(8,128)(2,1)S(1)} all-to-all(bf16[32,32,1536]{2,1,0:T(8,128)(2,1)} %get-tuple-element.35), channel_id=1, replica_groups=mesh['dp'=8,'seq'=32] {'seq'}, dimensions={0} | all-to-all | bytes 6291456 | tf_op jit(solution)/shard_map/all_to_all | solution.py:284
  91.2 2.3 %mix.1 = bf16[32,16,1536]{2,1,0:T(8,128)(2,1)} custom-call(bf16[512,512]{1,0:T(8,128)(2,1)S(1)} %copy-done.2, bf16[32,32,1536]{2,1,0:T(8,128)(2,1)S(1)} %all_to_all.15.refs_1_.gf_ref.f_ref), custom_call_target="tpu_custom_call" | custom-call | flops 805306368 | bytes 3145728 | tf_op jit(solution)/shard_map/mix/pallas_call | solution.py:116
  93.5 5.6 %all-to-all-start.2 = ((bf16[32,16,1536]{2,1,0:T(8,128)(2,1)}), bf16[32,16,1536]{2,1,0:T(8,128)(2,1)}, u32[]{:S(2)}, u32[]{:S(2)}) async-start(bf16[32,16,1536]{2,1,0:T(8,128)(2,1)} %mix.1), calls=%async_computation.2 | async-start | bytes 3145728 | tf_op jit(solution)/shard_map/all_to_all | solution.py:284
  99.1 0.0 copy-start
  99.1 1.4 %copy-done = bf16[4,128,1536]{2,1,0:T(8,128)(2,1)S(1)} copy-done((bf16[4,128,1536]{2,1,0:T(8,128)(2,1)S(1)}, bf16[4,128,1536]{2,1,0:T(8,128)(2,1)}, u32[]{:S(2)}) %copy-start) | copy-done | bytes 1572888
  100.5 6.2 %sums.1 = (f32[4,8,16,128]{3,2,1,0:T(8,128)S(1)}, f32[4,8,16,128]{3,2,1,0:T(8,128)S(1)}) custom-call(s32[1]{0:T(128)S(6)} %and.4.core_ref, f32[128,128]{1,0:T(8,128)S(1)} %get-tuple-element.40.pat_ref, bf16[4,128,1536]{2,1,0:T(8,128)(2,1)S(1)} %copy-done, bf16[32,32,1536]{2,1,0:T(8,128)(2,1)S(1)} %all_to_all.15.refs_1_.gf_ref.f_ref, ...), custom_call_target="tpu_custom_call" | custom-call | flops 2415919104 | bytes 7864320 | tf_op jit(solution)/shard_map/sums/pallas_call | solution.py:323
  106.7 0.1 collective-permute-start.4
  106.8 1.5 %collective-permute-done.4.got_ref = f32[4,8,16,128]{3,2,1,0:T(8,128)S(1)} collective-permute-done((f32[4,8,16,128]{3,2,1,0:T(8,128)S(1)}, f32[4,8,16,128]{3,2,1,0:T(8,128)S(1)}, u32[]{:S(2)}, u32[]{:S(2)}) %collective-permute-start.4) | collective-permute-done | bytes 262176 | tf_op jit(solution)/shard_map/ppermute | solution.py:333
  108.3 0.1 collective-permute-start.5
  108.4 3.2 %collective-permute-start.6 = (bf16[8,16,128]{2,1,0:T(8,128)(2,1)S(1)}, bf16[8,16,128]{2,1,0:T(8,128)(2,1)S(1)}, u32[]{:S(2)}, u32[]{:S(2)}) collective-permute-start(bf16[8,16,128]{2,1,0:T(8,128)(2,1)S(1)} %get-tuple-element.46), channel_id=1, source_target_pairs={{0,128},{32,160},{64,192},{96,224},{128,0},{160,32},{192,64},{224,... | collective-permute-start | bytes 98312 | tf_op jit(solution)/shard_map/ppermute | solution.py:341
  111.7 1.2 collective-permute-start.7
  112.8 6.3 %grads.1 = (bf16[512,1536]{1,0:T(8,128)(2,1)}, bf16[512,1536]{1,0:T(8,128)(2,1)}) custom-call(bf16[4,128,128]{2,1,0:T(8,128)(2,1)S(1)} %get-tuple-element.34.blocks, bf16[32,32,1536]{2,1,0:T(8,128)(2,1)S(1)} %all_to_all.15.refs_1_.gf_ref.f_ref, bf16[512,1536]{1,0:T(8,128)(2,1)} %bitcast.19, bf16[512,1536]{1,0:T(8,128)(2,1)} %bitcast.22), custom_call_target="tpu_custom_call" | custom-call | flops 805306368 | bytes 7864320 | tf_op jit(solution)/shard_map/grads/pallas_call | solution.py:329
  119.2 0.6 fusion
  119.8 3.8 %tail.1 = (bf16[512,1536]{1,0:T(8,128)(2,1)}, bf16[512,1536]{1,0:T(8,128)(2,1)}) custom-call(bf16[32,16,1536]{2,1,0:T(8,128)(2,1)} %all-to-all-done.2.refs_0_, bf16[512,1536]{1,0:T(8,128)(2,1)} %bitcast.24, bf16[512,1536]{1,0:T(8,128)(2,1)} %bitcast.26), custom_call_target="tpu_custom_call" | custom-call | flops 402653184 | bytes 7864320 | tf_op jit(solution)/shard_map/tail/pallas_call | solution.py:116
  (12 shorter events, 0.1 us)
Async XLA Ops:
  2.1 14.5 %collective-permute-start = (bf16[8,16,128]{2,1,0:T(8,128)(2,1)S(1)}, bf16[8,16,128]{2,1,0:T(8,128)(2,1)S(1)}, u32[]{:S(2)}, u32[]{:S(2)}) collective-permute-start(bf16[8,16,128]{2,1,0:T(8,128)(2,1)S(1)} %constant_dynamic-update-slice_fusion.w0_ref), channel_id=1, source_target_pairs={{0,64},{32,96},{64,128},{96,160},{128,192},{160,224},{192,0},{224,... | collective-permute-start | bytes 98312 | tf_op jit(solution)/shard_map/ppermute | solution.py:294
  5.3 11.2 %collective-permute-start.1 = (bf16[8,16,128]{2,1,0:T(8,128)(2,1)S(1)}, bf16[8,16,128]{2,1,0:T(8,128)(2,1)S(1)}, u32[]{:S(2)}, u32[]{:S(2)}) collective-permute-start(bf16[8,16,128]{2,1,0:T(8,128)(2,1)S(1)} %constant_dynamic-update-slice_fusion.w0_ref), channel_id=1, source_target_pairs={{0,128},{32,160},{64,192},{96,224},{128,0},{160,32},{192,64},{224,... | collective-permute-start | bytes 98312 | tf_op jit(solution)/shard_map/ppermute | solution.py:294
  10.7 5.8 %collective-permute-start.2 = (bf16[8,16,128]{2,1,0:T(8,128)(2,1)S(1)}, bf16[8,16,128]{2,1,0:T(8,128)(2,1)S(1)}, u32[]{:S(2)}, u32[]{:S(2)}) collective-permute-start(bf16[8,16,128]{2,1,0:T(8,128)(2,1)S(1)} %constant_dynamic-update-slice_fusion.w0_ref), channel_id=1, source_target_pairs={{0,192},{32,224},{64,0},{96,32},{128,64},{160,96},{192,128},{224,1... | collective-permute-start | bytes 98312 | tf_op jit(solution)/shard_map/ppermute | solution.py:294
  16.5 8.2 %copy-start.3 = (s32[128,16]{0,1:T(8,128)S(1)}, s32[128,16]{0,1:T(8,128)}, u32[]{:S(2)}) copy-start(s32[128,16]{0,1:T(8,128)} %param.12) | copy-start | bytes 24580
  16.6 28.6 %all-to-all-start = ((bf16[32,16,1536]{2,1,0:T(8,128)(2,1)}), bf16[32,16,1536]{2,1,0:T(8,128)(2,1)S(1)}, u32[]{:S(2)}, u32[]{:S(2)}) async-start(bf16[32,16,1536]{2,1,0:T(8,128)(2,1)} %gate.1), calls=%async_computation | async-start | bytes 3145728 | tf_op jit(solution)/shard_map/all_to_all | solution.py:284
  24.6 1.4 %collective-permute-start.3 = (bf16[4,8,16,128]{3,2,1,0:T(8,128)(2,1)S(1)}, bf16[4,8,16,128]{3,2,1,0:T(8,128)(2,1)S(1)}, u32[]{:S(2)}, u32[]{:S(2)}) collective-permute-start(bf16[4,8,16,128]{3,2,1,0:T(8,128)(2,1)S(1)} %pad_maximum_fusion), channel_id=1, source_target_pairs={{0,32},{32,0},{64,96},{96,64},{128,160},{160,128},{192,224},{224,1... | collective-permute-start | bytes 393224 | tf_op jit(solution)/shard_map/ppermute | solution.py:301
  27.8 0.8 copy-start.1
  48.0 43.2 %copy-start.2 = (bf16[512,512]{1,0:T(8,128)(2,1)S(1)}, bf16[512,512]{1,0:T(8,128)(2,1)}, u32[]{:S(2)}) copy-start(bf16[512,512]{1,0:T(8,128)(2,1)} %copy-done.1) | copy-start | bytes 1572868
  93.5 26.3 %all-to-all-start.2 = ((bf16[32,16,1536]{2,1,0:T(8,128)(2,1)}), bf16[32,16,1536]{2,1,0:T(8,128)(2,1)}, u32[]{:S(2)}, u32[]{:S(2)}) async-start(bf16[32,16,1536]{2,1,0:T(8,128)(2,1)} %mix.1), calls=%async_computation.2 | async-start | bytes 3145728 | tf_op jit(solution)/shard_map/all_to_all | solution.py:284
  99.1 1.4 %copy-start = (bf16[4,128,1536]{2,1,0:T(8,128)(2,1)S(1)}, bf16[4,128,1536]{2,1,0:T(8,128)(2,1)}, u32[]{:S(2)}) copy-start(bf16[4,128,1536]{2,1,0:T(8,128)(2,1)} %get-tuple-element.41.gm_ref) | copy-start | bytes 4718596
  106.7 1.6 %collective-permute-start.4 = (f32[4,8,16,128]{3,2,1,0:T(8,128)S(1)}, f32[4,8,16,128]{3,2,1,0:T(8,128)S(1)}, u32[]{:S(2)}, u32[]{:S(2)}) collective-permute-start(f32[4,8,16,128]{3,2,1,0:T(8,128)S(1)} %get-tuple-element.43), channel_id=1, source_target_pairs={{0,32},{32,0},{64,96},{96,64},{128,160},{160,128},{192,224},{224,1... | collective-permute-start | bytes 786440 | tf_op jit(solution)/shard_map/ppermute | solution.py:333
  108.3 10.8 %collective-permute-start.5 = (bf16[8,16,128]{2,1,0:T(8,128)(2,1)S(1)}, bf16[8,16,128]{2,1,0:T(8,128)(2,1)S(1)}, u32[]{:S(2)}, u32[]{:S(2)}) collective-permute-start(bf16[8,16,128]{2,1,0:T(8,128)(2,1)S(1)} %get-tuple-element.45), channel_id=1, source_target_pairs={{0,64},{32,96},{64,128},{96,160},{128,192},{160,224},{192,0},{224,... | collective-permute-start | bytes 98312 | tf_op jit(solution)/shard_map/ppermute | solution.py:341
  108.4 10.7 %collective-permute-start.6 = (bf16[8,16,128]{2,1,0:T(8,128)(2,1)S(1)}, bf16[8,16,128]{2,1,0:T(8,128)(2,1)S(1)}, u32[]{:S(2)}, u32[]{:S(2)}) collective-permute-start(bf16[8,16,128]{2,1,0:T(8,128)(2,1)S(1)} %get-tuple-element.46), channel_id=1, source_target_pairs={{0,128},{32,160},{64,192},{96,224},{128,0},{160,32},{192,64},{224,... | collective-permute-start | bytes 98312 | tf_op jit(solution)/shard_map/ppermute | solution.py:341
  111.7 7.5 %collective-permute-start.7 = (bf16[8,16,128]{2,1,0:T(8,128)(2,1)S(1)}, bf16[8,16,128]{2,1,0:T(8,128)(2,1)S(1)}, u32[]{:S(2)}, u32[]{:S(2)}) collective-permute-start(bf16[8,16,128]{2,1,0:T(8,128)(2,1)S(1)} %get-tuple-element.47), channel_id=1, source_target_pairs={{0,192},{32,224},{64,0},{96,32},{128,64},{160,96},{192,128},{224,1... | collective-permute-start | bytes 98312 | tf_op jit(solution)/shard_map/ppermute | solution.py:341

commit v4 on v3

--- a/solution.py
+++ b/solution.py
@@ -9,6 +9,7 @@
 F32 = jnp.float32
 MIB = 1024 * 1024
 STEP = 512
+WIDE = 512
 
 
 def dot(a, b, ca=1, cb=0):
@@ -51,7 +52,7 @@
     return (a.astype(F32) * b.astype(F32)).astype(BF16)
 
 
-def call(kernel, name, grid, in_specs, out_specs, out_shape, scratch=(), flops=0, nbytes=0, aliases=None, vmem=8):
+def call(kernel, name, grid, in_specs, out_specs, out_shape, scratch=(), flops=0, nbytes=0, aliases=None, vmem=12):
     return pl.pallas_call(
         kernel,
         name=name,
@@ -75,24 +76,30 @@
     return ref.at[:, pl.ds(rows, 16), columns] if ref.shape[0] == 32 else ref.at[:, :, columns]
 
 
-def streamed(body, name, ins, out_shapes, width, consts=(), out_rows=0, extra=(), aliases=None, scratch=(), prepare=None,
-             flops=0, nbytes=0, vmem=16):
-    channels = ins[0].shape[-1]
+def streamed(body, name, ins, out_shapes, width, consts=(), resident=None, out_rows=0, extra=(), aliases=None, scratch=(),
+             prepare=None, echo=None, flops=0, nbytes=0, vmem=16):
+    channels = out_shapes[0].shape[-1]
     count = channels // width
-    n_const, n_in, n_extra, n_out = len(consts), len(ins), len(extra), len(out_shapes)
+    vmem_in = list(consts) + ([] if resident is None else [resident])
+    n_vmem, n_in, n_extra, n_out = len(vmem_in), len(ins), len(extra), len(out_shapes)
 
     def buffer(array):
         shape = array.shape
         return pltpu.VMEM((count, *((32, 16) if len(shape) == 3 and shape[0] == 32 else shape[:-1]), width), BF16)
 
     def kernel(*refs):
-        const_refs, refs = refs[:n_const], refs[n_const:]
+        vmem_refs, refs = refs[:n_vmem], refs[n_vmem:]
         in_refs, refs = refs[:n_in], refs[n_in + n_extra :]
         out_refs, refs = refs[:n_out], refs[n_out:]
+        leaving = []
+        if echo is not None:
+            leaving.append(pltpu.make_async_copy(vmem_refs[-1], refs[0], refs[-1].at[0]))
+            leaving[0].start()
+            refs = refs[1:-1]
         bufs, refs = refs[:n_in], refs[n_in:]
         outs, refs = refs[:n_out], refs[n_out:]
         in_sem, out_sem, scratch_refs = refs[0], refs[1], refs[2:]
-        arriving, leaving = [], []
+        arriving = []
         for c in range(count):
             arriving.append([
                 pltpu.make_async_copy(chunk_of(in_refs[i], c, width), bufs[i].at[c], in_sem.at[i, c]) for i in range(n_in)
@@ -105,7 +112,9 @@
             for copy in arriving[c]:
                 copy.wait()
             values = [buf[c].reshape(512, width) for buf in bufs]
-            for o, make in enumerate(body(const_refs, scratch_refs, *values)):
+            if resident is not None:
+                values = [vmem_refs[-1][:, 0:16, c * width : c * width + width].reshape(512, width)] + values
+            for o, make in enumerate(body(vmem_refs, scratch_refs, *values)):
                 outs[o][c] = make().reshape(outs[o].shape[1:])
                 copy = pltpu.make_async_copy(outs[o].at[c], chunk_of(out_refs[o], c, width, out_rows), out_sem.at[o, c])
                 copy.start()
@@ -116,17 +125,18 @@
     return pl.pallas_call(
         kernel,
         name=name,
-        in_specs=[VMEM_SPEC] * n_const + [pl.BlockSpec(memory_space=pl.ANY)] * (n_in + n_extra),
-        out_specs=[pl.BlockSpec(memory_space=pltpu.HBM)] * n_out,
-        out_shape=list(out_shapes),
+        in_specs=[VMEM_SPEC] * n_vmem + [pl.BlockSpec(memory_space=pl.ANY)] * (n_in + n_extra),
+        out_specs=[pl.BlockSpec(memory_space=pltpu.HBM)] * (n_out + (echo is not None)),
+        out_shape=list(out_shapes) + ([] if echo is None else [echo]),
         scratch_shapes=[buffer(x) for x in ins]
         + [buffer(x) for x in out_shapes]
-        + [pltpu.SemaphoreType.DMA((n_in, count)), pltpu.SemaphoreType.DMA((n_out, count))]
-        + list(scratch),
+        + [pltpu.SemaphoreType.DMA((max(n_in, 1), count)), pltpu.SemaphoreType.DMA((n_out, count))]
+        + list(scratch)
+        + ([] if echo is None else [pltpu.SemaphoreType.DMA((1,))]),
         input_output_aliases=aliases or {},
         cost_estimate=pl.CostEstimate(flops=flops, transcendentals=0, bytes_accessed=nbytes),
         compiler_params=pltpu.CompilerParams(vmem_limit_bytes=vmem * MIB),
-    )(*[held(x) for x in consts], *ins, *extra)
+    )(*[held(x) for x in vmem_in], *ins, *extra)
 
 
 def pinned(x):
@@ -156,28 +166,42 @@
     perm[...] = one_hot(256, slab_order)
 
 
-def make_offset_order(perm):
-    perm[...] = one_hot(256, offset_order)
-
-
 def gate_body(consts, scratch, q, cot):
     return [lambda: to_slabs(scratch[0][...], times(q, cot))]
 
 
 def factor_body(consts, scratch, x):
     return [lambda: dot(consts[0][...], x).astype(BF16)]
-
-
-def back_body(consts, scratch, x):
-    return [
-        lambda: dot(consts[0][...], x).astype(BF16),
-        lambda: jnp.concatenate(by_offset(scratch[0][...], x), axis=0),
-    ]
 
 
 def tail_body(consts, scratch, x, q, cot):
     mixed = jnp.concatenate(from_slabs(scratch[0][...], x), axis=0)
     return [lambda: times(q, mixed), lambda: times(cot, mixed)]
+
+
+def pack_kernel(*refs):
+    ins, out_ref, sem = refs[:-2], refs[-2], refs[-1]
+    copies, start = [], 0
+    for i, ref in enumerate(ins):
+        copies.append(pltpu.make_async_copy(ref, out_ref.at[pl.ds(start, ref.shape[0])], sem.at[i]))
+        start += ref.shape[0]
+    for copy in copies:
+        copy.start()
+    for copy in copies:
+        copy.wait()
+
+
+def pack(name, *arrays):
+    shape = (sum(a.shape[0] for a in arrays), *arrays[0].shape[1:])
+    return pl.pallas_call(
+        pack_kernel,
+        name=name,
+        in_specs=[pl.BlockSpec(memory_space=pl.ANY)] * len(arrays),
+        out_specs=VMEM_SPEC,
+        out_shape=pltpu.VMEM(shape, arrays[0].dtype),
+        scratch_shapes=[pltpu.SemaphoreType.DMA((len(arrays),))],
+        compiler_params=pltpu.CompilerParams(vmem_limit_bytes=4 * MIB),
+    )(*[pinned(a) for a in arrays])
 
 
 def first_kernel(blocks, k_ref, v_ref, o_ref, perm):
@@ -230,9 +254,10 @@
     product = times(k_ref[...], v_ref[...])
     for k in range(4):
         acc[k] += dot(grad_first[k], product[k * 128 : k * 128 + 128], cb=1)
+    left = by_offset(sort[...], gm_ref[...].reshape(512, width))
     right = by_offset(sort[...], f_ref[...].reshape(512, width))
     for j in range(4):
-        acc[4 + j] += dot(gm_ref[j], right[j], cb=1)
+        acc[4 + j] += dot(left[j], right[j], cb=1)
 
     @pl.when(pl.program_id(0) == pl.num_programs(0) - 1)
     def _():
@@ -268,7 +293,7 @@
 def on_device(query, key, value, block_weights, mix_weights, block_index, cotangent):
     channels = query.shape[2]
     q, k, v, cot = (a.reshape(512, channels) for a in (query, key, value, cotangent))
-    width = 256
+    width = WIDE
     grid = (channels // width,)
     rows, slab = rows_spec(width), slab_spec(width)
     smem = pl.BlockSpec(memory_space=pltpu.SMEM)
@@ -290,7 +315,7 @@
         return [(i, ((i // 2 + r) % 4) * 2 + i % 2) for i in range(8)]
 
     mate = [(i, i ^ 1) for i in range(8)]
-    own_rows = jnp.concatenate([block_weights, mix_weights], axis=0)
+    own_rows = pack("weights", block_weights, mix_weights)
     column = [own_rows] + [lax.ppermute(own_rows, "dp", hop(r)) for r in (1, 2, 3)]
     (gated,) = streamed(
         gate_body, "gate", [pinned(q), pinned(cot)], [slab_shape], STEP, scratch=[perm], prepare=make_slab_order,
@@ -310,22 +335,24 @@
     out = call(first_kernel, "first", grid, [VMEM_SPEC, rows, rows], slab, pair_shape, [perm], work, 3 * size)(
         held(blocks), pinned(k), pinned(v)
     )
-    out, left = streamed(
-        back_body, "back", [grad_cols], [pair_shape, pltpu.HBM((4, 128, channels), BF16)], STEP, consts=[factor_t],
-        out_rows=16, extra=[out], aliases={2: 0}, scratch=[perm], prepare=make_offset_order,
-        flops=2 * work, nbytes=3 * size,
+    out, grad_cols = streamed(
+        factor_body, "back", [], [pair_shape], STEP, consts=[factor_t], resident=grad_cols, echo=slab_shape, out_rows=16, extra=[out],
+        aliases={2: 0}, flops=work, nbytes=2 * size,
     )
     got = exchange(out)
-    (mixed_cols,) = streamed(factor_body, "mix", [got], [slab_shape], STEP, consts=[factor], flops=work, nbytes=2 * size)
+    (mixed_cols,) = streamed(
+        factor_body, "mix", [], [slab_shape], STEP, consts=[factor], resident=got,
+        flops=work, nbytes=2 * size,
+    )
     returned = exchange(mixed_cols)
 
     part = jax.ShapeDtypeStruct((4, 8, 16, 128), F32)
     send, keep = call(
         sums_kernel, "sums", grid,
-        [smem, VMEM_SPEC, pl.BlockSpec((4, 128, width), lambda d: (0, 0, d)), slab, slab_spec(width, 1), rows, rows],
+        [smem, VMEM_SPEC, slab, slab, slab_spec(width, 1), rows, rows],
         [whole(4, 8, 16, 128), whole(4, 8, 16, 128)], [part, part],
         [perm, perm, pltpu.VMEM((8, 128, 128), F32)], 3 * work, 5 * size,
-    )(core, held(pattern), left, got, got, pinned(k), pinned(v))
+    )(core, held(pattern), grad_cols, got, got, pinned(k), pinned(v))
     grad_key, grad_value = call(
         grads_kernel, "grads", grid, [VMEM_SPEC, slab_spec(width, 1), rows, rows], [rows, rows],
         [row_shape, row_shape], [perm], work, 5 * size,

time: 125 us -> 123 us (0.984)
  Pallas kernels: 32.4 us -> 28.2 us
  waiting for transfers between devices: 13.3 us -> 17.3 us
  local copies, waits for them, and re-layouts: 4.38 us -> 2.93 us
    all_to_all x2, waiting for transfers between devices: 10.5 us -> 14.2 us  [exchange(): return lax.all_to_all(x, 'seq', split_axis=0, concat_axis=0, tiled=True)]
    pallas_call x5 -> x6, Pallas kernels: 18.2 us -> 16.6 us  [the longest x4 11 us: streamed(): pl.pallas_call(kernel, name=name, in_specs=[VMEM_SPEC] * n_vmem + [pl.Blo...]
    pallas_call x1, Pallas kernels: 6.08 us -> 4.62 us  [on_device(): call(first_kernel, 'first', grid, [VMEM_SPEC, rows, rows], slab, pair_sha...]
    unnamed x10 -> x9, local copies, waits for them, and re-layouts: 3.02 us -> 2.3 us
  transfers between devices with their start and end apart: 10 -> 10, of which waited for: 3 -> 5; matrix products, arithmetic and copies ran while one was open for 1% -> 1% of each run, Pallas kernels for 19% -> 16%
where the time goes in v4:
time: 123 us; the launch traced here: 122 us
  blocking collectives  43.2 us (35%)
  starting transfers between devices  29.9 us (24%)
  Pallas kernels  28.2 us (23%)
  waiting for transfers between devices  17.3 us (14%)
  local copies, waits for them, and re-layouts  2.93 us (2%)
    all_to_all x1, blocking collectives, exchange(): return lax.all_to_all(x, 'seq', split_axis=0, concat_axis=0, tiled=True)  43.2 us
    all_to_all x2, waiting for transfers between devices, exchange(): return lax.all_to_all(x, 'seq', split_axis=0, concat_axis=0, tiled=True)  14.2 us
    all_to_all x2, starting transfers between devices, exchange(): return lax.all_to_all(x, 'seq', split_axis=0, concat_axis=0, tiled=True)  13.6 us
    ppermute x3, starting transfers between devices, on_device(): lax.ppermute(own_rows, 'dp', hop(r))  11.4 us
    pallas_call x4, Pallas kernels, streamed(): pl.pallas_call(kernel, name=name, in_specs=[VMEM_SPEC] * n_vmem + [pl.Blo...  11 us
    pallas_call x1, Pallas kernels, on_device(): call(grads_kernel, 'grads', grid, [VMEM_SPEC, slab_spec(width, 1), rows,...  5.18 us
    pallas_call x1, Pallas kernels, on_device(): call(sums_kernel, 'sums', grid, [smem, VMEM_SPEC, slab, slab, slab_spec(w...  4.88 us
    ppermute x3, starting transfers between devices, on_device(): total = total + lax.ppermute(other, 'dp', hop(r)).astype(F32)  4.68 us
  transfers between devices with their start and end apart: 10, of which 5 were waited for; matrix products, arithmetic and copies ran while one was open for 1% of the time, Pallas kernels for 16%

profile of v4, /device:TPU:8, one launch (start us, length us, event | category | flops | bytes accessed | tf_op | source)
XLA Modules:
  0.0 122.3 jit_solution(14862613917108978562)
XLA Ops:
  0.6 0.8 weights.1.w0_ref
  1.4 3.3 %collective-permute-start = (bf16[8,16,128]{2,1,0:T(8,128)(2,1)S(1)}, bf16[8,16,128]{2,1,0:T(8,128)(2,1)S(1)}, u32[]{:S(2)}, u32[]{:S(2)}) collective-permute-start(bf16[8,16,128]{2,1,0:T(8,128)(2,1)S(1)} %weights.1.w0_ref), channel_id=1, source_target_pairs={{0,64},{32,96},{64,128},{96,160},{128,192},{160,224},{192,0},{224,... | collective-permute-start | bytes 98312 | tf_op jit(solution)/shard_map/ppermute | solution.py:319
  4.7 5.4 %collective-permute-start.1 = (bf16[8,16,128]{2,1,0:T(8,128)(2,1)S(1)}, bf16[8,16,128]{2,1,0:T(8,128)(2,1)S(1)}, u32[]{:S(2)}, u32[]{:S(2)}) collective-permute-start(bf16[8,16,128]{2,1,0:T(8,128)(2,1)S(1)} %weights.1.w0_ref), channel_id=1, source_target_pairs={{0,128},{32,160},{64,192},{96,224},{128,0},{160,32},{192,64},{224,... | collective-permute-start | bytes 98312 | tf_op jit(solution)/shard_map/ppermute | solution.py:319
  10.1 2.7 %collective-permute-start.2 = (bf16[8,16,128]{2,1,0:T(8,128)(2,1)S(1)}, bf16[8,16,128]{2,1,0:T(8,128)(2,1)S(1)}, u32[]{:S(2)}, u32[]{:S(2)}) collective-permute-start(bf16[8,16,128]{2,1,0:T(8,128)(2,1)S(1)} %weights.1.w0_ref), channel_id=1, source_target_pairs={{0,192},{32,224},{64,0},{96,32},{128,64},{160,96},{192,128},{224,1... | collective-permute-start | bytes 98312 | tf_op jit(solution)/shard_map/ppermute | solution.py:319
  12.8 3.1 %gate.1 = bf16[32,16,1536]{2,1,0:T(8,128)(2,1)} custom-call(bf16[512,1536]{1,0:T(8,128)(2,1)} %bitcast.23, bf16[512,1536]{1,0:T(8,128)(2,1)} %bitcast.25), custom_call_target="tpu_custom_call" | custom-call | flops 402653184 | bytes 4718592 | tf_op jit(solution)/shard_map/gate/pallas_call | solution.py:125
  15.9 0.0 copy-start.3
  16.0 8.0 %all-to-all-start = ((bf16[32,16,1536]{2,1,0:T(8,128)(2,1)}), bf16[32,16,1536]{2,1,0:T(8,128)(2,1)S(1)}, u32[]{:S(2)}, u32[]{:S(2)}) async-start(bf16[32,16,1536]{2,1,0:T(8,128)(2,1)} %gate.1), calls=%async_computation | async-start | bytes 3145728 | tf_op jit(solution)/shard_map/all_to_all | solution.py:309
  24.0 0.1 collective-permute-start.3
  24.1 0.1 copy.14.idx_ref
  24.2 1.2 collective-permute-done.3.mate_ref
  25.4 1.8 %factor.1 = (bf16[4,128,128]{2,1,0:T(8,128)(2,1)S(1)}, bf16[512,512]{1,0:T(8,128)(2,1)S(1)}, bf16[512,512]{1,0:T(8,128)(2,1)S(1)}, f32[128,128]{1,0:T(8,128)S(1)}) custom-call(s32[1]{0:T(128)} %bitcast.place_ref, bf16[8,16,128]{2,1,0:T(8,128)(2,1)S(1)} %weights.1.w0_ref, bf16[8,16,128]{2,1,0:T(8,128)(2,1)S(1)} %collective-permute-done.w1_ref, ...), custom_call_target="tpu_custom_call" | custom-call | flops 805306368 | bytes 1572864 | tf_op jit(solution)/shard_map/factor/pallas_call | solution.py:328
  27.2 0.0 copy-start.1
  27.2 0.8 copy-done.1
  28.0 4.6 %first.1.refs_2_ = bf16[32,32,1536]{2,1,0:T(8,128)(2,1)} custom-call(bf16[4,128,128]{2,1,0:T(8,128)(2,1)S(1)} %get-tuple-element.34.blocks, bf16[512,1536]{1,0:T(8,128)(2,1)} %bitcast.17, bf16[512,1536]{1,0:T(8,128)(2,1)} %bitcast.20), custom_call_target="tpu_custom_call" | custom-call | flops 805306368 | bytes 4718592 | tf_op jit(solution)/shard_map/first/pallas_call | solution.py:335
  32.6 12.0 %all-to-all-done.refs_1_ = bf16[32,16,1536]{2,1,0:T(8,128)(2,1)S(1)} async-done(((bf16[32,16,1536]{2,1,0:T(8,128)(2,1)}), bf16[32,16,1536]{2,1,0:T(8,128)(2,1)S(1)}, u32[]{:S(2)}, u32[]{:S(2)}) %all-to-all-start) | async-done | bytes 1572896 | tf_op jit(solution)/shard_map/all_to_all | solution.py:309
  44.6 2.2 %back.1 = (bf16[32,32,1536]{2,1,0:T(8,128)(2,1)}, bf16[32,16,1536]{2,1,0:T(8,128)(2,1)}) custom-call(bf16[512,512]{1,0:T(8,128)(2,1)S(1)} %get-tuple-element.32.refs_0_, bf16[32,16,1536]{2,1,0:T(8,128)(2,1)S(1)} %all-to-all-done.refs_1_, bf16[32,32,1536]{2,1,0:T(8,128)(2,1)} %first.1.refs_2_), custom_call_target="tpu_custom_call", output_to_operand_aliasing={{0}: (2, {})} | custom-call | flops 805306368 | bytes 3145728 | tf_op jit(solution)/shard_map/back/pallas_call | solution.py:125
  46.8 43.2 %all_to_all.15.refs_1_.gf_ref.f_ref = bf16[32,32,1536]{2,1,0:T(8,128)(2,1)S(1)} all-to-all(bf16[32,32,1536]{2,1,0:T(8,128)(2,1)} %get-tuple-element.35), channel_id=1, replica_groups=mesh['dp'=8,'seq'=32] {'seq'}, dimensions={0} | all-to-all | bytes 6291456 | tf_op jit(solution)/shard_map/all_to_all | solution.py:309
  90.0 1.8 %mix.1 = bf16[32,16,1536]{2,1,0:T(8,128)(2,1)} custom-call(bf16[512,512]{1,0:T(8,128)(2,1)S(1)} %copy-done.2, bf16[32,32,1536]{2,1,0:T(8,128)(2,1)S(1)} %all_to_all.15.refs_1_.gf_ref.f_ref), custom_call_target="tpu_custom_call" | custom-call | flops 805306368 | bytes 3145728 | tf_op jit(solution)/shard_map/mix/pallas_call | solution.py:125
  91.8 5.6 %all-to-all-start.2 = ((bf16[32,16,1536]{2,1,0:T(8,128)(2,1)}), bf16[32,16,1536]{2,1,0:T(8,128)(2,1)}, u32[]{:S(2)}, u32[]{:S(2)}) async-start(bf16[32,16,1536]{2,1,0:T(8,128)(2,1)} %mix.1), calls=%async_computation.2 | async-start | bytes 3145728 | tf_op jit(solution)/shard_map/all_to_all | solution.py:309
  97.4 0.0 copy-start
  97.4 1.4 %copy-done = bf16[32,16,1536]{2,1,0:T(8,128)(2,1)S(1)} copy-done((bf16[32,16,1536]{2,1,0:T(8,128)(2,1)S(1)}, bf16[32,16,1536]{2,1,0:T(8,128)(2,1)}, u32[]{:S(2)}) %copy-start) | copy-done | bytes 1572888
  98.8 4.9 %sums.1 = (f32[4,8,16,128]{3,2,1,0:T(8,128)S(1)}, f32[4,8,16,128]{3,2,1,0:T(8,128)S(1)}) custom-call(s32[1]{0:T(128)S(6)} %and.4.core_ref, f32[128,128]{1,0:T(8,128)S(1)} %get-tuple-element.40.pat_ref, bf16[32,16,1536]{2,1,0:T(8,128)(2,1)S(1)} %copy-done, bf16[32,32,1536]{2,1,0:T(8,128)(2,1)S(1)} %all_to_all.15.refs_1_.gf_ref.f_ref, ...), custom_call_target="tpu_custom_call" | custom-call | flops 2415919104 | bytes 7864320 | tf_op jit(solution)/shard_map/sums/pallas_call | solution.py:350
  103.7 0.1 collective-permute-start.4
  103.8 1.5 %collective-permute-done.4.got_ref = f32[4,8,16,128]{3,2,1,0:T(8,128)S(1)} collective-permute-done((f32[4,8,16,128]{3,2,1,0:T(8,128)S(1)}, f32[4,8,16,128]{3,2,1,0:T(8,128)S(1)}, u32[]{:S(2)}, u32[]{:S(2)}) %collective-permute-start.4) | collective-permute-done | bytes 262176 | tf_op jit(solution)/shard_map/ppermute | solution.py:360
  105.4 0.1 collective-permute-start.5
  105.5 3.2 %collective-permute-start.6 = (bf16[8,16,128]{2,1,0:T(8,128)(2,1)S(1)}, bf16[8,16,128]{2,1,0:T(8,128)(2,1)S(1)}, u32[]{:S(2)}, u32[]{:S(2)}) collective-permute-start(bf16[8,16,128]{2,1,0:T(8,128)(2,1)S(1)} %get-tuple-element.46), channel_id=1, source_target_pairs={{0,128},{32,160},{64,192},{96,224},{128,0},{160,32},{192,64},{224,... | collective-permute-start | bytes 98312 | tf_op jit(solution)/shard_map/ppermute | solution.py:368
  108.7 1.4 %collective-permute-start.7 = (bf16[8,16,128]{2,1,0:T(8,128)(2,1)S(1)}, bf16[8,16,128]{2,1,0:T(8,128)(2,1)S(1)}, u32[]{:S(2)}, u32[]{:S(2)}) collective-permute-start(bf16[8,16,128]{2,1,0:T(8,128)(2,1)S(1)} %get-tuple-element.47), channel_id=1, source_target_pairs={{0,192},{32,224},{64,0},{96,32},{128,64},{160,96},{192,128},{224,1... | collective-permute-start | bytes 98312 | tf_op jit(solution)/shard_map/ppermute | solution.py:368
  110.1 5.2 %grads.1 = (bf16[512,1536]{1,0:T(8,128)(2,1)}, bf16[512,1536]{1,0:T(8,128)(2,1)}) custom-call(bf16[4,128,128]{2,1,0:T(8,128)(2,1)S(1)} %get-tuple-element.34.blocks, bf16[32,32,1536]{2,1,0:T(8,128)(2,1)S(1)} %all_to_all.15.refs_1_.gf_ref.f_ref, bf16[512,1536]{1,0:T(8,128)(2,1)} %bitcast.19, bf16[512,1536]{1,0:T(8,128)(2,1)} %bitcast.22), custom_call_target="tpu_custom_call" | custom-call | flops 805306368 | bytes 7864320 | tf_op jit(solution)/shard_map/grads/pallas_call | solution.py:356
  115.3 0.3 collective-permute-done.7
  115.6 0.6 fusion
  116.2 2.2 %all-to-all-done.2.refs_0_ = bf16[32,16,1536]{2,1,0:T(8,128)(2,1)} async-done(((bf16[32,16,1536]{2,1,0:T(8,128)(2,1)}), bf16[32,16,1536]{2,1,0:T(8,128)(2,1)}, u32[]{:S(2)}, u32[]{:S(2)}) %all-to-all-start.2) | async-done | bytes 1572896 | tf_op jit(solution)/shard_map/all_to_all | solution.py:309
  118.5 3.8 %tail.1 = (bf16[512,1536]{1,0:T(8,128)(2,1)}, bf16[512,1536]{1,0:T(8,128)(2,1)}) custom-call(bf16[32,16,1536]{2,1,0:T(8,128)(2,1)} %all-to-all-done.2.refs_0_, bf16[512,1536]{1,0:T(8,128)(2,1)} %bitcast.24, bf16[512,1536]{1,0:T(8,128)(2,1)} %bitcast.26), custom_call_target="tpu_custom_call" | custom-call | flops 402653184 | bytes 7864320 | tf_op jit(solution)/shard_map/tail/pallas_call | solution.py:125
  (11 shorter events, 0.1 us)
Async XLA Ops:
  1.4 14.5 %collective-permute-start = (bf16[8,16,128]{2,1,0:T(8,128)(2,1)S(1)}, bf16[8,16,128]{2,1,0:T(8,128)(2,1)S(1)}, u32[]{:S(2)}, u32[]{:S(2)}) collective-permute-start(bf16[8,16,128]{2,1,0:T(8,128)(2,1)S(1)} %weights.1.w0_ref), channel_id=1, source_target_pairs={{0,64},{32,96},{64,128},{96,160},{128,192},{160,224},{192,0},{224,... | collective-permute-start | bytes 98312 | tf_op jit(solution)/shard_map/ppermute | solution.py:319
  4.7 11.2 %collective-permute-start.1 = (bf16[8,16,128]{2,1,0:T(8,128)(2,1)S(1)}, bf16[8,16,128]{2,1,0:T(8,128)(2,1)S(1)}, u32[]{:S(2)}, u32[]{:S(2)}) collective-permute-start(bf16[8,16,128]{2,1,0:T(8,128)(2,1)S(1)} %weights.1.w0_ref), channel_id=1, source_target_pairs={{0,128},{32,160},{64,192},{96,224},{128,0},{160,32},{192,64},{224,... | collective-permute-start | bytes 98312 | tf_op jit(solution)/shard_map/ppermute | solution.py:319
  10.1 5.8 %collective-permute-start.2 = (bf16[8,16,128]{2,1,0:T(8,128)(2,1)S(1)}, bf16[8,16,128]{2,1,0:T(8,128)(2,1)S(1)}, u32[]{:S(2)}, u32[]{:S(2)}) collective-permute-start(bf16[8,16,128]{2,1,0:T(8,128)(2,1)S(1)} %weights.1.w0_ref), channel_id=1, source_target_pairs={{0,192},{32,224},{64,0},{96,32},{128,64},{160,96},{192,128},{224,1... | collective-permute-start | bytes 98312 | tf_op jit(solution)/shard_map/ppermute | solution.py:319
  15.9 8.2 %copy-start.3 = (s32[128,16]{0,1:T(8,128)S(1)}, s32[128,16]{0,1:T(8,128)}, u32[]{:S(2)}) copy-start(s32[128,16]{0,1:T(8,128)} %param.12) | copy-start | bytes 24580
  16.0 28.6 %all-to-all-start = ((bf16[32,16,1536]{2,1,0:T(8,128)(2,1)}), bf16[32,16,1536]{2,1,0:T(8,128)(2,1)S(1)}, u32[]{:S(2)}, u32[]{:S(2)}) async-start(bf16[32,16,1536]{2,1,0:T(8,128)(2,1)} %gate.1), calls=%async_computation | async-start | bytes 3145728 | tf_op jit(solution)/shard_map/all_to_all | solution.py:309
  24.0 1.4 %collective-permute-start.3 = (bf16[4,8,16,128]{3,2,1,0:T(8,128)(2,1)S(1)}, bf16[4,8,16,128]{3,2,1,0:T(8,128)(2,1)S(1)}, u32[]{:S(2)}, u32[]{:S(2)}) collective-permute-start(bf16[4,8,16,128]{3,2,1,0:T(8,128)(2,1)S(1)} %pad_maximum_fusion), channel_id=1, source_target_pairs={{0,32},{32,0},{64,96},{96,64},{128,160},{160,128},{192,224},{224,1... | collective-permute-start | bytes 393224 | tf_op jit(solution)/shard_map/ppermute | solution.py:326
  27.2 0.8 copy-start.1
  46.8 43.2 %copy-start.2 = (bf16[512,512]{1,0:T(8,128)(2,1)S(1)}, bf16[512,512]{1,0:T(8,128)(2,1)}, u32[]{:S(2)}) copy-start(bf16[512,512]{1,0:T(8,128)(2,1)} %copy-done.1) | copy-start | bytes 1572868
  91.8 26.6 %all-to-all-start.2 = ((bf16[32,16,1536]{2,1,0:T(8,128)(2,1)}), bf16[32,16,1536]{2,1,0:T(8,128)(2,1)}, u32[]{:S(2)}, u32[]{:S(2)}) async-start(bf16[32,16,1536]{2,1,0:T(8,128)(2,1)} %mix.1), calls=%async_computation.2 | async-start | bytes 3145728 | tf_op jit(solution)/shard_map/all_to_all | solution.py:309
  97.4 1.4 %copy-start = (bf16[32,16,1536]{2,1,0:T(8,128)(2,1)S(1)}, bf16[32,16,1536]{2,1,0:T(8,128)(2,1)}, u32[]{:S(2)}) copy-start(bf16[32,16,1536]{2,1,0:T(8,128)(2,1)} %get-tuple-element.41.gm_ref) | copy-start | bytes 4718596
  103.7 1.6 %collective-permute-start.4 = (f32[4,8,16,128]{3,2,1,0:T(8,128)S(1)}, f32[4,8,16,128]{3,2,1,0:T(8,128)S(1)}, u32[]{:S(2)}, u32[]{:S(2)}) collective-permute-start(f32[4,8,16,128]{3,2,1,0:T(8,128)S(1)} %get-tuple-element.43), channel_id=1, source_target_pairs={{0,32},{32,0},{64,96},{96,64},{128,160},{160,128},{192,224},{224,1... | collective-permute-start | bytes 786440 | tf_op jit(solution)/shard_map/ppermute | solution.py:360
  105.4 9.9 %collective-permute-start.5 = (bf16[8,16,128]{2,1,0:T(8,128)(2,1)S(1)}, bf16[8,16,128]{2,1,0:T(8,128)(2,1)S(1)}, u32[]{:S(2)}, u32[]{:S(2)}) collective-permute-start(bf16[8,16,128]{2,1,0:T(8,128)(2,1)S(1)} %get-tuple-element.45), channel_id=1, source_target_pairs={{0,64},{32,96},{64,128},{96,160},{128,192},{160,224},{192,0},{224,... | collective-permute-start | bytes 98312 | tf_op jit(solution)/shard_map/ppermute | solution.py:368
  105.5 9.8 %collective-permute-start.6 = (bf16[8,16,128]{2,1,0:T(8,128)(2,1)S(1)}, bf16[8,16,128]{2,1,0:T(8,128)(2,1)S(1)}, u32[]{:S(2)}, u32[]{:S(2)}) collective-permute-start(bf16[8,16,128]{2,1,0:T(8,128)(2,1)S(1)} %get-tuple-element.46), channel_id=1, source_target_pairs={{0,128},{32,160},{64,192},{96,224},{128,0},{160,32},{192,64},{224,... | collective-permute-start | bytes 98312 | tf_op jit(solution)/shard_map/ppermute | solution.py:368
  108.7 6.9 %collective-permute-start.7 = (bf16[8,16,128]{2,1,0:T(8,128)(2,1)S(1)}, bf16[8,16,128]{2,1,0:T(8,128)(2,1)S(1)}, u32[]{:S(2)}, u32[]{:S(2)}) collective-permute-start(bf16[8,16,128]{2,1,0:T(8,128)(2,1)S(1)} %get-tuple-element.47), channel_id=1, source_target_pairs={{0,192},{32,224},{64,0},{96,32},{128,64},{160,96},{192,128},{224,1... | collective-permute-start | bytes 98312 | tf_op jit(solution)/shard_map/ppermute | solution.py:368

commit v5 on v4

--- a/solution.py
+++ b/solution.py
@@ -321,7 +321,6 @@
         gate_body, "gate", [pinned(q), pinned(cot)], [slab_shape], STEP, scratch=[perm], prepare=make_slab_order,
         flops=work // 2, nbytes=3 * size,
     )
-    gated, *column = lax.optimization_barrier((gated, *column))
     grad_cols = exchange(gated)
     other = lax.ppermute(jnp.stack(column), "dp", mate)
     shard_spec = whole(8, 16, 128)
@@ -332,7 +331,7 @@
          pltpu.VMEM((128, 128), F32)],
         [pltpu.VMEM((512, 512), BF16), pltpu.VMEM((4, 128, 128), BF16)], work, size,
     )(place, *column, other, block_index)
-    out = call(first_kernel, "first", grid, [VMEM_SPEC, rows, rows], slab, pair_shape, [perm], work, 3 * size)(
+    out = call(first_kernel, "first", grid, [VMEM_SPEC, rows, rows], slab, pair_shape, [perm], 36 * work, 3 * size)(
         held(blocks), pinned(k), pinned(v)
     )
     out, grad_cols = streamed(
@@ -352,7 +351,7 @@
         [smem, VMEM_SPEC, slab, slab, slab_spec(width, 1), rows, rows],
         [whole(4, 8, 16, 128), whole(4, 8, 16, 128)], [part, part],
         [perm, perm, pltpu.VMEM((8, 128, 128), F32)], 3 * work, 5 * size,
-    )(core, held(pattern), grad_cols, got, got, pinned(k), pinned(v))
+    )(core, held(pattern), pinned(grad_cols), got, got, pinned(k), pinned(v))
     grad_key, grad_value = call(
         grads_kernel, "grads", grid, [VMEM_SPEC, slab_spec(width, 1), rows, rows], [rows, rows],
         [row_shape, row_shape], [perm], work, 5 * size,

time: 123 us -> 123 us (level)
  local copies, waits for them, and re-layouts: 2.93 us -> 1.53 us
    ppermute x3, waiting for transfers between devices: 0.34 us -> 1.75 us  [on_device(): total = total + lax.ppermute(other, 'dp', hop(r)).astype(F32)]
    unnamed x9 -> x7, local copies, waits for them, and re-layouts: 2.3 us -> 0.9 us
  transfers between devices with their start and end apart: 10 -> 10, of which waited for: 5 -> 6; matrix products, arithmetic and copies ran while one was open for 1% -> 1% of each run, Pallas kernels for 16% -> 16%
where the time goes in v5:
time: 123 us
  blocking collectives  43.2 us (35%)
  starting transfers between devices  30.7 us (25%)
  Pallas kernels  28.4 us (23%)
  waiting for transfers between devices  17.9 us (15%)
  local copies, waits for them, and re-layouts  1.53 us (1%)
    all_to_all x1, blocking collectives, exchange(): return lax.all_to_all(x, 'seq', split_axis=0, concat_axis=0, tiled=True)  43.2 us
    all_to_all x2, starting transfers between devices, exchange(): return lax.all_to_all(x, 'seq', split_axis=0, concat_axis=0, tiled=True)  13.6 us
    all_to_all x2, waiting for transfers between devices, exchange(): return lax.all_to_all(x, 'seq', split_axis=0, concat_axis=0, tiled=True)  13.4 us
    ppermute x3, starting transfers between devices, on_device(): lax.ppermute(own_rows, 'dp', hop(r))  11.4 us
    pallas_call x4, Pallas kernels, streamed(): pl.pallas_call(kernel, name=name, in_specs=[VMEM_SPEC] * n_vmem + [pl.Blo...  11 us
    ppermute x3, starting transfers between devices, on_device(): total = total + lax.ppermute(other, 'dp', hop(r)).astype(F32)  5.53 us
    pallas_call x1, Pallas kernels, on_device(): call(grads_kernel, 'grads', grid, [VMEM_SPEC, slab_spec(width, 1), rows,...  5.16 us
    pallas_call x1, Pallas kernels, on_device(): call(sums_kernel, 'sums', grid, [smem, VMEM_SPEC, slab, slab, slab_spec(w...  5.03 us
  transfers between devices with their start and end apart: 10, of which 6 were waited for; matrix products, arithmetic and copies ran while one was open for 1% of the time, Pallas kernels for 16%

profile of v5, /device:TPU:8, one launch (start us, length us, event | category | flops | bytes accessed | tf_op | source)
XLA Modules:
  0.0 122.5 jit_solution(13814966873225176831)
XLA Ops:
  0.6 0.8 weights.1.w0_ref
  1.4 3.3 %collective-permute-start = (bf16[8,16,128]{2,1,0:T(8,128)(2,1)S(1)}, bf16[8,16,128]{2,1,0:T(8,128)(2,1)S(1)}, u32[]{:S(2)}, u32[]{:S(2)}) collective-permute-start(bf16[8,16,128]{2,1,0:T(8,128)(2,1)S(1)} %weights.1.w0_ref), channel_id=1, source_target_pairs={{0,64},{32,96},{64,128},{96,160},{128,192},{160,224},{192,0},{224,... | collective-permute-start | bytes 98312 | tf_op jit(solution)/shard_map/ppermute | solution.py:319
  4.7 5.4 %collective-permute-start.1 = (bf16[8,16,128]{2,1,0:T(8,128)(2,1)S(1)}, bf16[8,16,128]{2,1,0:T(8,128)(2,1)S(1)}, u32[]{:S(2)}, u32[]{:S(2)}) collective-permute-start(bf16[8,16,128]{2,1,0:T(8,128)(2,1)S(1)} %weights.1.w0_ref), channel_id=1, source_target_pairs={{0,128},{32,160},{64,192},{96,224},{128,0},{160,32},{192,64},{224,... | collective-permute-start | bytes 98312 | tf_op jit(solution)/shard_map/ppermute | solution.py:319
  10.1 2.7 %collective-permute-start.2 = (bf16[8,16,128]{2,1,0:T(8,128)(2,1)S(1)}, bf16[8,16,128]{2,1,0:T(8,128)(2,1)S(1)}, u32[]{:S(2)}, u32[]{:S(2)}) collective-permute-start(bf16[8,16,128]{2,1,0:T(8,128)(2,1)S(1)} %weights.1.w0_ref), channel_id=1, source_target_pairs={{0,192},{32,224},{64,0},{96,32},{128,64},{160,96},{192,128},{224,1... | collective-permute-start | bytes 98312 | tf_op jit(solution)/shard_map/ppermute | solution.py:319
  12.8 3.1 %gate.1 = bf16[32,16,1536]{2,1,0:T(8,128)(2,1)} custom-call(bf16[512,1536]{1,0:T(8,128)(2,1)} %bitcast.17, bf16[512,1536]{1,0:T(8,128)(2,1)} %bitcast.19), custom_call_target="tpu_custom_call" | custom-call | flops 402653184 | bytes 4718592 | tf_op jit(solution)/shard_map/gate/pallas_call | solution.py:125
  15.9 0.0 copy-start.2
  15.9 8.0 %all-to-all-start = ((bf16[32,16,1536]{2,1,0:T(8,128)(2,1)}), bf16[32,16,1536]{2,1,0:T(8,128)(2,1)S(1)}, u32[]{:S(2)}, u32[]{:S(2)}) async-start(bf16[32,16,1536]{2,1,0:T(8,128)(2,1)} %gate.1), calls=%async_computation | async-start | bytes 3145728 | tf_op jit(solution)/shard_map/all_to_all | solution.py:309
  24.0 0.1 collective-permute-start.3
  24.1 0.1 copy.14.idx_ref
  24.2 1.2 collective-permute-done.3.mate_ref
  25.4 1.8 %factor.1 = (bf16[4,128,128]{2,1,0:T(8,128)(2,1)S(1)}, bf16[512,512]{1,0:T(8,128)(2,1)S(1)}, bf16[512,512]{1,0:T(8,128)(2,1)S(1)}, f32[128,128]{1,0:T(8,128)S(1)}) custom-call(s32[1]{0:T(128)} %bitcast.place_ref, bf16[8,16,128]{2,1,0:T(8,128)(2,1)S(1)} %weights.1.w0_ref, bf16[8,16,128]{2,1,0:T(8,128)(2,1)S(1)} %collective-permute-done.w1_ref, ...), custom_call_target="tpu_custom_call" | custom-call | flops 805306368 | bytes 1572864 | tf_op jit(solution)/shard_map/factor/pallas_call | solution.py:327
  27.2 0.0 copy-start
  27.2 0.8 copy-done
  28.0 4.6 %first.1.refs_2_ = bf16[32,32,1536]{2,1,0:T(8,128)(2,1)} custom-call(bf16[4,128,128]{2,1,0:T(8,128)(2,1)S(1)} %get-tuple-element.24.blocks, bf16[512,1536]{1,0:T(8,128)(2,1)} %bitcast.21, bf16[512,1536]{1,0:T(8,128)(2,1)} %bitcast.24), custom_call_target="tpu_custom_call" | custom-call | flops 28991029248 | bytes 4718592 | tf_op jit(solution)/shard_map/first/pallas_call | solution.py:334
  32.6 11.9 %all-to-all-done.refs_1_ = bf16[32,16,1536]{2,1,0:T(8,128)(2,1)S(1)} async-done(((bf16[32,16,1536]{2,1,0:T(8,128)(2,1)}), bf16[32,16,1536]{2,1,0:T(8,128)(2,1)S(1)}, u32[]{:S(2)}, u32[]{:S(2)}) %all-to-all-start) | async-done | bytes 1572896 | tf_op jit(solution)/shard_map/all_to_all | solution.py:309
  44.5 2.2 %back.1 = (bf16[32,32,1536]{2,1,0:T(8,128)(2,1)}, bf16[32,16,1536]{2,1,0:T(8,128)(2,1)}) custom-call(bf16[512,512]{1,0:T(8,128)(2,1)S(1)} %get-tuple-element.23.refs_0_, bf16[32,16,1536]{2,1,0:T(8,128)(2,1)S(1)} %all-to-all-done.refs_1_, bf16[32,32,1536]{2,1,0:T(8,128)(2,1)} %first.1.refs_2_), custom_call_target="tpu_custom_call", output_to_operand_aliasing={{0}: (2, {})} | custom-call | flops 805306368 | bytes 3145728 | tf_op jit(solution)/shard_map/back/pallas_call | solution.py:125
  46.8 0.0 copy-start.1
  46.8 43.2 %all_to_all.15.refs_1_.gf_ref.f_ref = bf16[32,32,1536]{2,1,0:T(8,128)(2,1)S(1)} all-to-all(bf16[32,32,1536]{2,1,0:T(8,128)(2,1)} %get-tuple-element.25), channel_id=1, replica_groups=mesh['dp'=8,'seq'=32] {'seq'}, dimensions={0} | all-to-all | bytes 6291456 | tf_op jit(solution)/shard_map/all_to_all | solution.py:309
  90.0 1.8 %mix.1 = bf16[32,16,1536]{2,1,0:T(8,128)(2,1)} custom-call(bf16[512,512]{1,0:T(8,128)(2,1)S(1)} %copy-done.1, bf16[32,32,1536]{2,1,0:T(8,128)(2,1)S(1)} %all_to_all.15.refs_1_.gf_ref.f_ref), custom_call_target="tpu_custom_call" | custom-call | flops 805306368 | bytes 3145728 | tf_op jit(solution)/shard_map/mix/pallas_call | solution.py:125
  91.8 5.6 %all-to-all-start.2 = ((bf16[32,16,1536]{2,1,0:T(8,128)(2,1)}), bf16[32,16,1536]{2,1,0:T(8,128)(2,1)}, u32[]{:S(2)}, u32[]{:S(2)}) async-start(bf16[32,16,1536]{2,1,0:T(8,128)(2,1)} %mix.1), calls=%async_computation.2 | async-start | bytes 3145728 | tf_op jit(solution)/shard_map/all_to_all | solution.py:309
  97.4 5.0 %sums.1 = (f32[4,8,16,128]{3,2,1,0:T(8,128)S(1)}, f32[4,8,16,128]{3,2,1,0:T(8,128)S(1)}) custom-call(s32[1]{0:T(128)S(6)} %and.4.core_ref, f32[128,128]{1,0:T(8,128)S(1)} %get-tuple-element.30.pat_ref, bf16[32,16,1536]{2,1,0:T(8,128)(2,1)} %get-tuple-element.31.gm_ref, bf16[32,32,1536]{2,1,0:T(8,128)(2,1)S(1)} %all_to_all.15.refs_1_.gf_ref.f_ref, ...), custom_call_target="tpu_custom_call" | custom-call | flops 2415919104 | bytes 7864320 | tf_op jit(solution)/shard_map/sums/pallas_call | solution.py:349
  102.5 0.1 collective-permute-start.4
  102.6 1.5 %collective-permute-done.4.got_ref = f32[4,8,16,128]{3,2,1,0:T(8,128)S(1)} collective-permute-done((f32[4,8,16,128]{3,2,1,0:T(8,128)S(1)}, f32[4,8,16,128]{3,2,1,0:T(8,128)S(1)}, u32[]{:S(2)}, u32[]{:S(2)}) %collective-permute-start.4) | collective-permute-done | bytes 262176 | tf_op jit(solution)/shard_map/ppermute | solution.py:359
  104.1 0.3 collective-permute-start.5
  104.4 2.4 %collective-permute-start.6 = (bf16[8,16,128]{2,1,0:T(8,128)(2,1)S(1)}, bf16[8,16,128]{2,1,0:T(8,128)(2,1)S(1)}, u32[]{:S(2)}, u32[]{:S(2)}) collective-permute-start(bf16[8,16,128]{2,1,0:T(8,128)(2,1)S(1)} %get-tuple-element.36), channel_id=1, source_target_pairs={{0,128},{32,160},{64,192},{96,224},{128,0},{160,32},{192,64},{224,... | collective-permute-start | bytes 98312 | tf_op jit(solution)/shard_map/ppermute | solution.py:367
  106.8 2.8 %collective-permute-start.7 = (bf16[8,16,128]{2,1,0:T(8,128)(2,1)S(1)}, bf16[8,16,128]{2,1,0:T(8,128)(2,1)S(1)}, u32[]{:S(2)}, u32[]{:S(2)}) collective-permute-start(bf16[8,16,128]{2,1,0:T(8,128)(2,1)S(1)} %get-tuple-element.37), channel_id=1, source_target_pairs={{0,192},{32,224},{64,0},{96,32},{128,64},{160,96},{192,128},{224,1... | collective-permute-start | bytes 98312 | tf_op jit(solution)/shard_map/ppermute | solution.py:367
  109.7 5.2 %grads.1 = (bf16[512,1536]{1,0:T(8,128)(2,1)}, bf16[512,1536]{1,0:T(8,128)(2,1)}) custom-call(bf16[4,128,128]{2,1,0:T(8,128)(2,1)S(1)} %get-tuple-element.24.blocks, bf16[32,32,1536]{2,1,0:T(8,128)(2,1)S(1)} %all_to_all.15.refs_1_.gf_ref.f_ref, bf16[512,1536]{1,0:T(8,128)(2,1)} %bitcast.23, bf16[512,1536]{1,0:T(8,128)(2,1)} %bitcast.26), custom_call_target="tpu_custom_call" | custom-call | flops 805306368 | bytes 7864320 | tf_op jit(solution)/shard_map/grads/pallas_call | solution.py:355
  114.8 0.3 collective-permute-done.5
  115.1 1.4 %collective-permute-done.6 = bf16[8,16,128]{2,1,0:T(8,128)(2,1)S(1)} collective-permute-done((bf16[8,16,128]{2,1,0:T(8,128)(2,1)S(1)}, bf16[8,16,128]{2,1,0:T(8,128)(2,1)S(1)}, u32[]{:S(2)}, u32[]{:S(2)}) %collective-permute-start.6) | collective-permute-done | bytes 32800 | tf_op jit(solution)/shard_map/ppermute | solution.py:367
  116.6 0.6 fusion
  117.2 1.5 %all-to-all-done.2.refs_0_ = bf16[32,16,1536]{2,1,0:T(8,128)(2,1)} async-done(((bf16[32,16,1536]{2,1,0:T(8,128)(2,1)}), bf16[32,16,1536]{2,1,0:T(8,128)(2,1)}, u32[]{:S(2)}, u32[]{:S(2)}) %all-to-all-start.2) | async-done | bytes 1572896 | tf_op jit(solution)/shard_map/all_to_all | solution.py:309
  118.7 3.8 %tail.1 = (bf16[512,1536]{1,0:T(8,128)(2,1)}, bf16[512,1536]{1,0:T(8,128)(2,1)}) custom-call(bf16[32,16,1536]{2,1,0:T(8,128)(2,1)} %all-to-all-done.2.refs_0_, bf16[512,1536]{1,0:T(8,128)(2,1)} %bitcast.18, bf16[512,1536]{1,0:T(8,128)(2,1)} %bitcast.20), custom_call_target="tpu_custom_call" | custom-call | flops 402653184 | bytes 7864320 | tf_op jit(solution)/shard_map/tail/pallas_call | solution.py:125
  (9 shorter events, 0.1 us)
Async XLA Ops:
  1.4 22.5 %collective-permute-start = (bf16[8,16,128]{2,1,0:T(8,128)(2,1)S(1)}, bf16[8,16,128]{2,1,0:T(8,128)(2,1)S(1)}, u32[]{:S(2)}, u32[]{:S(2)}) collective-permute-start(bf16[8,16,128]{2,1,0:T(8,128)(2,1)S(1)} %weights.1.w0_ref), channel_id=1, source_target_pairs={{0,64},{32,96},{64,128},{96,160},{128,192},{160,224},{192,0},{224,... | collective-permute-start | bytes 98312 | tf_op jit(solution)/shard_map/ppermute | solution.py:319
  4.7 19.2 %collective-permute-start.1 = (bf16[8,16,128]{2,1,0:T(8,128)(2,1)S(1)}, bf16[8,16,128]{2,1,0:T(8,128)(2,1)S(1)}, u32[]{:S(2)}, u32[]{:S(2)}) collective-permute-start(bf16[8,16,128]{2,1,0:T(8,128)(2,1)S(1)} %weights.1.w0_ref), channel_id=1, source_target_pairs={{0,128},{32,160},{64,192},{96,224},{128,0},{160,32},{192,64},{224,... | collective-permute-start | bytes 98312 | tf_op jit(solution)/shard_map/ppermute | solution.py:319
  10.1 13.8 %collective-permute-start.2 = (bf16[8,16,128]{2,1,0:T(8,128)(2,1)S(1)}, bf16[8,16,128]{2,1,0:T(8,128)(2,1)S(1)}, u32[]{:S(2)}, u32[]{:S(2)}) collective-permute-start(bf16[8,16,128]{2,1,0:T(8,128)(2,1)S(1)} %weights.1.w0_ref), channel_id=1, source_target_pairs={{0,192},{32,224},{64,0},{96,32},{128,64},{160,96},{192,128},{224,1... | collective-permute-start | bytes 98312 | tf_op jit(solution)/shard_map/ppermute | solution.py:319
  15.9 8.2 %copy-start.2 = (s32[128,16]{0,1:T(8,128)S(1)}, s32[128,16]{0,1:T(8,128)}, u32[]{:S(2)}) copy-start(s32[128,16]{0,1:T(8,128)} %param.12) | copy-start | bytes 24580
  15.9 28.6 %all-to-all-start = ((bf16[32,16,1536]{2,1,0:T(8,128)(2,1)}), bf16[32,16,1536]{2,1,0:T(8,128)(2,1)S(1)}, u32[]{:S(2)}, u32[]{:S(2)}) async-start(bf16[32,16,1536]{2,1,0:T(8,128)(2,1)} %gate.1), calls=%async_computation | async-start | bytes 3145728 | tf_op jit(solution)/shard_map/all_to_all | solution.py:309
  24.0 1.4 %collective-permute-start.3 = (bf16[4,8,16,128]{3,2,1,0:T(8,128)(2,1)S(1)}, bf16[4,8,16,128]{3,2,1,0:T(8,128)(2,1)S(1)}, u32[]{:S(2)}, u32[]{:S(2)}) collective-permute-start(bf16[4,8,16,128]{3,2,1,0:T(8,128)(2,1)S(1)} %pad_maximum_fusion), channel_id=1, source_target_pairs={{0,32},{32,0},{64,96},{96,64},{128,160},{160,128},{192,224},{224,1... | collective-permute-start | bytes 393224 | tf_op jit(solution)/shard_map/ppermute | solution.py:325
  27.2 0.8 copy-start
  46.8 43.2 %copy-start.1 = (bf16[512,512]{1,0:T(8,128)(2,1)S(1)}, bf16[512,512]{1,0:T(8,128)(2,1)}, u32[]{:S(2)}) copy-start(bf16[512,512]{1,0:T(8,128)(2,1)} %copy-done) | copy-start | bytes 1572868
  91.8 26.9 %all-to-all-start.2 = ((bf16[32,16,1536]{2,1,0:T(8,128)(2,1)}), bf16[32,16,1536]{2,1,0:T(8,128)(2,1)}, u32[]{:S(2)}, u32[]{:S(2)}) async-start(bf16[32,16,1536]{2,1,0:T(8,128)(2,1)} %mix.1), calls=%async_computation.2 | async-start | bytes 3145728 | tf_op jit(solution)/shard_map/all_to_all | solution.py:309
  102.5 1.6 %collective-permute-start.4 = (f32[4,8,16,128]{3,2,1,0:T(8,128)S(1)}, f32[4,8,16,128]{3,2,1,0:T(8,128)S(1)}, u32[]{:S(2)}, u32[]{:S(2)}) collective-permute-start(f32[4,8,16,128]{3,2,1,0:T(8,128)S(1)} %get-tuple-element.33), channel_id=1, source_target_pairs={{0,32},{32,0},{64,96},{96,64},{128,160},{160,128},{192,224},{224,1... | collective-permute-start | bytes 786440 | tf_op jit(solution)/shard_map/ppermute | solution.py:359
  104.1 11.0 %collective-permute-start.5 = (bf16[8,16,128]{2,1,0:T(8,128)(2,1)S(1)}, bf16[8,16,128]{2,1,0:T(8,128)(2,1)S(1)}, u32[]{:S(2)}, u32[]{:S(2)}) collective-permute-start(bf16[8,16,128]{2,1,0:T(8,128)(2,1)S(1)} %get-tuple-element.35), channel_id=1, source_target_pairs={{0,64},{32,96},{64,128},{96,160},{128,192},{160,224},{192,0},{224,... | collective-permute-start | bytes 98312 | tf_op jit(solution)/shard_map/ppermute | solution.py:367
  104.4 12.1 %collective-permute-start.6 = (bf16[8,16,128]{2,1,0:T(8,128)(2,1)S(1)}, bf16[8,16,128]{2,1,0:T(8,128)(2,1)S(1)}, u32[]{:S(2)}, u32[]{:S(2)}) collective-permute-start(bf16[8,16,128]{2,1,0:T(8,128)(2,1)S(1)} %get-tuple-element.36), channel_id=1, source_target_pairs={{0,128},{32,160},{64,192},{96,224},{128,0},{160,32},{192,64},{224,... | collective-permute-start | bytes 98312 | tf_op jit(solution)/shard_map/ppermute | solution.py:367
  106.8 9.7 %collective-permute-start.7 = (bf16[8,16,128]{2,1,0:T(8,128)(2,1)S(1)}, bf16[8,16,128]{2,1,0:T(8,128)(2,1)S(1)}, u32[]{:S(2)}, u32[]{:S(2)}) collective-permute-start(bf16[8,16,128]{2,1,0:T(8,128)(2,1)S(1)} %get-tuple-element.37), channel_id=1, source_target_pairs={{0,192},{32,224},{64,0},{96,32},{128,64},{160,96},{192,128},{224,1... | collective-permute-start | bytes 98312 | tf_op jit(solution)/shard_map/ppermute | solution.py:367

commit v6 on v4

--- a/solution.py
+++ b/solution.py
@@ -9,6 +9,7 @@
 F32 = jnp.float32
 MIB = 1024 * 1024
 STEP = 512
+BROAD = 768
 WIDE = 512
 
 
@@ -318,7 +319,7 @@
     own_rows = pack("weights", block_weights, mix_weights)
     column = [own_rows] + [lax.ppermute(own_rows, "dp", hop(r)) for r in (1, 2, 3)]
     (gated,) = streamed(
-        gate_body, "gate", [pinned(q), pinned(cot)], [slab_shape], STEP, scratch=[perm], prepare=make_slab_order,
+        gate_body, "gate", [pinned(q), pinned(cot)], [slab_shape], BROAD, scratch=[perm], prepare=make_slab_order,
         flops=work // 2, nbytes=3 * size,
     )
     gated, *column = lax.optimization_barrier((gated, *column))
@@ -352,7 +353,7 @@
         [smem, VMEM_SPEC, slab, slab, slab_spec(width, 1), rows, rows],
         [whole(4, 8, 16, 128), whole(4, 8, 16, 128)], [part, part],
         [perm, perm, pltpu.VMEM((8, 128, 128), F32)], 3 * work, 5 * size,
-    )(core, held(pattern), grad_cols, got, got, pinned(k), pinned(v))
+    )(core, held(pattern), pinned(grad_cols), got, got, pinned(k), pinned(v))
     grad_key, grad_value = call(
         grads_kernel, "grads", grid, [VMEM_SPEC, slab_spec(width, 1), rows, rows], [rows, rows],
         [row_shape, row_shape], [perm], work, 5 * size,
@@ -368,7 +369,7 @@
         total = total + lax.ppermute(other, "dp", hop(r)).astype(F32)
 
     output, grad_query = streamed(
-        tail_body, "tail", [returned, pinned(q), pinned(cot)], [pinned_rows, pinned_rows], STEP,
+        tail_body, "tail", [returned, pinned(q), pinned(cot)], [pinned_rows, pinned_rows], BROAD,
         scratch=[perm], prepare=make_slab_order, flops=work // 2, nbytes=5 * size,
     )
     wide = query.shape

time: 123 us -> 124 us (level)
  waiting for transfers between devices: 17.3 us -> 19.2 us
  local copies, waits for them, and re-layouts: 2.93 us -> 1.53 us
    unnamed x9 -> x7, local copies, waits for them, and re-layouts: 2.3 us -> 0.9 us
    all_to_all x2, waiting for transfers between devices: 14.2 us -> 15.5 us  [exchange(): return lax.all_to_all(x, 'seq', split_axis=0, concat_axis=0, tiled=True)]
  transfers between devices with their start and end apart: 10 -> 10, of which waited for: 5 -> 6; matrix products, arithmetic and copies ran while one was open for 1% -> 1% of each run, Pallas kernels for 16% -> 16%
where the time goes in v6:
time: 124 us; the launch traced here: 123 us
  blocking collectives  43.2 us (35%)
  starting transfers between devices  29.8 us (24%)
  Pallas kernels  28.7 us (23%)
  waiting for transfers between devices  19.2 us (15%)
  local copies, waits for them, and re-layouts  1.53 us (1%)
    all_to_all x1, blocking collectives, exchange(): return lax.all_to_all(x, 'seq', split_axis=0, concat_axis=0, tiled=True)  43.2 us
    all_to_all x2, waiting for transfers between devices, exchange(): return lax.all_to_all(x, 'seq', split_axis=0, concat_axis=0, tiled=True)  15.5 us
    all_to_all x2, starting transfers between devices, exchange(): return lax.all_to_all(x, 'seq', split_axis=0, concat_axis=0, tiled=True)  13.6 us
    ppermute x3, starting transfers between devices, on_device(): lax.ppermute(own_rows, 'dp', hop(r))  11.4 us
    pallas_call x4, Pallas kernels, streamed(): pl.pallas_call(kernel, name=name, in_specs=[VMEM_SPEC] * n_vmem + [pl.Blo...  11.3 us
    pallas_call x1, Pallas kernels, on_device(): call(grads_kernel, 'grads', grid, [VMEM_SPEC, slab_spec(width, 1), rows,...  5.16 us
    pallas_call x1, Pallas kernels, on_device(): call(sums_kernel, 'sums', grid, [smem, VMEM_SPEC, slab, slab, slab_spec(w...  5.03 us
    pallas_call x1, Pallas kernels, on_device(): call(first_kernel, 'first', grid, [VMEM_SPEC, rows, rows], slab, pair_sha...  4.62 us
  transfers between devices with their start and end apart: 10, of which 6 were waited for; matrix products, arithmetic and copies ran while one was open for 1% of the time, Pallas kernels for 16%

profile of v6, /device:TPU:8, one launch (start us, length us, event | category | flops | bytes accessed | tf_op | source)
XLA Modules:
  0.0 123.2 jit_solution(2187170762147731162)
XLA Ops:
  0.6 0.8 weights.1.w0_ref
  1.4 3.3 %collective-permute-start = (bf16[8,16,128]{2,1,0:T(8,128)(2,1)S(1)}, bf16[8,16,128]{2,1,0:T(8,128)(2,1)S(1)}, u32[]{:S(2)}, u32[]{:S(2)}) collective-permute-start(bf16[8,16,128]{2,1,0:T(8,128)(2,1)S(1)} %weights.1.w0_ref), channel_id=1, source_target_pairs={{0,64},{32,96},{64,128},{96,160},{128,192},{160,224},{192,0},{224,... | collective-permute-start | bytes 98312 | tf_op jit(solution)/shard_map/ppermute | solution.py:320
  4.7 5.4 %collective-permute-start.1 = (bf16[8,16,128]{2,1,0:T(8,128)(2,1)S(1)}, bf16[8,16,128]{2,1,0:T(8,128)(2,1)S(1)}, u32[]{:S(2)}, u32[]{:S(2)}) collective-permute-start(bf16[8,16,128]{2,1,0:T(8,128)(2,1)S(1)} %weights.1.w0_ref), channel_id=1, source_target_pairs={{0,128},{32,160},{64,192},{96,224},{128,0},{160,32},{192,64},{224,... | collective-permute-start | bytes 98312 | tf_op jit(solution)/shard_map/ppermute | solution.py:320
  10.1 2.7 %collective-permute-start.2 = (bf16[8,16,128]{2,1,0:T(8,128)(2,1)S(1)}, bf16[8,16,128]{2,1,0:T(8,128)(2,1)S(1)}, u32[]{:S(2)}, u32[]{:S(2)}) collective-permute-start(bf16[8,16,128]{2,1,0:T(8,128)(2,1)S(1)} %weights.1.w0_ref), channel_id=1, source_target_pairs={{0,192},{32,224},{64,0},{96,32},{128,64},{160,96},{192,128},{224,1... | collective-permute-start | bytes 98312 | tf_op jit(solution)/shard_map/ppermute | solution.py:320
  12.8 3.2 %gate.1 = bf16[32,16,1536]{2,1,0:T(8,128)(2,1)} custom-call(bf16[512,1536]{1,0:T(8,128)(2,1)} %bitcast.23, bf16[512,1536]{1,0:T(8,128)(2,1)} %bitcast.25), custom_call_target="tpu_custom_call" | custom-call | flops 402653184 | bytes 4718592 | tf_op jit(solution)/shard_map/gate/pallas_call | solution.py:126
  16.0 0.0 copy-start.2
  16.0 8.0 %all-to-all-start = ((bf16[32,16,1536]{2,1,0:T(8,128)(2,1)}), bf16[32,16,1536]{2,1,0:T(8,128)(2,1)S(1)}, u32[]{:S(2)}, u32[]{:S(2)}) async-start(bf16[32,16,1536]{2,1,0:T(8,128)(2,1)} %gate.1), calls=%async_computation | async-start | bytes 3145728 | tf_op jit(solution)/shard_map/all_to_all | solution.py:310
  24.1 0.1 collective-permute-start.3
  24.2 0.1 copy.14.idx_ref
  24.3 1.2 collective-permute-done.3.mate_ref
  25.5 1.8 %factor.1 = (bf16[4,128,128]{2,1,0:T(8,128)(2,1)S(1)}, bf16[512,512]{1,0:T(8,128)(2,1)S(1)}, bf16[512,512]{1,0:T(8,128)(2,1)S(1)}, f32[128,128]{1,0:T(8,128)S(1)}) custom-call(s32[1]{0:T(128)} %bitcast.place_ref, bf16[8,16,128]{2,1,0:T(8,128)(2,1)S(1)} %weights.1.w0_ref, bf16[8,16,128]{2,1,0:T(8,128)(2,1)S(1)} %collective-permute-done.w1_ref, ...), custom_call_target="tpu_custom_call" | custom-call | flops 805306368 | bytes 1572864 | tf_op jit(solution)/shard_map/factor/pallas_call | solution.py:329
  27.3 0.0 copy-start
  27.3 0.8 copy-done
  28.1 4.6 %first.1.refs_2_ = bf16[32,32,1536]{2,1,0:T(8,128)(2,1)} custom-call(bf16[4,128,128]{2,1,0:T(8,128)(2,1)S(1)} %get-tuple-element.34.blocks, bf16[512,1536]{1,0:T(8,128)(2,1)} %bitcast.17, bf16[512,1536]{1,0:T(8,128)(2,1)} %bitcast.20), custom_call_target="tpu_custom_call" | custom-call | flops 805306368 | bytes 4718592 | tf_op jit(solution)/shard_map/first/pallas_call | solution.py:336
  32.7 12.0 %all-to-all-done.refs_1_ = bf16[32,16,1536]{2,1,0:T(8,128)(2,1)S(1)} async-done(((bf16[32,16,1536]{2,1,0:T(8,128)(2,1)}), bf16[32,16,1536]{2,1,0:T(8,128)(2,1)S(1)}, u32[]{:S(2)}, u32[]{:S(2)}) %all-to-all-start) | async-done | bytes 1572896 | tf_op jit(solution)/shard_map/all_to_all | solution.py:310
  44.6 2.2 %back.1 = (bf16[32,32,1536]{2,1,0:T(8,128)(2,1)}, bf16[32,16,1536]{2,1,0:T(8,128)(2,1)}) custom-call(bf16[512,512]{1,0:T(8,128)(2,1)S(1)} %get-tuple-element.32.refs_0_, bf16[32,16,1536]{2,1,0:T(8,128)(2,1)S(1)} %all-to-all-done.refs_1_, bf16[32,32,1536]{2,1,0:T(8,128)(2,1)} %first.1.refs_2_), custom_call_target="tpu_custom_call", output_to_operand_aliasing={{0}: (2, {})} | custom-call | flops 805306368 | bytes 3145728 | tf_op jit(solution)/shard_map/back/pallas_call | solution.py:126
  46.9 0.0 copy-start.1
  46.9 43.2 %all_to_all.15.refs_1_.gf_ref.f_ref = bf16[32,32,1536]{2,1,0:T(8,128)(2,1)S(1)} all-to-all(bf16[32,32,1536]{2,1,0:T(8,128)(2,1)} %get-tuple-element.35), channel_id=1, replica_groups=mesh['dp'=8,'seq'=32] {'seq'}, dimensions={0} | all-to-all | bytes 6291456 | tf_op jit(solution)/shard_map/all_to_all | solution.py:310
  90.1 1.8 %mix.1 = bf16[32,16,1536]{2,1,0:T(8,128)(2,1)} custom-call(bf16[512,512]{1,0:T(8,128)(2,1)S(1)} %copy-done.1, bf16[32,32,1536]{2,1,0:T(8,128)(2,1)S(1)} %all_to_all.15.refs_1_.gf_ref.f_ref), custom_call_target="tpu_custom_call" | custom-call | flops 805306368 | bytes 3145728 | tf_op jit(solution)/shard_map/mix/pallas_call | solution.py:126
  91.9 5.6 %all-to-all-start.2 = ((bf16[32,16,1536]{2,1,0:T(8,128)(2,1)}), bf16[32,16,1536]{2,1,0:T(8,128)(2,1)}, u32[]{:S(2)}, u32[]{:S(2)}) async-start(bf16[32,16,1536]{2,1,0:T(8,128)(2,1)} %mix.1), calls=%async_computation.2 | async-start | bytes 3145728 | tf_op jit(solution)/shard_map/all_to_all | solution.py:310
  97.5 5.0 %sums.1 = (f32[4,8,16,128]{3,2,1,0:T(8,128)S(1)}, f32[4,8,16,128]{3,2,1,0:T(8,128)S(1)}) custom-call(s32[1]{0:T(128)S(6)} %and.4.core_ref, f32[128,128]{1,0:T(8,128)S(1)} %get-tuple-element.40.pat_ref, bf16[32,16,1536]{2,1,0:T(8,128)(2,1)} %get-tuple-element.41.gm_ref, bf16[32,32,1536]{2,1,0:T(8,128)(2,1)S(1)} %all_to_all.15.refs_1_.gf_ref.f_ref, ...), custom_call_target="tpu_custom_call" | custom-call | flops 2415919104 | bytes 7864320 | tf_op jit(solution)/shard_map/sums/pallas_call | solution.py:351
  102.6 0.1 collective-permute-start.4
  102.7 1.5 %collective-permute-done.4.got_ref = f32[4,8,16,128]{3,2,1,0:T(8,128)S(1)} collective-permute-done((f32[4,8,16,128]{3,2,1,0:T(8,128)S(1)}, f32[4,8,16,128]{3,2,1,0:T(8,128)S(1)}, u32[]{:S(2)}, u32[]{:S(2)}) %collective-permute-start.4) | collective-permute-done | bytes 262176 | tf_op jit(solution)/shard_map/ppermute | solution.py:361
  104.2 0.1 collective-permute-start.5
  104.3 3.1 %collective-permute-start.6 = (bf16[8,16,128]{2,1,0:T(8,128)(2,1)S(1)}, bf16[8,16,128]{2,1,0:T(8,128)(2,1)S(1)}, u32[]{:S(2)}, u32[]{:S(2)}) collective-permute-start(bf16[8,16,128]{2,1,0:T(8,128)(2,1)S(1)} %get-tuple-element.46), channel_id=1, source_target_pairs={{0,128},{32,160},{64,192},{96,224},{128,0},{160,32},{192,64},{224,... | collective-permute-start | bytes 98312 | tf_op jit(solution)/shard_map/ppermute | solution.py:369
  107.5 1.4 %collective-permute-start.7 = (bf16[8,16,128]{2,1,0:T(8,128)(2,1)S(1)}, bf16[8,16,128]{2,1,0:T(8,128)(2,1)S(1)}, u32[]{:S(2)}, u32[]{:S(2)}) collective-permute-start(bf16[8,16,128]{2,1,0:T(8,128)(2,1)S(1)} %get-tuple-element.47), channel_id=1, source_target_pairs={{0,192},{32,224},{64,0},{96,32},{128,64},{160,96},{192,128},{224,1... | collective-permute-start | bytes 98312 | tf_op jit(solution)/shard_map/ppermute | solution.py:369
  108.8 5.2 %grads.1 = (bf16[512,1536]{1,0:T(8,128)(2,1)}, bf16[512,1536]{1,0:T(8,128)(2,1)}) custom-call(bf16[4,128,128]{2,1,0:T(8,128)(2,1)S(1)} %get-tuple-element.34.blocks, bf16[32,32,1536]{2,1,0:T(8,128)(2,1)S(1)} %all_to_all.15.refs_1_.gf_ref.f_ref, bf16[512,1536]{1,0:T(8,128)(2,1)} %bitcast.19, bf16[512,1536]{1,0:T(8,128)(2,1)} %bitcast.22), custom_call_target="tpu_custom_call" | custom-call | flops 805306368 | bytes 7864320 | tf_op jit(solution)/shard_map/grads/pallas_call | solution.py:357
  114.0 0.7 collective-permute-done.5
  114.7 0.2 collective-permute-done.6
  115.0 0.6 fusion
  115.6 3.5 %all-to-all-done.2.refs_0_ = bf16[32,16,1536]{2,1,0:T(8,128)(2,1)} async-done(((bf16[32,16,1536]{2,1,0:T(8,128)(2,1)}), bf16[32,16,1536]{2,1,0:T(8,128)(2,1)}, u32[]{:S(2)}, u32[]{:S(2)}) %all-to-all-start.2) | async-done | bytes 1572896 | tf_op jit(solution)/shard_map/all_to_all | solution.py:310
  119.1 4.1 %tail.1 = (bf16[512,1536]{1,0:T(8,128)(2,1)}, bf16[512,1536]{1,0:T(8,128)(2,1)}) custom-call(bf16[32,16,1536]{2,1,0:T(8,128)(2,1)} %all-to-all-done.2.refs_0_, bf16[512,1536]{1,0:T(8,128)(2,1)} %bitcast.24, bf16[512,1536]{1,0:T(8,128)(2,1)} %bitcast.26), custom_call_target="tpu_custom_call" | custom-call | flops 402653184 | bytes 7864320 | tf_op jit(solution)/shard_map/tail/pallas_call | solution.py:126
  (9 shorter events, 0.1 us)
Async XLA Ops:
  1.4 14.6 %collective-permute-start = (bf16[8,16,128]{2,1,0:T(8,128)(2,1)S(1)}, bf16[8,16,128]{2,1,0:T(8,128)(2,1)S(1)}, u32[]{:S(2)}, u32[]{:S(2)}) collective-permute-start(bf16[8,16,128]{2,1,0:T(8,128)(2,1)S(1)} %weights.1.w0_ref), channel_id=1, source_target_pairs={{0,64},{32,96},{64,128},{96,160},{128,192},{160,224},{192,0},{224,... | collective-permute-start | bytes 98312 | tf_op jit(solution)/shard_map/ppermute | solution.py:320
  4.7 11.3 %collective-permute-start.1 = (bf16[8,16,128]{2,1,0:T(8,128)(2,1)S(1)}, bf16[8,16,128]{2,1,0:T(8,128)(2,1)S(1)}, u32[]{:S(2)}, u32[]{:S(2)}) collective-permute-start(bf16[8,16,128]{2,1,0:T(8,128)(2,1)S(1)} %weights.1.w0_ref), channel_id=1, source_target_pairs={{0,128},{32,160},{64,192},{96,224},{128,0},{160,32},{192,64},{224,... | collective-permute-start | bytes 98312 | tf_op jit(solution)/shard_map/ppermute | solution.py:320
  10.1 5.9 %collective-permute-start.2 = (bf16[8,16,128]{2,1,0:T(8,128)(2,1)S(1)}, bf16[8,16,128]{2,1,0:T(8,128)(2,1)S(1)}, u32[]{:S(2)}, u32[]{:S(2)}) collective-permute-start(bf16[8,16,128]{2,1,0:T(8,128)(2,1)S(1)} %weights.1.w0_ref), channel_id=1, source_target_pairs={{0,192},{32,224},{64,0},{96,32},{128,64},{160,96},{192,128},{224,1... | collective-permute-start | bytes 98312 | tf_op jit(solution)/shard_map/ppermute | solution.py:320
  16.0 8.2 %copy-start.2 = (s32[128,16]{0,1:T(8,128)S(1)}, s32[128,16]{0,1:T(8,128)}, u32[]{:S(2)}) copy-start(s32[128,16]{0,1:T(8,128)} %param.12) | copy-start | bytes 24580
  16.0 28.6 %all-to-all-start = ((bf16[32,16,1536]{2,1,0:T(8,128)(2,1)}), bf16[32,16,1536]{2,1,0:T(8,128)(2,1)S(1)}, u32[]{:S(2)}, u32[]{:S(2)}) async-start(bf16[32,16,1536]{2,1,0:T(8,128)(2,1)} %gate.1), calls=%async_computation | async-start | bytes 3145728 | tf_op jit(solution)/shard_map/all_to_all | solution.py:310
  24.1 1.4 %collective-permute-start.3 = (bf16[4,8,16,128]{3,2,1,0:T(8,128)(2,1)S(1)}, bf16[4,8,16,128]{3,2,1,0:T(8,128)(2,1)S(1)}, u32[]{:S(2)}, u32[]{:S(2)}) collective-permute-start(bf16[4,8,16,128]{3,2,1,0:T(8,128)(2,1)S(1)} %pad_maximum_fusion), channel_id=1, source_target_pairs={{0,32},{32,0},{64,96},{96,64},{128,160},{160,128},{192,224},{224,1... | collective-permute-start | bytes 393224 | tf_op jit(solution)/shard_map/ppermute | solution.py:327
  27.3 0.8 copy-start
  46.9 43.2 %copy-start.1 = (bf16[512,512]{1,0:T(8,128)(2,1)S(1)}, bf16[512,512]{1,0:T(8,128)(2,1)}, u32[]{:S(2)}) copy-start(bf16[512,512]{1,0:T(8,128)(2,1)} %copy-done) | copy-start | bytes 1572868
  91.9 27.2 %all-to-all-start.2 = ((bf16[32,16,1536]{2,1,0:T(8,128)(2,1)}), bf16[32,16,1536]{2,1,0:T(8,128)(2,1)}, u32[]{:S(2)}, u32[]{:S(2)}) async-start(bf16[32,16,1536]{2,1,0:T(8,128)(2,1)} %mix.1), calls=%async_computation.2 | async-start | bytes 3145728 | tf_op jit(solution)/shard_map/all_to_all | solution.py:310
  102.6 1.6 %collective-permute-start.4 = (f32[4,8,16,128]{3,2,1,0:T(8,128)S(1)}, f32[4,8,16,128]{3,2,1,0:T(8,128)S(1)}, u32[]{:S(2)}, u32[]{:S(2)}) collective-permute-start(f32[4,8,16,128]{3,2,1,0:T(8,128)S(1)} %get-tuple-element.43), channel_id=1, source_target_pairs={{0,32},{32,0},{64,96},{96,64},{128,160},{160,128},{192,224},{224,1... | collective-permute-start | bytes 786440 | tf_op jit(solution)/shard_map/ppermute | solution.py:361
  104.2 10.5 %collective-permute-start.5 = (bf16[8,16,128]{2,1,0:T(8,128)(2,1)S(1)}, bf16[8,16,128]{2,1,0:T(8,128)(2,1)S(1)}, u32[]{:S(2)}, u32[]{:S(2)}) collective-permute-start(bf16[8,16,128]{2,1,0:T(8,128)(2,1)S(1)} %get-tuple-element.45), channel_id=1, source_target_pairs={{0,64},{32,96},{64,128},{96,160},{128,192},{160,224},{192,0},{224,... | collective-permute-start | bytes 98312 | tf_op jit(solution)/shard_map/ppermute | solution.py:369
  104.3 10.6 %collective-permute-start.6 = (bf16[8,16,128]{2,1,0:T(8,128)(2,1)S(1)}, bf16[8,16,128]{2,1,0:T(8,128)(2,1)S(1)}, u32[]{:S(2)}, u32[]{:S(2)}) collective-permute-start(bf16[8,16,128]{2,1,0:T(8,128)(2,1)S(1)} %get-tuple-element.46), channel_id=1, source_target_pairs={{0,128},{32,160},{64,192},{96,224},{128,0},{160,32},{192,64},{224,... | collective-permute-start | bytes 98312 | tf_op jit(solution)/shard_map/ppermute | solution.py:369
  107.5 7.5 %collective-permute-start.7 = (bf16[8,16,128]{2,1,0:T(8,128)(2,1)S(1)}, bf16[8,16,128]{2,1,0:T(8,128)(2,1)S(1)}, u32[]{:S(2)}, u32[]{:S(2)}) collective-permute-start(bf16[8,16,128]{2,1,0:T(8,128)(2,1)S(1)} %get-tuple-element.47), channel_id=1, source_target_pairs={{0,192},{32,224},{64,0},{96,32},{128,64},{160,96},{192,128},{224,1... | collective-permute-start | bytes 98312 | tf_op jit(solution)/shard_map/ppermute | solution.py:369
